TPU v7x, 32 devices: a whole 2x2x4 slice. The times are simulated.
32 devices in a mesh: dp: 8 (over y, x, core), tensor: 4 (over z).
Axes of the slice: x: 2, y: 2, z: 4, core: 2. Of those that a mesh axis runs over, the one named last changes fastest.
Arguments:
- tokens: bfloat16 [8192, 2048], P(('dp', 'tensor')), may hold values from -6 to 6
- cotangent: bfloat16 [8192, 2048], P(('dp', 'tensor')), may hold values from -6 to 6
- norm_gains: float32 [2, 2048], replicated, may hold values from 0.1 to 1.9
- norm_shifts: float32 [2, 2048], replicated, may hold values from -4 to 4
- query_key_value_weight: bfloat16 [2048, 3, 2048], P(None, None, 'tensor'), may hold values from -0.125 to 0.125
- b_qv: float32 [2, 2048], P(None, 'tensor'), may hold values from -4 to 4
- output_weight: bfloat16 [2048, 2048], P('tensor'), may hold values from -0.375 to 0.375
- output_bias_vector: float32 [2048], replicated, may hold values from -4 to 4
- up_weight: bfloat16 [2048, 8192], P(None, 'tensor'), may hold values from -0.125 to 0.125
- b_up: float32 [8192], P('tensor'), may hold values from -4 to 4
- down_weight: bfloat16 [8192, 2048], P('tensor'), may hold values from -0.0625 to 0.0625
- down_bias_vector: float32 [2048], replicated, may hold values from -4 to 4
- adapter_query_key_value_input: bfloat16 [8, 16, 2048], replicated, may hold values from -0.125 to 0.125
- qkv_out: bfloat16 [8, 16, 3, 2048], P(None, None, None, 'tensor'), may hold values from -1.5 to 1.5
- adapter_output_input: bfloat16 [8, 16, 2048], P(None, None, 'tensor'), may hold values from -0.375 to 0.375
- adapter_output_output: bfloat16 [8, 16, 2048], replicated, may hold values from -1.5 to 1.5
- adapter_up_input: bfloat16 [8, 16, 2048], replicated, may hold values from -0.125 to 0.125
- up_out: bfloat16 [8, 16, 8192], P(None, None, 'tensor'), may hold values from -1.5 to 1.5
- down_in: bfloat16 [8, 16, 8192], P(None, None, 'tensor'), may hold values from -0.0625 to 0.0625
- adapter_down_output: bfloat16 [8, 16, 2048], replicated, may hold values from -1.5 to 1.5
- offsets: int32 [8, 2], P('dp'), may hold values from 0 to 768, as said below
- adapter_ids: int32 [8, 4], P('dp'), may hold values from 0 to 7
Outputs:
- out: bfloat16 [8192, 2048], P(('dp', 'tensor'))
- in_grad: bfloat16 [8192, 2048], P(('dp', 'tensor'))
- g_qkv_in: float32 [8, 16, 2048], replicated
- g_qkv_out: float32 [8, 16, 3, 2048], P(None, None, None, 'tensor')
- g_out_in: float32 [8, 16, 2048], P(None, None, 'tensor')
- g_out_out: float32 [8, 16, 2048], replicated
- g_up_in: float32 [8, 16, 2048], replicated
- g_up_out: float32 [8, 16, 8192], P(None, None, 'tensor')
- g_down_in: float32 [8, 16, 8192], P(None, None, 'tensor')
- g_down_out: float32 [8, 16, 2048], replicated
Inputs may be any that keep to these rules, and one draw needn't show every extreme that they name: For every sequence s, offsets[s, 0] + 256 <= offsets[s, 1]: the two pieces of 256 positions lie inside the sequence and don't intersect.
All inputs are finite; a program needn't handle non-finite values.
Results may differ from a plain program's by a relative error of at most 0.02.
Values may be sent and summed in bfloat16 or wider, within the bound.
A program may use at most 192 MiB of HBM per device.

v0:
```python
import math

import jax
import jax.numpy as jnp
from jax import lax
from jax.sharding import PartitionSpec as P

HEADS = 16
HEAD_DIM = 128
PIECE = 256


EPS = 1e-05
GELU_C = 0.7978845608028654
GELU_K = 0.044715
NEGATIVE = -1e30
EXACT_MODE = lax.Precision.HIGHEST


def layer_norm(values, gain_row, shift_row):
    centre = values - jnp.mean(values, axis=-1, keepdims=True)
    spread = jnp.mean(centre * centre, axis=-1, keepdims=True)
    inverse = lax.rsqrt(spread + EPS)
    scaled = centre * inverse
    return (scaled * gain_row + shift_row, scaled, inverse)


def norm_back(grad_rows, scaled, inverse, gain_row):
    inner_grad = grad_rows * gain_row
    first_mean = jnp.mean(inner_grad, axis=-1, keepdims=True)
    second_mean = jnp.mean(inner_grad * scaled, axis=-1, keepdims=True)
    return inverse * (inner_grad - first_mean - scaled * second_mean)


def gelu_parts(values):
    cubic = GELU_K * values * values * values
    tangent = jnp.tanh(GELU_C * (values + cubic))
    gelu_value = 0.5 * values * (1.0 + tangent)
    gelu_slope = 0.5 * (1.0 + tangent) + 0.5 * values * (1.0 - tangent * tangent) * GELU_C * (
        1.0 + 3.0 * GELU_K * values * values
    )
    return (gelu_value, gelu_slope)


def dot_transposed(left, right):
    return lax.dot_general(
        left, right, (((1,), (1,)), ((), ())), preferred_element_type=jnp.float32
    )


def choose(adapter_table, indicator_matrix):
    picked = jnp.einsum(
        "ge,erm->grm", indicator_matrix, adapter_table, preferred_element_type=jnp.float32
    )
    return picked.astype(jnp.bfloat16)


def low_rank_down(activations, chosen):
    shaped = activations.reshape(chosen.shape[0], -1, activations.shape[-1])
    return jnp.einsum("glm,grm->glr", shaped, chosen, preferred_element_type=jnp.float32)


def low_rank_upward(rank_rows, chosen):
    product = jnp.einsum(
        "glr,grm->glm", rank_rows, chosen.astype(jnp.float32), precision=EXACT_MODE
    )
    return product.reshape(-1, product.shape[-1])


def rank_grad(rank_rows, activations):
    shaped = activations.reshape(rank_rows.shape[0], -1, activations.shape[-1]).astype(jnp.float32)
    return jnp.einsum("glr,glm->grm", rank_rows, shaped, precision=EXACT_MODE)


def to_tables(per_sequence, indicator_matrix):
    return jnp.einsum("ge,grm->erm", indicator_matrix, per_sequence, precision=EXACT_MODE)


def block_scores(query_rows, key_rows, pieces, slopes, first_row):
    rows_here = query_rows.shape[1]
    length = key_rows.shape[1]
    keys_at = jnp.arange(length, dtype=jnp.int32)
    query_at = first_row + jnp.arange(rows_here, dtype=jnp.int32)
    scaling = 1.0 / math.sqrt(key_rows.shape[3])
    scores = (
        jnp.einsum("gqhd,gkhd->ghqk", query_rows, key_rows, preferred_element_type=jnp.float32)
        * scaling
    )
    distance = jnp.abs(query_at[:, None] - keys_at[None, :]).astype(jnp.float32)
    scores = scores - slopes[None, :, None, None] * distance[None, None]
    piece_rows = pieces[:, first_row : first_row + rows_here]
    allowed = (keys_at[None, None, :] <= query_at[None, :, None]) | (
        piece_rows[:, :, None] == pieces[:, None, :]
    ) & (piece_rows[:, :, None] > 0)
    return jnp.where(allowed[:, None], scores, NEGATIVE)


def attend(queries, key_rows, values, pieces, slopes):
    length = queries.shape[1]
    block_rows = min(512, length)
    contexts = []
    log_sums = []
    for first_row in range(0, length, block_rows):
        scores = block_scores(
            queries[:, first_row : first_row + block_rows], key_rows, pieces, slopes, first_row
        )
        row_peak = jnp.max(scores, axis=-1, keepdims=True)
        exponent = jnp.exp(scores - row_peak)
        total_sum = jnp.sum(exponent, axis=-1, keepdims=True)
        weights = (exponent / total_sum).astype(jnp.bfloat16)
        contexts.append(
            jnp.einsum("ghqk,gkhd->gqhd", weights, values, preferred_element_type=jnp.float32)
        )
        log_sums.append(row_peak + jnp.log(total_sum))
    return (jnp.concatenate(contexts, 1), jnp.concatenate(log_sums, 2))


def attend_back(queries, key_rows, values, pieces, slopes, log_sums, grad_context):
    length = queries.shape[1]
    block_rows = min(512, length)
    scaling = 1.0 / math.sqrt(key_rows.shape[3])
    grad_queries = []
    grad_keys = jnp.zeros(key_rows.shape, jnp.float32)
    grad_values = jnp.zeros(values.shape, jnp.float32)
    for first_row in range(0, length, block_rows):
        query_rows = queries[:, first_row : first_row + block_rows]
        grad_rows = grad_context[:, first_row : first_row + block_rows]
        scores = block_scores(query_rows, key_rows, pieces, slopes, first_row)
        probability = jnp.exp(scores - log_sums[:, :, first_row : first_row + block_rows])
        grad_values = grad_values + jnp.einsum(
            "ghqk,gqhd->gkhd",
            probability.astype(jnp.bfloat16),
            grad_rows,
            preferred_element_type=jnp.float32,
        )
        grad_probs = jnp.einsum(
            "gqhd,gkhd->ghqk", grad_rows, values, preferred_element_type=jnp.float32
        )
        inner_sum = jnp.sum(probability * grad_probs, axis=-1, keepdims=True)
        grad_scores = (probability * (grad_probs - inner_sum)).astype(jnp.bfloat16)
        grad_queries.append(
            jnp.einsum("ghqk,gkhd->gqhd", grad_scores, key_rows, preferred_element_type=jnp.float32)
            * scaling
        )
        grad_keys = (
            grad_keys
            + jnp.einsum(
                "ghqk,gqhd->gkhd", grad_scores, query_rows, preferred_element_type=jnp.float32
            )
            * scaling
        )
    return (jnp.concatenate(grad_queries, 1), grad_keys, grad_values)


def body(
    tokens,
    cotangent,
    norm_gains,
    norm_shifts,
    query_key_value_weight,
    b_qv,
    output_weight,
    output_bias_vector,
    up_weight,
    b_up,
    down_weight,
    down_bias_vector,
    adapter_query_key_value_input,
    qkv_out,
    adapter_output_input,
    adapter_output_output,
    adapter_up_input,
    up_out,
    down_in,
    adapter_down_output,
    offsets,
    adapter_ids,
):
    row_count = tokens.shape[0]
    model_width = tokens.shape[1]
    position = lax.axis_index("tensor")
    seq_count = offsets.shape[0]
    full_rows = row_count * lax.axis_size("tensor")
    length = full_rows // seq_count
    local_width = query_key_value_weight.shape[2]
    local_heads = local_width // HEAD_DIM
    table_count = adapter_query_key_value_input.shape[0]
    indicator_matrix = (
        adapter_ids[:, :, None] == jnp.arange(table_count, dtype=jnp.int32)[None, None, :]
    ).astype(jnp.float32)
    one_low = indicator_matrix.astype(jnp.bfloat16)
    chosen_qkv_in = choose(adapter_query_key_value_input, one_low[:, 0])
    chosen_qkv_out = choose(
        qkv_out.reshape(table_count, qkv_out.shape[1], 3 * local_width), one_low[:, 0]
    )
    chosen_out_in = choose(adapter_output_input, one_low[:, 1])
    chosen_out_out = choose(adapter_output_output, one_low[:, 1])
    chosen_up_in = choose(adapter_up_input, one_low[:, 2])
    chosen_up_out = choose(up_out, one_low[:, 2])
    chosen_down_in = choose(down_in, one_low[:, 3])
    chosen_down_out = choose(adapter_down_output, one_low[:, 3])
    where_at = jnp.arange(length, dtype=jnp.int32)
    first_piece = (
        (where_at[None, :] >= offsets[:, 0:1]) & (where_at[None, :] < offsets[:, 0:1] + PIECE)
    ).astype(jnp.int32)
    second_piece = (
        (where_at[None, :] >= offsets[:, 1:2]) & (where_at[None, :] < offsets[:, 1:2] + PIECE)
    ).astype(jnp.int32)
    pieces = first_piece + 2 * second_piece
    head_ids = (position * local_heads + jnp.arange(local_heads, dtype=jnp.int32)).astype(
        jnp.float32
    )
    slopes = jnp.exp2(-8.0 * (head_ids + 1.0) / HEADS)
    qkv_flat = query_key_value_weight.reshape(model_width, 3 * local_width)
    qkv_bias = jnp.concatenate([b_qv[0], jnp.zeros_like(b_qv[0]), b_qv[1]])
    inputs = tokens.astype(jnp.float32)
    normed_local, scaled_first, inverse_first = layer_norm(inputs, norm_gains[0], norm_shifts[0])
    sent_in = normed_local.astype(jnp.bfloat16)
    arrived = lax.all_gather(sent_in, "tensor", axis=0, tiled=True)
    low_rank_query_key_value = low_rank_down(arrived, chosen_qkv_in)
    projection_result = (
        jnp.dot(arrived, qkv_flat, preferred_element_type=jnp.float32)
        + low_rank_upward(low_rank_query_key_value, chosen_qkv_out)
        + qkv_bias
    )
    projection_result = projection_result.astype(jnp.bfloat16).reshape(
        seq_count, length, 3, local_heads, HEAD_DIM
    )
    queries = projection_result[:, :, 0]
    key_rows = projection_result[:, :, 1]
    values = projection_result[:, :, 2]
    attended_context, log_sums = attend(queries, key_rows, values, pieces, slopes)
    attended_context = attended_context.astype(jnp.bfloat16).reshape(full_rows, local_width)
    rank_ctx = low_rank_down(attended_context, chosen_out_in)
    ctx_term = low_rank_upward(rank_ctx, chosen_out_out)
    row_block = attended_context
    side_path = lax.psum_scatter(
        (jnp.dot(row_block, output_weight, preferred_element_type=jnp.float32) + ctx_term).astype(
            jnp.bfloat16
        ),
        "tensor",
        scatter_dimension=0,
        tiled=True,
    ).astype(jnp.float32)
    middle = inputs + (side_path + output_bias_vector)
    normed_mid_local, scaled_second, inverse_second = layer_norm(
        middle, norm_gains[1], norm_shifts[1]
    )
    normalized_middle = lax.all_gather(
        normed_mid_local.astype(jnp.bfloat16), "tensor", axis=0, tiled=True
    )
    rank_upper = low_rank_down(normalized_middle, chosen_up_in)
    gate_input_rows = (
        jnp.dot(normalized_middle, up_weight, preferred_element_type=jnp.float32)
        + low_rank_upward(rank_upper, chosen_up_out)
        + b_up
    )
    hidden_value, hidden_slope = gelu_parts(gate_input_rows)
    hidden_rows = hidden_value.astype(jnp.bfloat16)
    rank_lower = low_rank_down(hidden_rows, chosen_down_in)
    lower_term = low_rank_upward(rank_lower, chosen_down_out)
    row_block = hidden_rows
    mlp_part = lax.psum_scatter(
        (jnp.dot(row_block, down_weight, preferred_element_type=jnp.float32) + lower_term).astype(
            jnp.bfloat16
        ),
        "tensor",
        scatter_dimension=0,
        tiled=True,
    ).astype(jnp.float32)
    result = (middle + (mlp_part + down_bias_vector)).astype(jnp.bfloat16)
    grad_out = lax.all_gather(cotangent, "tensor", axis=0, tiled=True)
    grad_rank_lower = low_rank_down(grad_out, chosen_down_out)
    table_down_out = rank_grad(rank_lower, grad_out)
    table_down_in = rank_grad(grad_rank_lower, hidden_rows)
    grad_hidden = dot_transposed(grad_out, down_weight) + low_rank_upward(
        grad_rank_lower, chosen_down_in
    )
    grad_gate = (grad_hidden * hidden_slope).astype(jnp.bfloat16)
    grad_rank_upper = low_rank_down(grad_gate, chosen_up_out)
    table_up_out = rank_grad(rank_upper, grad_gate)
    table_up_in = rank_grad(grad_rank_upper, normalized_middle)
    upper_back = low_rank_upward(grad_rank_upper, chosen_up_in)
    row_block = grad_gate
    grad_mid_norm = lax.psum_scatter(
        (dot_transposed(row_block, up_weight) + upper_back).astype(jnp.bfloat16),
        "tensor",
        scatter_dimension=0,
        tiled=True,
    ).astype(jnp.float32)
    grad_middle = cotangent.astype(jnp.float32) + norm_back(
        grad_mid_norm, scaled_second, inverse_second, norm_gains[1]
    )
    grad_mid_low = lax.all_gather(grad_middle.astype(jnp.bfloat16), "tensor", axis=0, tiled=True)
    grad_rank_ctx = low_rank_down(grad_mid_low, chosen_out_out)
    table_out_out = rank_grad(rank_ctx, grad_mid_low)
    table_out_in = rank_grad(grad_rank_ctx, attended_context)
    grad_context = dot_transposed(grad_mid_low, output_weight) + low_rank_upward(
        grad_rank_ctx, chosen_out_in
    )
    grad_context = grad_context.astype(jnp.bfloat16).reshape(
        seq_count, length, local_heads, HEAD_DIM
    )
    grad_queries, grad_keys, grad_values = attend_back(
        queries, key_rows, values, pieces, slopes, log_sums, grad_context
    )
    grad_proj = (
        jnp.stack([grad_queries, grad_keys, grad_values], 2)
        .astype(jnp.bfloat16)
        .reshape(full_rows, 3 * local_width)
    )
    grad_rank_qkv = low_rank_down(grad_proj, chosen_qkv_out)
    table_qkv_out = rank_grad(low_rank_query_key_value, grad_proj)
    table_qkv_in = rank_grad(grad_rank_qkv, arrived)
    first_back = low_rank_upward(grad_rank_qkv, chosen_qkv_in)
    row_block = grad_proj
    grad_first = lax.psum_scatter(
        (dot_transposed(row_block, qkv_flat) + first_back).astype(jnp.bfloat16),
        "tensor",
        scatter_dimension=0,
        tiled=True,
    ).astype(jnp.float32)
    grad_tokens = (
        grad_middle + norm_back(grad_first, scaled_first, inverse_first, norm_gains[0])
    ).astype(jnp.bfloat16)
    shared = lax.psum(
        (
            to_tables(table_qkv_in, indicator_matrix[:, 0]),
            to_tables(table_out_out, indicator_matrix[:, 1]),
            to_tables(table_up_in, indicator_matrix[:, 2]),
            to_tables(table_down_out, indicator_matrix[:, 3]),
        ),
        ("dp", "tensor"),
    )
    owned_sums = (
        lax.psum(
            to_tables(table_qkv_out, indicator_matrix[:, 0])
            .reshape(qkv_out.shape)
            .astype(jnp.bfloat16),
            "dp",
        ).astype(jnp.float32),
        lax.psum(to_tables(table_out_in, indicator_matrix[:, 1]).astype(jnp.bfloat16), "dp").astype(
            jnp.float32
        ),
        lax.psum(to_tables(table_up_out, indicator_matrix[:, 2]).astype(jnp.bfloat16), "dp").astype(
            jnp.float32
        ),
        lax.psum(
            to_tables(table_down_in, indicator_matrix[:, 3]).astype(jnp.bfloat16), "dp"
        ).astype(jnp.float32),
    )
    return (
        result,
        grad_tokens,
        shared[0],
        owned_sums[0],
        owned_sums[1],
        shared[1],
        shared[2],
        owned_sums[2],
        owned_sums[3],
        shared[3],
    )


def solution(mesh):
    placed = (
        P(("dp", "tensor"), None),
        P(("dp", "tensor"), None),
        P(),
        P(),
        P(None, None, "tensor"),
        P(None, "tensor"),
        P("tensor", None),
        P(),
        P(None, "tensor"),
        P("tensor"),
        P("tensor", None),
        P(),
        P(),
        P(None, None, None, "tensor"),
        P(None, None, "tensor"),
        P(),
        P(),
        P(None, None, "tensor"),
        P(None, None, "tensor"),
        P(),
        P("dp", None),
        P("dp", None),
    )
    return jax.shard_map(
        body,
        mesh=mesh,
        in_specs=placed,
        out_specs=(
            P(("dp", "tensor"), None),
            P(("dp", "tensor"), None),
            P(),
            P(None, None, None, "tensor"),
            P(None, None, "tensor"),
            P(),
            P(),
            P(None, None, "tensor"),
            P(None, None, "tensor"),
            P(),
        ),
        check_vma=False,
    )
```

profile of v0, /device:TPU:1, one launch (start us, length us, event | category | flops | bytes accessed | tf_op | source)
XLA Modules:
  0.0 1039.0 jit_solution(12768031125403590012)
XLA Ops:
  12.2 2.7 fusion.25
  17.7 9.0 copy.45
  38.1 59.8 %all-gather.5.cloned.1.call-done = bf16[1024,2048]{1,0:T(8,128)(2,1)} async-done(((bf16[256,2048]{1,0:T(8,128)(2,1)}), bf16[1024,2048]{1,0:T(8,128)(2,1)}) %all-gather.5.cloned.1.call-update) | async-done | bytes 4194320 | tf_op jit(solution)/shard_map/all_gather | solution.py:219
  97.9 3.5 fusion.69
  101.4 8.8 fusion.112
  110.3 4.5 add_convert_fusion.4
  114.7 6.2 reshape.957
  121.0 4.2 fusion.104
  125.2 3.1 copy.86
  129.7 4.5 fusion.110
  140.0 2.7 fusion.111
  148.7 2.4 fusion.64
  151.1 5.6 add_convert_fusion.3
  157.6 74.7 %reduce-scatter.5.cloned.1.call-done = bf16[256,2048]{1,0:T(8,128)(2,1)} async-done(((bf16[1024,2048]{1,0:T(8,128)(2,1)}), bf16[256,2048]{1,0:T(8,128)(2,1)}) %reduce-scatter.5.cloned.1.call-update) | async-done | bytes 1048592 | tf_op jit(solution)/shard_map/reduce_scatter | solution.py:237
  245.0 70.2 %all-gather.9.cloned.1.call-done = bf16[1024,2048]{1,0:T(8,128)(2,1)} async-done(((bf16[256,2048]{1,0:T(8,128)(2,1)}), bf16[1024,2048]{1,0:T(8,128)(2,1)}) %all-gather.9.cloned.1.call-update) | async-done | bytes 4194320 | tf_op jit(solution)/shard_map/all_gather | solution.py:272
  315.2 4.2 fusion.74
  319.4 13.4 %fusion.115 = f32[1024,2048]{1,0:T(8,128)} fusion(bf16[1024,2048]{1,0:T(8,128)(2,1)S(1)} %copy-done.14, bf16[2048,2048]{1,0:T(8,128)(2,1)} %param.32), kind=kOutput, calls=%fused_computation.205 | convolution fusion | flops 8589934592 | bytes 20971520 | tf_op jit(solution)/shard_map/dot_general | solution.py:46
  332.8 63.8 %all-gather.7.cloned.1.call-done = bf16[1024,2048]{1,0:T(8,128)(2,1)} async-done(((bf16[256,2048]{1,0:T(8,128)(2,1)}), bf16[1024,2048]{1,0:T(8,128)(2,1)}) %all-gather.7.cloned.1.call-update) | async-done | bytes 4194320 | tf_op jit(solution)/shard_map/all_gather | solution.py:249
  396.6 3.5 fusion.71
  400.1 13.3 %fusion.113 = f32[1024,2048]{1,0:T(8,128)} fusion(bf16[1024,2048]{1,0:T(8,128)(2,1)S(1)} %copy-done.9, bf16[2048,2048]{1,0:T(8,128)(2,1)} %param.30), kind=kOutput, calls=%fused_computation.203 | convolution fusion | flops 8589934592 | bytes 20971520 | tf_op jit(solution)/shard_map/dot_general | solution.py:254
  413.5 10.2 multiply_convert_fusion.2
  423.6 11.1 %fusion.6 = bf16[1024,2048]{1,0:T(8,128)(2,1)S(1)} fusion(f32[1024,2048]{1,0:T(8,128)S(1)} %get-tuple-element.55, f32[1024,2048]{1,0:T(8,128)} %fusion.115, f32[16,1024]{1,0:T(8,128)S(1)} %copy-done.49, bf16[1,16,2048]{2,0,1:T(2,128)(2,1)S(1)} %copy-done.45), kind=kOutput, calls=%fused_computation.8 | convolution fusion | flops 444596224 | bytes 21102592 | tf_op jit(solution)/shard_map/glr,grm->glm/dot_general | solution.py:64
  436.0 8.8 fusion.116
  444.9 5.3 add_convert_fusion.1
  450.7 3.5 fusion.73
  454.2 12.0 %fusion.114 = f32[1024,2048]{1,0:T(8,128)S(1)} fusion(bf16[1024,2048]{1,0:T(8,128)(2,1)S(1)} %copy-done.13, bf16[2048,2048]{1,0:T(8,128)(2,1)} %param.32), kind=kOutput, calls=%fused_computation.204 | convolution fusion | flops 8589934592 | bytes 20971520 | tf_op jit(solution)/shard_map/dot_general | solution.py:264
  466.2 5.5 add_convert_fusion.2
  471.8 53.9 %reduce-scatter.9.cloned.1.call-done = bf16[256,2048]{1,0:T(8,128)(2,1)} async-done(((bf16[1024,2048]{1,0:T(8,128)(2,1)}), bf16[256,2048]{1,0:T(8,128)(2,1)}) %reduce-scatter.9.cloned.1.call-update) | async-done | bytes 1048592 | tf_op jit(solution)/shard_map/reduce_scatter | solution.py:285
  525.7 2.4 fusion.33
  528.1 77.0 %reduce-scatter.7.cloned.1.call-done = bf16[256,2048]{1,0:T(8,128)(2,1)} async-done(((bf16[1024,2048]{1,0:T(8,128)(2,1)}), bf16[256,2048]{1,0:T(8,128)(2,1)}) %reduce-scatter.7.cloned.1.call-update) | async-done | bytes 1048592 | tf_op jit(solution)/shard_map/reduce_scatter | solution.py:263
  605.2 5.7 fusion.103
  613.9 4.1 fusion.123
  626.0 66.3 %all-gather.11.cloned.1.call-done = bf16[1024,2048]{1,0:T(8,128)(2,1)} async-done(((bf16[256,2048]{1,0:T(8,128)(2,1)}), bf16[1024,2048]{1,0:T(8,128)(2,1)}) %all-gather.11.cloned.1.call-update) | async-done | bytes 4194320 | tf_op jit(solution)/shard_map/all_gather | solution.py:294
  692.3 3.5 fusion.70
  700.4 2.8 multiply_reduce_fusion.1
  709.6 2.8 fusion.11
  712.4 3.4 multiply_reduce_fusion
  715.9 3.9 add_bitcast_fusion
  725.0 2.5 fusion.67
  727.8 9.5 fusion.118
  739.0 2.4 fusion.75
  741.4 7.5 add_convert_fusion
  749.7 4.1 fusion.120
  757.9 38.2 %all-reduce.7.cloned.1.call-done = (bf16[8,16,3,512]{3,1,2,0:T(8,128)(2,1)}, bf16[8,16,512]{2,1,0:T(8,128)(2,1)}, bf16[8,16,2048]{2,1,0:T(8,128)(2,1)}, bf16[8,16,2048]{2,1,0:T(8,128)(2,1)}) async-done(((bf16[8,16,3,512]{3,1,2,0:T(8,128)(2,1)}, bf16[8,16,512]{2,1,0:T(8,128)(2,1)}, bf16[8,16,2048]{2,1,0:T(8,128)(2,1)}, bf16[8,16,2048]{2,1,0:T(8,128)(2,1)}), (bf16[8,16,3,512]{3,1,2,0:T(8,128)(2,1)}, ...) | async-done | bytes 1572880 | tf_op jit(solution)/shard_map/psum | solution.py:336
  803.9 71.5 %reduce-scatter.11.cloned.1.call-done = bf16[256,2048]{1,0:T(8,128)(2,1)} async-done(((bf16[1024,2048]{1,0:T(8,128)(2,1)}), bf16[256,2048]{1,0:T(8,128)(2,1)}) %reduce-scatter.11.cloned.1.call-update) | async-done | bytes 1048592 | tf_op jit(solution)/shard_map/reduce_scatter | solution.py:317
  877.4 3.7 fusion.30
  881.1 144.0 %all-reduce.5.cloned.1.call-done = (f32[8,16,2048]{2,1,0:T(8,128)}, f32[8,16,2048]{2,1,0:T(8,128)}, f32[8,16,2048]{2,1,0:T(8,128)}, f32[8,16,2048]{2,1,0:T(8,128)}) async-done(((f32[8,16,2048]{2,1,0:T(8,128)}, f32[8,16,2048]{2,1,0:T(8,128)}, f32[8,16,2048]{2,1,0:T(8,128)}, f32[8,16,2048]{2,1,0:T(8,128)}), (f32[8,16,2048]{2,1,0:T(8,128)}, f32[8,16,2048]{2,1,0:T(8,128)}, f32[8,16,2048]{2,1,0:T(8,128)}, ...) | async-done | bytes 4194320 | tf_op jit(solution)/shard_map/psum | solution.py:326
  1025.1 2.4 copy.150
  (280 shorter events, 93.5 us)
Async XLA Ops:
  7.2 141.5 %copy-start = (bf16[512,2048]{1,0:T(8,128)(2,1)S(1)}, bf16[512,2048]{1,0:T(8,128)(2,1)}, u32[]{:S(2)}) copy-start(bf16[512,2048]{1,0:T(8,128)(2,1)} %param.28) | copy-start | bytes 6291460
  7.2 9.6 copy-start.42
  7.2 90.7 %all-gather.5.cloned.1.call-start = ((), (), s32[]{:S(2)}) async-start(), calls=%async_computation.4 | async-start | bytes 5242880 | tf_op jit(solution)/shard_map/all_gather | solution.py:219
  8.9 17.9 %copy-start.64 = (f32[256]{0:T(256)}, f32[256]{0:T(256)S(1)}, u32[]{:S(2)}) copy-start(f32[256]{0:T(256)S(1)} %broadcast_multiply_fusion.9) | copy-start | bytes 3076
  10.5 16.2 %copy-start.66 = (f32[256]{0:T(256)}, f32[256]{0:T(256)S(1)}, u32[]{:S(2)}) copy-start(f32[256]{0:T(256)S(1)} %add_rsqrt_fusion.1) | copy-start | bytes 3076
  11.4 15.4 %copy-start.52 = (f32[1,2048]{1,0:T(1,128)}, f32[1,2048]{1,0:T(1,128)S(1)}, u32[]{:S(2)}) copy-start(f32[1,2048]{1,0:T(1,128)S(1)} %get-tuple-element.28) | copy-start | bytes 24580
  14.9 217.4 %reduce-scatter.5.cloned.1.call-start = ((), (), s32[]{:S(2)}) async-start(), calls=%async_computation.5 | async-start | bytes 5242880 | tf_op jit(solution)/shard_map/reduce_scatter | solution.py:237
  17.7 11.7 %copy-start.73 = (f32[2,512]{1,0:T(2,128)S(1)}, f32[2,512]{1,0:T(2,128)}, u32[]{:S(2)}) copy-start(f32[2,512]{1,0:T(2,128)} %param.27) | copy-start | bytes 12292
  17.7 13.4 %copy-start.75 = (s32[1,4]{1,0:T(1,128)S(1)}, s32[1,4]{1,0:T(1,128)}, u32[]{:S(2)}) copy-start(s32[1,4]{1,0:T(1,128)} %param.43) | copy-start | bytes 52
  17.7 13.9 %copy-start.54 = (bf16[8,16,512]{2,1,0:T(8,128)(2,1)S(1)}, bf16[8,16,512]{2,1,0:T(8,128)(2,1)}, u32[]{:S(2)}) copy-start(bf16[8,16,512]{2,1,0:T(8,128)(2,1)} %param.36) | copy-start | bytes 393220
  17.7 14.4 %copy-start.38 = (bf16[8,16,2048]{2,1,0:T(8,128)(2,1)S(1)}, bf16[8,16,2048]{2,1,0:T(8,128)(2,1)}, u32[]{:S(2)}) copy-start(bf16[8,16,2048]{2,1,0:T(8,128)(2,1)} %param.37) | copy-start | bytes 1572868
  31.6 205.9 %copy-start.55 = (bf16[1,4,8]{2,1,0:T(4,128)(2,1)}, bf16[1,4,8]{2,1,0:T(4,128)(2,1)S(1)}, u32[]{:S(2)}) copy-start(bf16[1,4,8]{2,1,0:T(4,128)(2,1)S(1)} %get-tuple-element.47) | copy-start | bytes 196
  31.9 116.5 %copy-start.56 = (bf16[1,16,512]{2,0,1:T(2,128)(2,1)}, bf16[1,16,512]{2,0,1:T(2,128)(2,1)S(1)}, u32[]{:S(2)}) copy-start(bf16[1,16,512]{2,0,1:T(2,128)(2,1)S(1)} %fusion.65) | copy-start | bytes 49156
  32.1 78.1 %copy-start.40 = (bf16[1,16,1536]{2,0,1:T(2,128)(2,1)}, bf16[1,16,1536]{2,0,1:T(2,128)(2,1)S(1)}, u32[]{:S(2)}) copy-start(bf16[1,16,1536]{2,0,1:T(2,128)(2,1)S(1)} %fusion.89) | copy-start | bytes 147460
  34.1 67.3 %copy-start.34 = (bf16[1,16,2048]{2,0,1:T(2,128)(2,1)}, bf16[1,16,2048]{2,0,1:T(2,128)(2,1)S(1)}, u32[]{:S(2)}) copy-start(bf16[1,16,2048]{2,0,1:T(2,128)(2,1)S(1)} %fusion.59) | copy-start | bytes 196612
  101.4 8.9 copy-start.32
  125.2 14.7 %copy-start.16 = (bf16[1,1024,1,4,128]{4,3,2,1,0:T(4,128)(2,1)}, bf16[1,1024,1,4,128]{4,3,2,1,0:T(4,128)(2,1)S(1)}, u32[]{:S(2)}) copy-start(bf16[1,1024,1,4,128]{4,3,2,1,0:T(4,128)(2,1)S(1)} %get-tuple-element.25) | copy-start | bytes 3145732
  129.7 10.3 copy-start.24
  156.7 75.5 %copy-start.3 = (bf16[256,2048]{1,0:T(8,128)(2,1)S(1)}, bf16[256,2048]{1,0:T(8,128)(2,1)}, u32[]{:S(2)}) copy-start(bf16[256,2048]{1,0:T(8,128)(2,1)} %param.22) | copy-start | bytes 3145732
  156.7 75.5 %copy-start.51 = (f32[2048]{0:T(1024)S(1)}, f32[2048]{0:T(1024)}, u32[]{:S(2)}) copy-start(f32[2048]{0:T(1024)} %param.29) | copy-start | bytes 24580
  156.8 158.4 %all-gather.9.cloned.1.call-start = ((), (), s32[]{:S(2)}) async-start(), calls=%async_computation.8 | async-start | bytes 5242880 | tf_op jit(solution)/shard_map/all_gather | solution.py:272
  157.5 239.1 %all-gather.7.cloned.1.call-start = ((), (), s32[]{:S(2)}) async-start(), calls=%async_computation.6 | async-start | bytes 5242880 | tf_op jit(solution)/shard_map/all_gather | solution.py:249
  237.5 288.2 %reduce-scatter.9.cloned.1.call-start = ((), (), s32[]{:S(2)}) async-start(), calls=%async_computation.9 | async-start | bytes 5242880 | tf_op jit(solution)/shard_map/reduce_scatter | solution.py:285
  245.0 151.6 %copy-start.36 = (bf16[1,16,2048]{2,0,1:T(2,128)(2,1)}, bf16[1,16,2048]{2,0,1:T(2,128)(2,1)S(1)}, u32[]{:S(2)}) copy-start(bf16[1,16,2048]{2,0,1:T(2,128)(2,1)S(1)} %fusion.55) | copy-start | bytes 196612
  400.1 13.3 %copy-start.43 = (f32[1024,16]{0,1:T(8,128)}, f32[1024,16]{0,1:T(8,128)S(1)}, u32[]{:S(2)}) copy-start(f32[1024,16]{0,1:T(8,128)S(1)} %fusion.71) | copy-start | bytes 196612
  400.1 13.3 %copy-start.46 = (bf16[1,16,2048]{2,0,1:T(2,128)(2,1)S(1)}, bf16[1,16,2048]{2,0,1:T(2,128)(2,1)}, u32[]{:S(2)}) copy-start(bf16[1,16,2048]{2,0,1:T(2,128)(2,1)} %fusion.53) | copy-start | bytes 196612
  400.1 13.3 %copy-start.76 = (f32[2048]{0:T(1024)S(1)}, f32[2048]{0:T(1024)}, u32[]{:S(2)}) copy-start(f32[2048]{0:T(1024)} %param.31) | copy-start | bytes 24580
  413.4 10.2 copy-start.45
  413.5 10.2 copy-start.49
  413.5 22.5 %slice-start.6 = ((s8[8388608]{0:T(1024)(128)(4,1)}), s8[4194304]{0:T(1024)(128)(4,1)S(1)}, s32[]{:S(2)}) async-start(s8[8388608]{0:T(1024)(128)(4,1)} %bitcast.268), calls=%async_computation.20 | async-start | bytes 8388608
  423.6 12.3 %slice-start.7 = ((s8[8388608]{0:T(1024)(128)(4,1)}), s8[4194304]{0:T(1024)(128)(4,1)S(1)}, s32[]{:S(2)}) async-start(s8[8388608]{0:T(1024)(128)(4,1)} %bitcast.268), calls=%async_computation.21 | async-start | bytes 8388608
  434.8 10.1 copy-start.11
  450.2 154.9 %reduce-scatter.7.cloned.1.call-start = ((), (), s32[]{:S(2)}) async-start(), calls=%async_computation.7 | async-start | bytes 5242880 | tf_op jit(solution)/shard_map/reduce_scatter | solution.py:263
  471.7 54.0 %copy-start.63 = (f32[256]{0:T(256)S(1)}, f32[256]{0:T(256)}, u32[]{:S(2)}) copy-start(f32[256]{0:T(256)} %copy-done.62) | copy-start | bytes 3076
  471.7 54.0 %copy-start.69 = (f32[256]{0:T(256)S(1)}, f32[256]{0:T(256)}, u32[]{:S(2)}) copy-start(f32[256]{0:T(256)} %copy-done.68) | copy-start | bytes 3076
  471.7 133.4 %copy-start.70 = (f32[2048]{0:T(1024)S(1)}, f32[2048]{0:T(1024)}, u32[]{:S(2)}) copy-start(f32[2048]{0:T(1024)} %param.33) | copy-start | bytes 24580
  471.8 220.5 %all-gather.11.cloned.1.call-start = ((), (), s32[]{:S(2)}) async-start(), calls=%async_computation.10 | async-start | bytes 5242880 | tf_op jit(solution)/shard_map/all_gather | solution.py:294
  528.1 85.8 %copy-start.50 = (f32[16,1024]{1,0:T(8,128)S(1)}, f32[16,1024]{1,0:T(8,128)}, u32[]{:S(2)}) copy-start(f32[16,1024]{1,0:T(8,128)} %fusion.74) | copy-start | bytes 196612
  610.9 185.2 %all-reduce.7.cloned.1.call-start = ((), (), s32[]{:S(2)}) async-start(), calls=%async_computation.13 | async-start | bytes 3145728 | tf_op jit(solution)/shard_map/psum | solution.py:336
  724.8 12.5 %copy-start.4 = (bf16[1,1024,3,4,128]{1,4,3,2,0:T(8,128)(2,1)}, bf16[1,1024,3,4,128]{1,4,3,2,0:T(8,128)(2,1)S(1)}, u32[]{:S(2)}) copy-start(bf16[1,1024,3,4,128]{1,4,3,2,0:T(8,128)(2,1)S(1)} %maximum_convert_fusion) | copy-start | bytes 9437188
  727.8 9.5 copy-start.72
  727.8 10.2 copy-start.71
  727.8 11.2 %copy-start.41 = (bf16[1,16,1536]{2,0,1:T(2,128)(2,1)S(1)}, bf16[1,16,1536]{2,0,1:T(2,128)(2,1)}, u32[]{:S(2)}) copy-start(bf16[1,16,1536]{2,0,1:T(2,128)(2,1)} %copy-done.40) | copy-start | bytes 147460
  738.9 136.5 %reduce-scatter.11.cloned.1.call-start = ((), (), s32[]{:S(2)}) async-start(), calls=%async_computation.11 | async-start | bytes 5242880 | tf_op jit(solution)/shard_map/reduce_scatter | solution.py:317
  748.9 276.1 %all-reduce.5.cloned.1.call-start = ((), (), s32[]{:S(2)}) async-start(), calls=%async_computation.12 | async-start | bytes 8388608 | tf_op jit(solution)/shard_map/psum | solution.py:326
  757.9 117.6 %copy-start.53 = (f32[1,2048]{1,0:T(1,128)S(1)}, f32[1,2048]{1,0:T(1,128)}, u32[]{:S(2)}) copy-start(f32[1,2048]{1,0:T(1,128)} %copy-done.52) | copy-start | bytes 24580
  757.9 117.6 %copy-start.65 = (f32[256]{0:T(256)S(1)}, f32[256]{0:T(256)}, u32[]{:S(2)}) copy-start(f32[256]{0:T(256)} %copy-done.64) | copy-start | bytes 3076
  757.9 117.6 %copy-start.67 = (f32[256]{0:T(256)S(1)}, f32[256]{0:T(256)}, u32[]{:S(2)}) copy-start(f32[256]{0:T(256)} %copy-done.66) | copy-start | bytes 3076
  (51 other events, 186.9 us)
Sparse Core Ops, SparseCore 0:
  15.0 82.8 all-gather.4
  156.9 75.2 reduce-scatter.4
  233.9 81.2 all-gather.8
  317.3 79.2 all-gather.6
  450.3 75.3 reduce-scatter.8
  527.9 77.2 reduce-scatter.6
  611.0 81.2 all-gather.10
  739.1 57.0 all-reduce.6
  798.4 77.0 reduce-scatter.10
  883.3 141.6 all-reduce.4
where the time goes:
time: 1050 us; the launch traced here: 1040 us
  waiting for transfers between devices  720 us (69%)
  matrix products  202 us (19%)
  other arithmetic  58.5 us (6%)
  local copies, waits for them, and re-layouts  39.8 us (4%)
  between operations  17 us (2%)
    psum x1, waiting for transfers between devices, body(): lax.psum((to_tables(table_qkv_in, indicator_matrix[:, 0]), to_tables(tabl...  144 us
    reduce_scatter x1, waiting for transfers between devices, body(): lax.psum_scatter((jnp.dot(row_block, down_weight, preferred_element_type=...  77 us
    reduce_scatter x1, waiting for transfers between devices, body(): lax.psum_scatter((jnp.dot(row_block, output_weight, preferred_element_typ...  74.7 us
    reduce_scatter x1, waiting for transfers between devices, body(): lax.psum_scatter((dot_transposed(row_block, qkv_flat) + first_back).astyp...  71.5 us
    all_gather x1, waiting for transfers between devices, body(): grad_out = lax.all_gather(cotangent, 'tensor', axis=0, tiled=True)  70.2 us
    all_gather x1, waiting for transfers between devices, body(): lax.all_gather(grad_middle.astype(jnp.bfloat16), 'tensor', axis=0, tiled=...  66.3 us
    all_gather x1, waiting for transfers between devices, body(): lax.all_gather(normed_mid_local.astype(jnp.bfloat16), 'tensor', axis=0, t...  63.8 us
    all_gather x1, waiting for transfers between devices, body(): arrived = lax.all_gather(sent_in, 'tensor', axis=0, tiled=True)  59.8 us
  transfers between devices with their start and end apart: 10, of which 10 were waited for; matrix products, arithmetic and copies ran while one was open for 12% of the time, Pallas kernels for 0%

commit v1 on v0

v1 whole, which is shorter than its diff:
```python
import functools
import math

import jax
import jax.numpy as jnp
from jax import lax
from jax.experimental import pallas as pl
from jax.experimental.pallas import tpu as pltpu
from jax.sharding import PartitionSpec as P

HEADS = 16
HEAD_DIM = 128
PIECE = 256
PAD = 128
EPS = 1e-05
GELU_C = 0.7978845608028654
GELU_K = 0.044715
LOG2E = 1.4426950408889634
FAR = 1e32
F32 = jnp.float32
BF16 = jnp.bfloat16
AXES = ("dp", "tensor")
SLOT = (0, 2, 1, 3)
VM = pltpu.VMEM


def dot(a, b):
    return lax.dot_general(a, b, (((1,), (0,)), ((), ())), preferred_element_type=F32)


def dot_t(a, b):
    return lax.dot_general(a, b, (((1,), (1,)), ((), ())), preferred_element_type=F32)


def t_dot(a, b):
    return lax.dot_general(a, b, (((0,), (0,)), ((), ())), preferred_element_type=F32)


def whole(shape):
    zeros = (0,) * len(shape)
    return pl.BlockSpec(shape, lambda *_: zeros)


def params(mib=56):
    return pltpu.CompilerParams(vmem_limit_bytes=mib << 20)


def cost(flops, read):
    return pl.CostEstimate(flops=int(flops), bytes_accessed=int(read), transcendentals=0)


def fwd_qkv_kernel(x, w, a, b, bias, out, rank):
    @pl.when(pl.program_id(0) == 0)
    def _():
        rank[...] = dot_t(x[...], a[...]).astype(BF16)

    out[...] = (dot(x[...], w[0]) + dot(rank[...], b[...]) + bias[...]).astype(BF16)


def fwd_qkv(x, w3, a, b, bias):
    n, k = x.shape
    cols = w3.shape[2]
    return pl.pallas_call(
        fwd_qkv_kernel,
        grid=(3,),
        in_specs=[
            whole((n, k)),
            pl.BlockSpec((1, k, cols), lambda j: (j, 0, 0)),
            whole(a.shape),
            pl.BlockSpec((PAD, cols), lambda j: (0, j)),
            pl.BlockSpec((1, cols), lambda j: (0, j)),
        ],
        out_specs=[pl.BlockSpec((n, cols), lambda j: (0, j)), whole((n, PAD))],
        out_shape=[jax.ShapeDtypeStruct((n, 3 * cols), BF16), jax.ShapeDtypeStruct((n, PAD), BF16)],
        compiler_params=params(),
        cost_estimate=cost(6 * n * k * cols, 2 * (n * k + 3 * k * cols)),
        name="fwd_qkv",
    )(x, w3, a, b, bias)


def fwd_o_kernel(x, w, a, b, out, rank):
    r = dot_t(x[...], a[...]).astype(BF16)
    rank[...] = r
    out[...] = (dot(x[...], w[...]) + dot(r, b[...])).astype(BF16)


def fwd_o(x, w, a, b, tile):
    n, k = x.shape
    cols = w.shape[1]
    return pl.pallas_call(
        fwd_o_kernel,
        grid=(n // tile,),
        in_specs=[pl.BlockSpec((tile, k), lambda i: (i, 0)), whole(w.shape), whole(a.shape), whole(b.shape)],
        out_specs=[pl.BlockSpec((tile, cols), lambda i: (i, 0)), pl.BlockSpec((tile, PAD), lambda i: (i, 0))],
        out_shape=[jax.ShapeDtypeStruct((n, cols), BF16), jax.ShapeDtypeStruct((n, PAD), BF16)],
        compiler_params=params(),
        cost_estimate=cost(2 * n * k * cols, 2 * (n * k + k * cols + n * cols)),
        name="fwd_o",
    )(x, w, a, b)


def bwd_o_kernel(g, w, b, a, rank, x, out, tb, ta):
    first = pl.program_id(0) == 0
    r = dot_t(g[...], b[...]).astype(BF16)
    out[...] = (dot_t(g[...], w[...]) + dot(r, a[...])).astype(BF16)
    one = t_dot(rank[...], g[...])
    two = t_dot(r, x[...])

    @pl.when(first)
    def _():
        tb[...] = one
        ta[...] = two

    @pl.when(jnp.logical_not(first))
    def _():
        tb[...] += one
        ta[...] += two


def bwd_o(g, w, b, a, rank, x, tile):
    n, k = g.shape
    cols = w.shape[0]
    row = lambda c: pl.BlockSpec((tile, c), lambda i: (i, 0))
    return pl.pallas_call(
        bwd_o_kernel,
        grid=(n // tile,),
        in_specs=[row(k), whole(w.shape), whole(b.shape), whole(a.shape), row(PAD), row(cols)],
        out_specs=[row(cols), whole((PAD, k)), whole((PAD, cols))],
        out_shape=[
            jax.ShapeDtypeStruct((n, cols), BF16),
            jax.ShapeDtypeStruct((PAD, k), F32),
            jax.ShapeDtypeStruct((PAD, cols), F32),
        ],
        compiler_params=params(),
        cost_estimate=cost(2 * n * k * cols, 2 * (n * k + k * cols + n * cols)),
        name="bwd_o",
    )(g, w, b, a, rank, x)


def bwd_qkv_kernel(g, w, b, a, rank, x, out, tb, ta):
    first = pl.program_id(0) == 0
    cols = w.shape[2]
    r = dot_t(g[...], b[...]).astype(BF16)
    acc = dot(r, a[...])
    for j in range(3):
        acc = acc + dot_t(g[:, j * cols : (j + 1) * cols], w[j])
    out[...] = acc.astype(BF16)
    one = t_dot(rank[...], g[...])
    two = t_dot(r, x[...])

    @pl.when(first)
    def _():
        tb[...] = one
        ta[...] = two

    @pl.when(jnp.logical_not(first))
    def _():
        tb[...] += one
        ta[...] += two


def bwd_qkv(g, w3, b, a, rank, x, tile):
    n, k = g.shape
    cols = w3.shape[1]
    row = lambda c: pl.BlockSpec((tile, c), lambda i: (i, 0))
    return pl.pallas_call(
        bwd_qkv_kernel,
        grid=(n // tile,),
        in_specs=[row(k), whole(w3.shape), whole(b.shape), whole(a.shape), row(PAD), row(cols)],
        out_specs=[row(cols), whole((PAD, k)), whole((PAD, cols))],
        out_shape=[
            jax.ShapeDtypeStruct((n, cols), BF16),
            jax.ShapeDtypeStruct((PAD, k), F32),
            jax.ShapeDtypeStruct((PAD, cols), F32),
        ],
        compiler_params=params(),
        cost_estimate=cost(2 * n * k * cols, 2 * (n * k + k * cols + n * cols)),
        name="bwd_qkv",
    )(g, w3, b, a, rank, x)


def distances(ints, rows, step, dist):
    me, s0, s1 = ints[0], ints[1], ints[2]
    length = dist.shape[0]

    def piece(pos, none):
        one = jnp.where((pos >= s0) & (pos < s0 + PIECE), 1, none)
        return jnp.where((pos >= s1) & (pos < s1 + PIECE), 2, one)

    def rel(j):
        return ((j & 1) << 1) | (j >> 1)

    i = lax.broadcasted_iota(jnp.int32, (length, PAD), 0)
    kpos = (me ^ rel(i // rows)) * rows + i % rows
    kpos = kpos[:, :1]
    qpos = (me ^ rel(step)) * rows + lax.broadcasted_iota(jnp.int32, (1, rows), 1)
    seen = (kpos <= qpos) | (piece(kpos, -1) == piece(qpos, -2))
    dist[...] = jnp.where(seen, jnp.abs(kpos - qpos).astype(F32), FAR)


def attend_kernel(ints, slopes, q, k, v, ctx, lse, dist, vt):
    step = pl.program_id(0)
    rows = q.shape[0]
    heads = q.shape[1] // HEAD_DIM
    scale = LOG2E / math.sqrt(HEAD_DIM)
    distances(ints, rows, step, dist)

    @pl.when(step == 0)
    def _():
        vt[...] = v[...].T

    for h in range(heads):
        span = slice(h * HEAD_DIM, (h + 1) * HEAD_DIM)
        s = dot_t(k[:, span], q[:, span]) * scale - dist[...] * (slopes[h] * LOG2E)
        peak = jnp.max(s, axis=0, keepdims=True)
        e = jnp.exp2(s - peak)
        total = jnp.sum(e, axis=0, keepdims=True)
        c = dot(vt[span, :], e.astype(BF16)) * (1.0 / total)
        ctx[:, span] = c.T.astype(BF16)
        lse[h : h + 1, :] = peak + jnp.log2(total)


def attend(ints, slopes, proj, rows):
    length, three = proj.shape
    local = three // 3
    heads = local // HEAD_DIM
    return pl.pallas_call(
        attend_kernel,
        grid_spec=pltpu.PrefetchScalarGridSpec(
            num_scalar_prefetch=2,
            grid=(length // rows,),
            in_specs=[
                pl.BlockSpec((rows, local), lambda i, *_: (i, 0)),
                pl.BlockSpec((length, local), lambda i, *_: (0, 1)),
                pl.BlockSpec((length, local), lambda i, *_: (0, 2)),
            ],
            out_specs=[
                pl.BlockSpec((rows, local), lambda i, *_: (i, 0)),
                pl.BlockSpec((heads, rows), lambda i, *_: (0, i)),
            ],
            scratch_shapes=[VM((length, rows), F32), VM((local, length), BF16)],
        ),
        out_shape=[jax.ShapeDtypeStruct((length, local), BF16), jax.ShapeDtypeStruct((heads, length), F32)],
        compiler_params=params(),
        cost_estimate=cost(4 * length * length * local, 8 * length * local),
        name="attend",
    )(ints, slopes, proj, proj, proj)


def attend_back_kernel(ints, slopes, q, k, v, g, lse, out, dist, kt, gk, gv):
    step = pl.program_id(0)
    rows = q.shape[0]
    local = q.shape[1]
    heads = local // HEAD_DIM
    scale = 1.0 / math.sqrt(HEAD_DIM)
    distances(ints, rows, step, dist)

    @pl.when(step == 0)
    def _():
        kt[...] = k[...].T
        gk[...] = jnp.zeros_like(gk)
        gv[...] = jnp.zeros_like(gv)

    at = pl.ds(pl.multiple_of(step * rows, rows), rows)
    for h in range(heads):
        span = slice(h * HEAD_DIM, (h + 1) * HEAD_DIM)
        s = dot_t(k[:, span], q[:, span]) * (scale * LOG2E) - dist[...] * (slopes[h] * LOG2E)
        p = jnp.exp2(s - lse[h : h + 1, :])
        gv[:, span] += dot(p.astype(BF16), g[:, span])
        gp = dot_t(v[:, span], g[:, span])
        inner = jnp.sum(p * gp, axis=0, keepdims=True)
        gs = (p * (gp - inner)).astype(BF16)
        gk[:, span] += dot(gs, q[:, span])
        out[at, span] = (dot(kt[span, :], gs).T * scale).astype(BF16)

    @pl.when(step == pl.num_programs(0) - 1)
    def _():
        out[:, local : 2 * local] = (gk[...] * scale).astype(BF16)
        out[:, 2 * local :] = gv[...].astype(BF16)


def attend_back(ints, slopes, proj, g, lse, rows):
    length, three = proj.shape
    local = three // 3
    heads = local // HEAD_DIM
    return pl.pallas_call(
        attend_back_kernel,
        grid_spec=pltpu.PrefetchScalarGridSpec(
            num_scalar_prefetch=2,
            grid=(length // rows,),
            in_specs=[
                pl.BlockSpec((rows, local), lambda i, *_: (i, 0)),
                pl.BlockSpec((length, local), lambda i, *_: (0, 1)),
                pl.BlockSpec((length, local), lambda i, *_: (0, 2)),
                pl.BlockSpec((rows, local), lambda i, *_: (i, 0)),
                pl.BlockSpec((heads, rows), lambda i, *_: (0, i)),
            ],
            out_specs=pl.BlockSpec((length, three), lambda i, *_: (0, 0)),
            scratch_shapes=[
                VM((length, rows), F32),
                VM((local, length), BF16),
                VM((length, local), F32),
                VM((length, local), F32),
            ],
        ),
        out_shape=jax.ShapeDtypeStruct((length, three), BF16),
        compiler_params=params(),
        cost_estimate=cost(10 * length * length * local, 16 * length * local),
        name="attend_back",
    )(ints, slopes, proj, proj, proj, g, lse)


def gelu_parts(values):
    square = values * values
    tangent = jnp.tanh(GELU_C * (values + GELU_K * square * values))
    half = 0.5 * (1.0 + tangent)
    slope = half + (0.5 * GELU_C) * values * (1.0 - tangent * tangent) * (1.0 + 3.0 * GELU_K * square)
    return values * half, slope


def mlp_kernel(
    n0, n1, c0, c1, wu, wd, au, bu, ad, bd, bias, part, back, tuo, tdi, tui, tdo,
    nm, cot, up_rank, down_rank, g_up, g_down, acc, gacc,
):
    step = pl.program_id(0)
    last = pl.num_programs(0) - 1
    rows = n0.shape[0]

    @pl.when(step == 0)
    def _():
        nm[:rows] = n0[...]
        nm[rows:] = n1[...]
        cot[:rows] = c0[...]
        cot[rows:] = c1[...]
        up_rank[...] = dot_t(nm[...], au[...]).astype(BF16)
        g_down[...] = dot_t(cot[...], bd[...]).astype(BF16)
        down_rank[...] = jnp.zeros_like(down_rank)
        g_up[...] = jnp.zeros_like(g_up)
        acc[...] = jnp.zeros_like(acc)
        gacc[...] = jnp.zeros_like(gacc)

    gate = dot(nm[...], wu[...]) + dot(up_rank[...], bu[...]) + bias[...]
    value, slope = gelu_parts(gate)
    hidden = value.astype(BF16)
    grad = dot_t(cot[...], wd[...]) + dot(g_down[...], ad[...])
    grad_gate = (grad * slope).astype(BF16)
    down_rank[...] += dot_t(hidden, ad[...])
    g_up[...] += dot_t(grad_gate, bu[...])
    acc[...] += dot(hidden, wd[...])
    gacc[...] += dot_t(grad_gate, wu[...])
    tuo[...] = t_dot(up_rank[...], grad_gate)
    tdi[...] = t_dot(g_down[...], hidden)

    @pl.when(step == last)
    def _():
        dr = down_rank[...].astype(BF16)
        gu = g_up[...].astype(BF16)
        part[...] = (acc[...] + dot(dr, bd[...])).astype(BF16)
        back[...] = (gacc[...] + dot(gu, au[...])).astype(BF16)
        tui[...] = t_dot(gu, nm[...])
        tdo[...] = t_dot(dr, cot[...])


def mlp(n0, n1, c0, c1, wu, wd, au, bu, ad, bd, bias, tile):
    rows, width = n0.shape
    n = 2 * rows
    hidden = wu.shape[1]
    cut = lambda r: pl.BlockSpec((r, tile), lambda j: (0, j))
    return pl.pallas_call(
        mlp_kernel,
        grid=(hidden // tile,),
        in_specs=[
            whole((rows, width)), whole((rows, width)), whole((rows, width)), whole((rows, width)),
            cut(width), pl.BlockSpec((tile, width), lambda j: (j, 0)),
            whole(au.shape), cut(PAD), cut(PAD), whole(bd.shape), cut(1),
        ],
        out_specs=[
            whole((n, width)), whole((n, width)), cut(PAD), cut(PAD), whole((PAD, width)), whole((PAD, width)),
        ],
        out_shape=[
            jax.ShapeDtypeStruct((n, width), BF16),
            jax.ShapeDtypeStruct((n, width), BF16),
            jax.ShapeDtypeStruct((PAD, hidden), F32),
            jax.ShapeDtypeStruct((PAD, hidden), F32),
            jax.ShapeDtypeStruct((PAD, width), F32),
            jax.ShapeDtypeStruct((PAD, width), F32),
        ],
        scratch_shapes=[
            VM((n, width), BF16), VM((n, width), BF16), VM((n, PAD), BF16), VM((n, PAD), F32), VM((n, PAD), F32),
            VM((n, PAD), BF16), VM((n, width), F32), VM((n, width), F32),
        ],
        compiler_params=params(60),
        cost_estimate=cost(8 * n * width * hidden, 4 * width * hidden + 12 * n * width),
        name="mlp",
    )(n0, n1, c0, c1, wu, wd, au, bu, ad, bd, bias)


MESH = pl.DeviceIdType.MESH
CHUNKS = 4


def places():
    d, t = lax.axis_index("dp"), lax.axis_index("tensor")
    core, zh = d % 2, t // 2
    core_d = d + 1 - 2 * core
    near_t = t + 1 - 2 * (t % 2)
    left = d + 2 - 4 * ((d // 2) % 2)
    up = 4 - 8 * ((d // 4) % 2)
    return dict(
        moved=(core + zh) % 2 == 1,
        line=(d // 2) % 4,
        core=(core_d, t),
        near=(d, near_t),
        cross=(core_d, t + 2 - 4 * zh),
        left=(left, t),
        up=(d + up, t),
        both=(left + up, t),
    )


def greet(always, sometimes=(), when=None):
    barrier = pltpu.get_barrier_semaphore()
    for peer in always:
        pl.semaphore_signal(barrier, inc=1, device_id=peer, device_id_type=MESH)
    count = len(always)
    if sometimes:

        @pl.when(when)
        def _():
            for peer in sometimes:
                pl.semaphore_signal(barrier, inc=1, device_id=peer, device_id_type=MESH)

        count = count + len(sometimes) * when.astype(jnp.int32)
    pl.semaphore_wait(barrier, count)


def remote(src, dst, send, recv, peer):
    return pltpu.make_async_remote_copy(
        src_ref=src, dst_ref=dst, send_sem=send, recv_sem=recv, device_id=peer, device_id_type=MESH
    )


def unit_rows(v):
    centre = v - jnp.mean(v, axis=-1, keepdims=True)
    inverse = lax.rsqrt(jnp.mean(centre * centre, axis=-1, keepdims=True) + EPS)
    return centre * inverse, inverse


def unit_back(grad, scaled, inverse, gain):
    inner = grad * gain
    first = jnp.mean(inner, axis=-1, keepdims=True)
    second = jnp.mean(inner * scaled, axis=-1, keepdims=True)
    return inverse * (inner - first - scaled * second)


class Spread:
    def __init__(self, at, full, send, recv):
        self.at, self.full, self.send, self.recv = at, full, send, recv
        self.rows = full.shape[0] // 4
        self.step = self.rows // CHUNKS

    def block(self, k, i):
        return self.full.at[pl.ds(k * self.rows + i * self.step, self.step)]

    def side(self, i):
        return remote(self.block(0, i), self.block(1, i), self.send.at[0, i], self.recv.at[0, i], self.at["core"])

    def far(self, i):
        return remote(self.block(0, i), self.block(2, i), self.send.at[1, i], self.recv.at[1, i], self.at["near"])

    def onward(self, i):
        return remote(self.block(2, i), self.block(3, i), self.send.at[2, i], self.recv.at[2, i], self.at["core"])

    def post(self, i):
        self.far(i).start()
        self.side(i).start()

    def forward(self, i):
        self.far(i).wait_recv()
        self.onward(i).start()

    def finish(self):
        for i in range(CHUNKS):
            self.side(i).wait()
            self.far(i).wait_send()
            self.onward(i).wait()


class Gathered:
    def __init__(self, at, part, side, far, mix, send, recv):
        self.at, self.part, self.side, self.far, self.mix = at, part, side, far, mix
        self.send, self.recv = send, recv
        self.rows = part.shape[0] // 4
        self.step = self.rows // CHUNKS

    def away(self, i):
        src = self.part.at[pl.ds(3 * self.rows + i * self.step, self.step)]
        dst = self.side.at[pl.ds(self.rows + i * self.step, self.step)]
        return remote(src, dst, self.send.at[0, i], self.recv.at[0, i], self.at["core"])

    def home(self, i):
        src = self.part.at[pl.ds(self.rows + i * self.step, self.step)]
        dst = self.side.at[pl.ds(i * self.step, self.step)]
        return remote(src, dst, self.send.at[1, i], self.recv.at[1, i], self.at["core"])

    def over(self, i):
        here = pl.ds(i * self.step, self.step)
        return remote(self.mix.at[here], self.far.at[here], self.send.at[2, i], self.recv.at[2, i], self.at["near"])

    def begin(self):
        for i in range(CHUNKS):
            self.away(i).start()
        for i in range(CHUNKS):
            self.home(i).start()
        for i in range(CHUNKS):
            self.away(i).wait_recv()
            here = pl.ds(i * self.step, self.step)
            ours = self.part[pl.ds(2 * self.rows + i * self.step, self.step)].astype(F32)
            theirs = self.side[pl.ds(self.rows + i * self.step, self.step)].astype(F32)
            self.mix[here] = (ours + theirs).astype(BF16)
            self.over(i).start()

    def take(self, i):
        self.home(i).wait_recv()
        self.over(i).wait_recv()
        here = pl.ds(i * self.step, self.step)
        return self.part[here].astype(F32) + self.side[here].astype(F32) + self.far[here].astype(F32)

    def finish(self):
        for i in range(CHUNKS):
            self.away(i).wait_send()
            self.home(i).wait_send()
            self.over(i).wait_send()


def sems(*shape):
    return [pltpu.SemaphoreType.DMA(shape), pltpu.SemaphoreType.DMA(shape)]


def comm_params(number, mib=56):
    return pltpu.CompilerParams(collective_id=number, has_side_effects=True, vmem_limit_bytes=mib << 20)


VMEM_SPEC = pl.BlockSpec(memory_space=pltpu.VMEM)
ANY_SPEC = pl.BlockSpec(memory_space=pl.ANY)


def enter_kernel(tokens, w, gain, shift, full, tok, role, ts, tr, gs, gr, ws, wr, bs, br, local):
    at = places()
    moved = at["moved"]
    still = jnp.logical_not(moved)
    rows = tokens.shape[0]
    step = rows // CHUNKS
    peers = (at["left"], at["up"], at["both"])
    size = w.shape[1] // 4
    piece = pl.ds(pl.multiple_of(at["line"] * size, size), size)
    greet((at["core"], at["near"]), (at["cross"],) + peers, moved)

    def token(i):
        here = pl.ds(i * step, step)
        return remote(tokens.at[here], tok.at[here], ts.at[i], tr.at[i], at["cross"])

    def cross(j):
        return remote(w.at[j, piece], role.at[j, piece], ws.at[j], wr.at[j], at["cross"])

    def share(j, k):
        return remote(role.at[j, piece], role.at[j, piece], bs.at[j, k], br.at[j, k], peers[k])

    def own(j):
        return pltpu.make_async_copy(w.at[j], role.at[j], local.at[j])

    @pl.when(moved)
    def _():
        for i in range(CHUNKS):
            token(i).start()

    @pl.when(still)
    def _():
        tok[...] = tokens[...]
        for j in range(3):
            own(j).start()

    spread = Spread(at, full, gs, gr)
    for i in range(CHUNKS):
        here = slice(i * step, (i + 1) * step)

        @pl.when(moved)
        def _():
            token(i).wait_recv()

        unit, _ = unit_rows(tok[here].astype(F32))
        full[here] = (unit * gain[...] + shift[...]).astype(BF16)
        spread.post(i)

    @pl.when(moved)
    def _():
        for j in range(3):
            cross(j).start()

    for i in range(CHUNKS):
        spread.forward(i)

    @pl.when(moved)
    def _():
        for j in range(3):
            cross(j).wait_recv()
            for k in range(3):
                share(j, k).start()
        for i in range(CHUNKS):
            token(i).wait_send()
        for j in range(3):
            cross(j).wait_send()
            for k in range(3):
                share(j, k).wait()

    @pl.when(still)
    def _():
        for j in range(3):
            own(j).wait()

    spread.finish()


def enter(tokens, w3, gain, shift):
    rows, width = tokens.shape
    return pl.pallas_call(
        enter_kernel,
        in_specs=[VMEM_SPEC, ANY_SPEC, VMEM_SPEC, VMEM_SPEC],
        out_specs=[VMEM_SPEC, VMEM_SPEC, ANY_SPEC],
        out_shape=[
            jax.ShapeDtypeStruct((4 * rows, width), BF16),
            jax.ShapeDtypeStruct((rows, width), BF16),
            jax.ShapeDtypeStruct(w3.shape, BF16),
        ],
        scratch_shapes=sems(CHUNKS) + sems(3, CHUNKS) + sems(3) + sems(3, 3) + [pltpu.SemaphoreType.DMA((3,))],
        compiler_params=comm_params(1, 24),
        name="enter",
    )(tokens, w3, gain, shift)


def middle_kernel(part, tok, bias, gain, shift, full, mid, side, far, mix, rs, rr, gs, gr):
    at = places()
    greet((at["core"], at["near"]))
    step = tok.shape[0] // CHUNKS
    total = Gathered(at, part, side, far, mix, rs, rr)
    spread = Spread(at, full, gs, gr)
    total.begin()
    for i in range(CHUNKS):
        here = slice(i * step, (i + 1) * step)
        value = tok[here].astype(F32) + (total.take(i) + bias[...])
        mid[here] = value
        unit, _ = unit_rows(value)
        full[here] = (unit * gain[...] + shift[...]).astype(BF16)
        spread.post(i)
    for i in range(CHUNKS):
        spread.forward(i)
    total.finish()
    spread.finish()


def middle_rows(part, tok, bias, gain, shift):
    rows, width = tok.shape
    return pl.pallas_call(
        middle_kernel,
        in_specs=[VMEM_SPEC] * 5,
        out_specs=[VMEM_SPEC] * 2,
        out_shape=[jax.ShapeDtypeStruct((4 * rows, width), BF16), jax.ShapeDtypeStruct((rows, width), F32)],
        scratch_shapes=[VM((2 * rows, width), BF16), VM((rows, width), BF16), VM((rows, width), BF16)]
        + sems(3, CHUNKS) + sems(3, CHUNKS),
        compiler_params=comm_params(2, 40),
        name="middle_rows",
    )(part, tok, bias, gain, shift)


def turn_kernel(part, cot, mid, gain, full, grad, side, far, mix, rs, rr, gs, gr):
    at = places()
    greet((at["core"], at["near"]))
    step = cot.shape[0] // CHUNKS
    total = Gathered(at, part, side, far, mix, rs, rr)
    spread = Spread(at, full, gs, gr)
    total.begin()
    for i in range(CHUNKS):
        here = slice(i * step, (i + 1) * step)
        unit, inverse = unit_rows(mid[here])
        value = cot[here].astype(F32) + unit_back(total.take(i), unit, inverse, gain[...])
        grad[here] = value
        full[here] = value.astype(BF16)
        spread.post(i)
    for i in range(CHUNKS):
        spread.forward(i)
    total.finish()
    spread.finish()


def turn_rows(part, cot, mid, gain):
    rows, width = cot.shape
    return pl.pallas_call(
        turn_kernel,
        in_specs=[VMEM_SPEC] * 4,
        out_specs=[VMEM_SPEC] * 2,
        out_shape=[jax.ShapeDtypeStruct((4 * rows, width), BF16), jax.ShapeDtypeStruct((rows, width), F32)],
        scratch_shapes=[VM((2 * rows, width), BF16), VM((rows, width), BF16), VM((rows, width), BF16)]
        + sems(3, CHUNKS) + sems(3, CHUNKS),
        compiler_params=comm_params(3, 40),
        name="turn_rows",
    )(part, cot, mid, gain)


def leave_kernel(part, tok, grad, gain, out, side, far, mix, done, rs, rr, os, orr):
    at = places()
    moved = at["moved"]
    greet((at["core"], at["near"]), (at["cross"],), moved)
    step = tok.shape[0] // CHUNKS
    total = Gathered(at, part, side, far, mix, rs, rr)

    def back(i):
        here = pl.ds(i * step, step)
        return remote(done.at[here], out.at[here], os.at[i], orr.at[i], at["cross"])

    total.begin()
    for i in range(CHUNKS):
        here = slice(i * step, (i + 1) * step)
        unit, inverse = unit_rows(tok[here].astype(F32))
        value = (grad[here] + unit_back(total.take(i), unit, inverse, gain[...])).astype(BF16)

        @pl.when(moved)
        def _():
            done[here] = value
            back(i).start()

        @pl.when(jnp.logical_not(moved))
        def _():
            out[here] = value

    total.finish()

    @pl.when(moved)
    def _():
        for i in range(CHUNKS):
            back(i).wait()


def leave(part, tok, grad, gain):
    rows, width = tok.shape
    return pl.pallas_call(
        leave_kernel,
        in_specs=[VMEM_SPEC] * 4,
        out_specs=VMEM_SPEC,
        out_shape=jax.ShapeDtypeStruct((rows, width), BF16),
        scratch_shapes=[
            VM((2 * rows, width), BF16), VM((rows, width), BF16), VM((rows, width), BF16), VM((rows, width), BF16)
        ] + sems(3, CHUNKS) + sems(CHUNKS),
        compiler_params=comm_params(4, 40),
        name="leave",
    )(part, tok, grad, gain)


def routes(nd, nt):
    def lin(d, t):
        return d * nt + t

    every = [(d, t) for d in range(nd) for t in range(nt)]
    moved = [(d, t) for d, t in every if (d & 1) != (t >> 1)]
    both = [(lin(d, t), lin(d ^ 1, t ^ 2)) for d, t in moved]
    return dict(
        swap=both + [(lin(d, t), lin(d, t)) for d, t in every if (d & 1) == (t >> 1)],
        cross=both,
        core=[(lin(d, t), lin(d ^ 1, t)) for d, t in every],
        near=[(lin(d, t), lin(d, t ^ 1)) for d, t in every],
        left=[(lin(d, t), lin(d ^ 2, t)) for d, t in moved],
        up=[(lin(d, t), lin(d ^ 4, t)) for d, t in moved],
    )


def pick(table, e):
    return lax.dynamic_index_in_dim(table, e, 0, keepdims=False)


def norm_rows(values):
    centre = values - jnp.mean(values, axis=-1, keepdims=True)
    inverse = lax.rsqrt(jnp.mean(centre * centre, axis=-1, keepdims=True) + EPS)
    return centre * inverse, inverse


def norm_back(grad_rows, scaled, inverse, gain_row):
    inner = grad_rows * gain_row
    first = jnp.mean(inner, axis=-1, keepdims=True)
    second = jnp.mean(inner * scaled, axis=-1, keepdims=True)
    return inverse * (inner - first - scaled * second)


def body(
    tokens, cotangent, norm_gains, norm_shifts, query_key_value_weight, b_qv, output_weight,
    output_bias_vector, up_weight, b_up, down_weight, down_bias_vector, adapter_query_key_value_input,
    qkv_out, adapter_output_input, adapter_output_output, adapter_up_input, up_out, down_in,
    adapter_down_output, offsets, adapter_ids,
):
    nd, nt = lax.axis_size("dp"), lax.axis_size("tensor")
    route = routes(nd, nt)
    d, t = lax.axis_index("dp"), lax.axis_index("tensor")
    c, p = d % 2, (d // 2) % 4
    moved = c != t // 2
    me = 2 * c + t % 2
    rows, width = tokens.shape
    length = rows * nt
    local = output_weight.shape[0]
    local_heads = local // HEAD_DIM
    hidden_width = up_weight.shape[1]
    rank = adapter_up_input.shape[1]
    tables = adapter_up_input.shape[0]

    def go(x, name):
        return lax.ppermute(x, AXES, route[name])

    ids = adapter_ids[0]
    w3 = jnp.transpose(query_key_value_weight, (1, 0, 2))
    b3 = jnp.transpose(qkv_out, (0, 2, 1, 3))
    small = jnp.concatenate(
        [
            jnp.transpose(pick(b3, ids[0]), (1, 0, 2)).reshape(rank, 3 * local),
            pick(adapter_output_input, ids[1]),
            pick(up_out, ids[2]),
            pick(down_in, ids[3]),
        ],
        1,
    )
    small = go(small, "swap")
    biases = go(jnp.concatenate([b_qv.reshape(1, 2 * local), b_up.reshape(1, hidden_width)], 1), "swap")
    numbers = go(jnp.concatenate([offsets, adapter_ids], 1), "swap")
    cuts = [3 * local, 4 * local, 4 * local + hidden_width]
    bq, ao, bu, ad = jnp.split(small, cuts, 1)
    bias_q, bias_v, bias_up = jnp.split(biases, [local, 2 * local], 1)
    own_ids = numbers[0, 2:6]
    aq = pick(adapter_query_key_value_input, own_ids[0])
    bo = pick(adapter_output_output, own_ids[1])
    au = pick(adapter_up_input, own_ids[2])
    bd = pick(adapter_down_output, own_ids[3])

    def bring(weight, axis):
        size = weight.shape[axis] // 4
        r0 = go(lax.dynamic_slice_in_dim(weight, p * size, size, axis), "cross")
        r1 = go(r0, "left")
        r2 = go(r0, "up")
        r3 = go(r1, "up")
        parts = [r0, r1, r2, r3]
        whole = []
        for j in range(4):
            part = parts[j]
            for q in range(1, 4):
                part = jnp.where(p == q, parts[j ^ q], part)
            whole.append(part)
        return jnp.where(moved, jnp.concatenate(whole, axis), weight)

    gain = [norm_gains[i : i + 1] for i in range(2)]
    shift = [norm_shifts[i : i + 1] for i in range(2)]
    x, tok, wqkv = enter(tokens, w3, gain[0], shift[0])
    output_weight, up_weight, down_weight, cotangent, _ = lax.optimization_barrier(
        (output_weight, up_weight, down_weight, cotangent, x)
    )
    cot_own = go(cotangent, "swap")
    wo = bring(output_weight, 0)
    wu = bring(up_weight, 1)
    wd = bring(down_weight, 0)

    def gather(own):
        far = go(own, "near")
        side = go(own, "core")
        last = go(far, "core")
        return own, side, far, last

    def scatter(home, away):
        far = (away[:rows].astype(F32) + go(away[rows:], "core").astype(F32)).astype(BF16)
        far = go(far, "near")
        side = go(home[rows:], "core")
        return home[:rows].astype(F32) + side.astype(F32) + far.astype(F32)

    def wide(a):
        return jnp.pad(a, ((0, PAD - rank), (0, 0)))

    ints = jnp.concatenate([jnp.reshape(me, (1,)).astype(jnp.int32), numbers[0, 0:2]])
    head_ids = (me * local_heads + jnp.arange(local_heads, dtype=jnp.int32)).astype(F32)
    slopes = jnp.exp2(-8.0 * (head_ids + 1.0) / HEADS)
    bq, ao, bu, ad, aq, bo, au, bd = [wide(a) for a in (bq, ao, bu, ad, aq, bo, au, bd)]

    qkv_bias = jnp.concatenate([bias_q, jnp.zeros_like(bias_q), bias_v], 1)
    proj, rank_qkv = fwd_qkv(x, wqkv, aq, bq, qkv_bias)
    ctx, lse = attend(ints, slopes, proj, rows)
    part, rank_out = fwd_o(ctx, wo, ao, bo, rows)
    nm, middle = middle_rows(part, tok, output_bias_vector.reshape(1, width), gain[1], shift[1])
    n0, n1, n2, n3 = [nm[i * rows : (i + 1) * rows] for i in range(4)]
    c0, c1, c2, c3 = gather(cot_own)
    tile = hidden_width // 4
    p0, q0, tuo0, tdi0, tui0, tdo0 = mlp(n0, n1, c0, c1, wu, wd, au, bu, ad, bd, bias_up, tile)
    p1, q1, tuo1, tdi1, tui1, tdo1 = mlp(n2, n3, c2, c3, wu, wd, au, bu, ad, bd, bias_up, tile)
    t_up_out, t_down_in, t_up_in, t_down_out = tuo0 + tuo1, tdi0 + tdi1, tui0 + tui1, tdo0 + tdo1
    gm, grad_middle = turn_rows(jnp.concatenate([q0, q1], 0), cot_own, middle, gain[1])
    result = (middle + (scatter(p0, p1) + down_bias_vector)).astype(BF16)
    grad_ctx, t_out_out, t_out_in = bwd_o(gm, wo, bo, ao, rank_out, ctx, rows)
    grad_proj = attend_back(ints, slopes, proj, grad_ctx, lse, rows)
    gx, t_qkv_out, t_qkv_in = bwd_qkv(grad_proj, wqkv, bq, aq, rank_qkv, x, rows)
    in_grad = leave(gx, tok, grad_middle, gain[0])

    result = go(result, "swap")

    def owned(pieces):
        return lax.all_gather(go(jnp.concatenate(pieces, 1).astype(BF16), "swap"), "dp", axis=0)

    everyone = lax.all_gather(adapter_ids, "dp", axis=0, tiled=True)
    hot = (everyone[:, :, None] == jnp.arange(tables, dtype=jnp.int32)).astype(BF16)

    def combine(per, which):
        return jnp.einsum("se,srm->erm", hot[:, which], per, preferred_element_type=F32)

    own = owned([t[:rank] for t in (t_qkv_out, t_out_in, t_up_out, t_down_in)])
    g_qkv_out = jnp.einsum(
        "se,srkm->erkm", hot[:, 0], own[:, :, : cuts[0]].reshape(nd, rank, 3, local), preferred_element_type=F32
    )
    g_out_in = combine(own[:, :, cuts[0] : cuts[1]], 1)
    g_up_out = combine(own[:, :, cuts[1] : cuts[2]], 2)
    g_down_in = combine(own[:, :, cuts[2] :], 3)

    shared = jnp.stack([t[:rank] for t in (t_qkv_in, t_out_out, t_up_in, t_down_out)]).astype(BF16)
    shared = shared.astype(F32) + go(shared, "core").astype(F32)
    shared = (shared + go(shared.astype(BF16), "near").astype(F32)).astype(BF16)
    quarter = width // 4
    mine = lax.dynamic_slice_in_dim(shared, me * quarter, quarter, 2)
    mine = go(mine, "swap")
    mine = lax.all_gather(mine, "dp", axis=0)
    sums = jnp.einsum("ske,skrm->kerm", hot.transpose(0, 1, 2), mine, preferred_element_type=F32)
    whole = lax.all_gather(sums.astype(BF16), "tensor", axis=3, tiled=True).astype(F32)
    return (
        result, in_grad, whole[0], g_qkv_out, g_out_in, whole[1], whole[2], g_up_out, g_down_in, whole[3],
    )


def solution(mesh):
    placed = (
        P(("dp", "tensor"), None), P(("dp", "tensor"), None), P(), P(), P(None, None, "tensor"), P(None, "tensor"),
        P("tensor", None), P(), P(None, "tensor"), P("tensor"), P("tensor", None), P(), P(),
        P(None, None, None, "tensor"), P(None, None, "tensor"), P(), P(), P(None, None, "tensor"),
        P(None, None, "tensor"), P(), P("dp", None), P("dp", None),
    )
    return jax.shard_map(
        body, mesh=mesh, in_specs=placed,
        out_specs=(
            P(("dp", "tensor"), None), P(("dp", "tensor"), None), P(), P(None, None, None, "tensor"),
            P(None, None, "tensor"), P(), P(), P(None, None, "tensor"), P(None, None, "tensor"), P(),
        ),
        check_vma=False,
    )
```

time: 1050 us -> 774 us (0.74)
  waiting for transfers between devices: 720 us -> 110 us
  Pallas kernels: 0 us -> 428 us
  matrix products: 202 us -> 3.77 us
  starting transfers between devices: 0.99 us -> 66.7 us
  local copies, waits for them, and re-layouts: 39.8 us -> 68.8 us
  blocking collectives: 0 us -> 17.6 us
  other arithmetic: 58.5 us -> 41.4 us
  between operations: 17 us -> 30.8 us
    pallas_call x0 -> x12, Pallas kernels: none -> 428 us  [the longest x1 87.3 us: leave(): pl.pallas_call(leave_kernel, in_specs=[VMEM_SPEC] * 4, out_specs=VMEM_SPE...]
    reduce_scatter x4 -> x0, waiting for transfers between devices: 277 us -> none  [the longest x1 77 us: body(): lax.psum_scatter((jnp.dot(row_block, down_weight, preferred_element_type=...]
    all_gather x4 -> x2, waiting for transfers between devices: 260 us -> 0.02 us  [the longest x1 0.02 us: owned(): lax.all_gather(go(jnp.concatenate(pieces, 1).astype(BF16), 'swap'), 'dp',...]
    dot_general x52 -> x5, matrix products: 202 us -> 3.77 us  [the longest x3 2.05 us: combine(): jnp.einsum('se,srm->erm', hot[:, which], per, preferred_element_type=F32)]
    psum x2 -> x0, waiting for transfers between devices: 182 us -> none  [the longest x1 144 us: body(): lax.psum((to_tables(table_qkv_in, indicator_matrix[:, 0]), to_tables(tabl...]
    ppermute x0 -> x27, waiting for transfers between devices: none -> 110 us  [go(): return lax.ppermute(x, AXES, route[name])]
    ppermute x0 -> x27, starting transfers between devices: none -> 66.6 us  [go(): return lax.ppermute(x, AXES, route[name])]
    convert_element_type x17 -> x5, other arithmetic: 33.2 us -> 10.1 us  [the longest x1 3.48 us: body(): result = (middle + (scatter(p0, p1) + down_bias_vector)).astype(BF16)]
  transfers between devices with their start and end apart: 10 -> 29, of which waited for: 10 -> 6; matrix products, arithmetic and copies ran while one was open for 12% -> 10% of each run, Pallas kernels for 0% -> 38%
where the time goes in v1:
time: 774 us; the launch traced here: 766 us
  Pallas kernels  428 us (55%)
  waiting for transfers between devices  110 us (14%)
  local copies, waits for them, and re-layouts  68.8 us (9%)
  starting transfers between devices  66.7 us (9%)
  other arithmetic  41.4 us (5%)
  between operations  30.8 us (4%)
  blocking collectives  17.6 us (2%)
    ppermute x27, waiting for transfers between devices, go(): return lax.ppermute(x, AXES, route[name])  110 us
    pallas_call x1, Pallas kernels, leave(): pl.pallas_call(leave_kernel, in_specs=[VMEM_SPEC] * 4, out_specs=VMEM_SPE...  87.3 us
    pallas_call x1, Pallas kernels, enter(): pl.pallas_call(enter_kernel, in_specs=[VMEM_SPEC, ANY_SPEC, VMEM_SPEC, VM...  83.3 us
    ppermute x27, starting transfers between devices, go(): return lax.ppermute(x, AXES, route[name])  66.6 us
    pallas_call x2, Pallas kernels, mlp(): pl.pallas_call(mlp_kernel, grid=(hidden // tile,), in_specs=[whole((rows,...  64 us
    pallas_call x1, Pallas kernels, middle_rows(): pl.pallas_call(middle_kernel, in_specs=[VMEM_SPEC] * 5, out_specs=[VMEM_S...  51.2 us
    pallas_call x1, Pallas kernels, turn_rows(): pl.pallas_call(turn_kernel, in_specs=[VMEM_SPEC] * 4, out_specs=[VMEM_SPE...  51.1 us
    unnamed x72, local copies, waits for them, and re-layouts  34.1 us
  transfers between devices with their start and end apart: 29, of which 6 were waited for; matrix products, arithmetic and copies ran while one was open for 10% of the time, Pallas kernels for 38%

profile of v1, /device:TPU:1, one launch (start us, length us, event | category | flops | bytes accessed | tf_op | source)
XLA Modules:
  0.0 766.4 jit_solution(11200299278141207547)
XLA Ops:
  8.0 5.6 collective-permute-start
  14.5 2.8 copy-done.2
  18.5 83.3 %enter.1 = (bf16[1024,2048]{1,0:T(8,128)(2,1)S(1)}, bf16[256,2048]{1,0:T(8,128)(2,1)S(1)}, bf16[3,2048,512]{2,1,0:T(8,128)(2,1)S(1)}) custom-call(bf16[256,2048]{1,0:T(8,128)(2,1)S(1)} %copy-done.10, bf16[3,2048,512]{2,1,0:T(8,128)(2,1)S(1)} %bitcast.84, f32[1,2048]{1,0:T(1,128)S(1)} %get-tuple-element.160.gain, f32[1,2048]{1,0:T(1,128)S(1)} %get-tuple-element.147.shift), custom_call_target="tpu_custom_call" | custom-call | tf_op jit(solution)/shard_map/enter/pallas_call | solution.py:626
  101.9 2.6 copy-done.12
  106.5 3.2 constant_dynamic-slice_fusion.1
  122.5 4.5 collective-permute-start.1
  130.1 4.5 collective-permute-start.3
  135.3 3.1 constant_dynamic-slice_fusion
  140.3 50.7 %collective-permute-done.9 = bf16[2048,512]{1,0:T(8,128)(2,1)} collective-permute-done((bf16[2048,512]{1,0:T(8,128)(2,1)}, bf16[2048,512]{1,0:T(8,128)(2,1)}, u32[]{:S(2)}, u32[]{:S(2)}) %collective-permute-start.9) | collective-permute-done | bytes 2097184 | tf_op jit(solution)/shard_map/ppermute | solution.py:813
  212.1 3.2 collective-permute-start.4
  217.4 13.2 %fwd_qkv.1 = (bf16[1024,1536]{1,0:T(8,128)(2,1)}, bf16[1024,128]{1,0:T(8,128)(2,1)}) custom-call(bf16[1024,2048]{1,0:T(8,128)(2,1)} %copy-done.13, bf16[3,2048,512]{2,1,0:T(8,128)(2,1)} %copy-done.12, bf16[128,2048]{1,0:T(8,128)(2,1)} %pad.27.a, bf16[128,1536]{1,0:T(8,128)(2,1)} %pad.28.b, f32[1,1536]{1,0:T(1,128)} %fusion.19.bias), custom_call_target="tpu_custom_call" | custom-call | flops 6442450944 | bytes 10485760 | tf_op jit(solution)/shard_map/fwd_qkv/pallas_call | solution.py:63
  230.6 3.2 collective-permute-start.5
  235.9 2.3 collective-permute-start.14
  238.3 3.1 collective-permute-start.11
  243.9 17.5 %attend.1 = (bf16[1024,512]{1,0:T(8,128)(2,1)}, f32[4,1024]{1,0:T(4,128)}) custom-call(s32[3]{0:T(128)} %pad_add_fusion.1.ints, f32[4]{0:T(128)} %multiply_exponential_fusion.slopes, bf16[1024,1536]{1,0:T(8,128)(2,1)} %get-tuple-element.47.q.k.v, bf16[1024,1536]{1,0:T(8,128)(2,1)} %get-tuple-element.47.q.k.v, bf16[1024,1536]{1,0:T(8,128)(2,1)} %get-tuple-element.47.q.k.v), custom_call_target="tpu_custom_call" | custom-call | flops 2147483648 | bytes 4194304 | tf_op jit(solution)/shard_map/attend/pallas_call | solution.py:227
  265.4 2.3 maximum_select_fusion.2.w
  267.7 7.9 %fwd_o.1 = (bf16[1024,2048]{1,0:T(8,128)(2,1)}, bf16[1024,128]{1,0:T(8,128)(2,1)}) custom-call(bf16[1024,512]{1,0:T(8,128)(2,1)} %get-tuple-element.48.x, bf16[512,2048]{1,0:T(8,128)(2,1)} %maximum_select_fusion.2.w, bf16[128,512]{1,0:T(8,128)(2,1)} %pad.29.a, bf16[128,2048]{1,0:T(8,128)(2,1)} %pad.30.b), custom_call_target="tpu_custom_call" | custom-call | flops 2147483648 | bytes 7340032 | tf_op jit(solution)/shard_map/fwd_o/pallas_call | solution.py:90
  277.8 51.2 %middle_rows.1 = (bf16[1024,2048]{1,0:T(8,128)(2,1)S(1)}, f32[256,2048]{1,0:T(8,128)S(1)}) custom-call(bf16[1024,2048]{1,0:T(8,128)(2,1)S(1)} %copy-done.4, bf16[256,2048]{1,0:T(8,128)(2,1)S(1)} %get-tuple-element.51.tok, f32[1,2048]{1,0:T(1,128)S(1)} %bitcast.85, f32[1,2048]{1,0:T(1,128)S(1)} %get-tuple-element.161.gain, f32[1,2048]{1,0:T(1,128)S(1)} %get-tuple-element.146.shift), custom_call_target="tpu_custom_call" | custom-call | tf_op jit(solution)/shard_map/middle_rows/pallas_call | solution.py:663
  329.0 2.2 fusion.21
  331.2 2.8 collective-permute-start.16
  334.1 3.1 collective-permute-start.15
  337.3 3.5 select_select_fusion.7
  340.8 4.9 maximum_select_fusion.wu
  345.7 12.9 %collective-permute-done.16 = bf16[512,2048]{1,0:T(8,128)(2,1)} collective-permute-done((bf16[512,2048]{1,0:T(8,128)(2,1)}, bf16[512,2048]{1,0:T(8,128)(2,1)}, u32[]{:S(2)}, u32[]{:S(2)}) %collective-permute-start.16) | collective-permute-done | bytes 2097184 | tf_op jit(solution)/shard_map/ppermute | solution.py:813
  358.5 22.5 %collective-permute-done.15 = bf16[512,2048]{1,0:T(8,128)(2,1)} collective-permute-done((bf16[512,2048]{1,0:T(8,128)(2,1)S(1)}, bf16[512,2048]{1,0:T(8,128)(2,1)}, u32[]{:S(2)}, u32[]{:S(2)}) %collective-permute-start.15) | collective-permute-done | bytes 2097184 | tf_op jit(solution)/shard_map/ppermute | solution.py:813
  381.0 3.3 select_select_fusion.3
  384.4 6.7 maximum_select_fusion.1.wd
  391.1 31.9 %mlp.3 = (bf16[512,2048]{1,0:T(8,128)(2,1)}, bf16[512,2048]{1,0:T(8,128)(2,1)}, f32[128,2048]{1,0:T(8,128)}, f32[128,2048]{1,0:T(8,128)}, f32[128,2048]{1,0:T(8,128)}, /*index=5*/f32[128,2048]{1,0:T(8,128)}) custom-call(bf16[256,2048]{1,0:T(8,128)(2,1)} %get-tuple-element.134.n0, bf16[256,2048]{1,0:T(8,128)(2,1)} %get-tuple-element.133.n1, ...), custom_call_target="tpu_custom_call" | custom-call | flops 17179869184 | bytes 29360128 | tf_op jit(solution)/shard_map/mlp/pallas_call | solution.py:369
  423.0 32.1 %mlp.2 = (bf16[512,2048]{1,0:T(8,128)(2,1)}, bf16[512,2048]{1,0:T(8,128)(2,1)}, f32[128,2048]{1,0:T(8,128)}, f32[128,2048]{1,0:T(8,128)}, f32[128,2048]{1,0:T(8,128)}, /*index=5*/f32[128,2048]{1,0:T(8,128)}) custom-call(bf16[256,2048]{1,0:T(8,128)(2,1)} %get-tuple-element.135.n0, bf16[256,2048]{1,0:T(8,128)(2,1)} %get-tuple-element.132.n1, ...), custom_call_target="tpu_custom_call" | custom-call | flops 17179869184 | bytes 29360128 | tf_op jit(solution)/shard_map/mlp/pallas_call | solution.py:369
  455.1 2.5 pad_maximum_fusion.part
  457.6 51.1 %turn_rows.1 = (bf16[1024,2048]{1,0:T(8,128)(2,1)S(1)}, f32[256,2048]{1,0:T(8,128)S(1)}) custom-call(bf16[1024,2048]{1,0:T(8,128)(2,1)S(1)} %pad_maximum_fusion.part, bf16[256,2048]{1,0:T(8,128)(2,1)} %collective-permute-done.7.c0.cot, f32[256,2048]{1,0:T(8,128)S(1)} %get-tuple-element.52.mid, f32[1,2048]{1,0:T(1,128)S(1)} %get-tuple-element.161.gain), custom_call_target="tpu_custom_call" | custom-call | tf_op jit(solution)/shard_map/turn_rows/pallas_call | solution.py:697
  512.2 11.3 %bwd_o.1 = (bf16[1024,512]{1,0:T(8,128)(2,1)}, f32[128,2048]{1,0:T(8,128)}, f32[128,512]{1,0:T(8,128)}) custom-call(bf16[1024,2048]{1,0:T(8,128)(2,1)} %copy-done.7, bf16[512,2048]{1,0:T(8,128)(2,1)} %maximum_select_fusion.2.w, bf16[128,2048]{1,0:T(8,128)(2,1)} %pad.30.b, bf16[128,512]{1,0:T(8,128)(2,1)} %pad.29.a, ...), custom_call_target="tpu_custom_call" | custom-call | flops 2147483648 | bytes 7340032 | tf_op jit(solution)/shard_map/bwd_o/pallas_call | solution.py:124
  524.3 24.7 %attend_back.1.g = bf16[1024,1536]{1,0:T(8,128)(2,1)} custom-call(s32[3]{0:T(128)} %pad_add_fusion.1.ints, f32[4]{0:T(128)} %multiply_exponential_fusion.slopes, bf16[1024,1536]{1,0:T(8,128)(2,1)} %get-tuple-element.47.q.k.v, bf16[1024,1536]{1,0:T(8,128)(2,1)} %get-tuple-element.47.q.k.v, bf16[1024,1536]{1,0:T(8,128)(2,1)} %get-tuple-element.47.q.k.v, ...), custom_call_target="tpu_custom_call" | custom-call | flops 5368709120 | bytes 8388608 | tf_op jit(solution)/shard_map/attend_back/pallas_call | solution.py:286
  549.0 16.0 %bwd_qkv.1 = (bf16[1024,2048]{1,0:T(8,128)(2,1)}, f32[128,1536]{1,0:T(8,128)}, f32[128,2048]{1,0:T(8,128)}) custom-call(bf16[1024,1536]{1,0:T(8,128)(2,1)} %attend_back.1.g, bf16[3,2048,512]{2,1,0:T(8,128)(2,1)} %copy-done.12, bf16[128,1536]{1,0:T(8,128)(2,1)} %pad.28.b, bf16[128,2048]{1,0:T(8,128)(2,1)} %pad.27.a, ...), custom_call_target="tpu_custom_call" | custom-call | flops 6442450944 | bytes 13631488 | tf_op jit(solution)/shard_map/bwd_qkv/pallas_call | solution.py:166
  567.9 7.3 collective-permute-start.26
  578.0 2.4 collective-permute-done.26
  582.1 2.3 slice.164
  585.9 8.1 %collective-permute-done.24 = bf16[4,16,2048]{2,1,0:T(8,128)(2,1)S(1)} collective-permute-done((bf16[4,16,2048]{2,1,0:T(8,128)(2,1)}, bf16[4,16,2048]{2,1,0:T(8,128)(2,1)S(1)}, u32[]{:S(2)}, u32[]{:S(2)}) %collective-permute-start.24) | collective-permute-done | bytes 262176 | tf_op jit(solution)/shard_map/ppermute | solution.py:813
  595.0 3.7 collective-permute-start.25
  598.6 7.5 all-gather.2
  606.3 2.5 slice.160
  608.9 10.0 %all-gather = bf16[32,16,512]{2,1,0:T(8,128)(2,1)S(1)} all-gather(bf16[4,16,512]{2,1,0:T(8,128)(2,1)S(1)} %collective-permute-done.25), channel_id=2, replica_groups=mesh['dp'=8,'tensor'=4] {'dp'}, dimensions={0}, use_global_device_ids=true | all-gather | bytes 589824 | tf_op jit(solution)/shard_map/all_gather | solution.py:928
  618.9 2.6 add_convert_fusion.1
  624.4 2.2 copy-done.3
  628.2 87.3 %leave.1 = bf16[256,2048]{1,0:T(8,128)(2,1)S(1)} custom-call(bf16[1024,2048]{1,0:T(8,128)(2,1)S(1)} %copy-done.3, bf16[256,2048]{1,0:T(8,128)(2,1)S(1)} %get-tuple-element.51.tok, f32[256,2048]{1,0:T(8,128)S(1)} %copy-done.9, f32[1,2048]{1,0:T(1,128)S(1)} %get-tuple-element.160.gain), custom_call_target="tpu_custom_call" | custom-call | tf_op jit(solution)/shard_map/leave/pallas_call | solution.py:745
  715.5 3.5 add_convert_fusion
  719.0 5.3 collective-permute-start.22
  735.2 13.1 %collective-permute-done.22 = bf16[256,2048]{1,0:T(8,128)(2,1)S(1)} collective-permute-done((bf16[256,2048]{1,0:T(8,128)(2,1)}, bf16[256,2048]{1,0:T(8,128)(2,1)S(1)}, u32[]{:S(2)}, u32[]{:S(2)}) %collective-permute-start.22) | collective-permute-done | bytes 1048608 | tf_op jit(solution)/shard_map/ppermute | solution.py:813
  (172 shorter events, 82.1 us)
Async XLA Ops:
  7.2 194.4 %copy-start = (bf16[8,16,2048]{2,1,0:T(8,128)(2,1)S(1)}, bf16[8,16,2048]{2,1,0:T(8,128)(2,1)}, u32[]{:S(2)}) copy-start(bf16[8,16,2048]{2,1,0:T(8,128)(2,1)} %param.34) | copy-start | bytes 1572868
  7.2 717.2 %all-gather.8.cloned.1.call-start = ((), (), s32[]{:S(2)}) async-start(), calls=%async_computation.1 | async-start | bytes 1769472 | tf_op jit(solution)/shard_map/all_gather | solution.py:906
  8.0 130.4 %collective-permute-start = (s32[1,6]{1,0:T(1,128)S(1)}, s32[1,6]{1,0:T(1,128)S(1)}, u32[]{:S(2)}, u32[]{:S(2)}) collective-permute-start(s32[1,6]{1,0:T(1,128)S(1)} %pad_add_fusion), channel_id=1, source_target_pairs={{2,4},{3,5},{4,2},{5,3},{10,12},{11,13},{12,10},{13,11},{18,20},{1... | collective-permute-start | bytes 80 | tf_op jit(solution)/shard_map/ppermute | solution.py:813
  14.5 2.8 copy-start.2
  106.5 5.1 copy-start.22
  106.5 20.5 %copy-start.25 = (f32[2,512]{1,0:T(2,128)S(1)}, f32[2,512]{1,0:T(2,128)}, u32[]{:S(2)}) copy-start(f32[2,512]{1,0:T(2,128)} %param.27) | copy-start | bytes 12292
  106.5 20.5 %copy-start.24 = (f32[2048]{0:T(1024)S(1)}, f32[2048]{0:T(1024)}, u32[]{:S(2)}) copy-start(f32[2048]{0:T(1024)} %param.31) | copy-start | bytes 24580
  109.7 81.4 %collective-permute-start.9 = (bf16[2048,512]{1,0:T(8,128)(2,1)}, bf16[2048,512]{1,0:T(8,128)(2,1)}, u32[]{:S(2)}, u32[]{:S(2)}) collective-permute-start(bf16[2048,512]{1,0:T(8,128)(2,1)} %constant_dynamic-slice_fusion.1), channel_id=1, source_target_pairs={{2,4},{3,5},{4,2},{5,3},{10,12},{11,13},{12,10},{13,11},{18,20},{1... | collective-permute-start | bytes 6291464 | tf_op jit(solution)/shard_map/ppermute | solution.py:813
  122.5 88.8 %collective-permute-start.1 = (bf16[16,6144]{1,0:T(8,128)(2,1)S(1)}, bf16[16,6144]{1,0:T(8,128)(2,1)S(1)}, u32[]{:S(2)}, u32[]{:S(2)}) collective-permute-start(bf16[16,6144]{1,0:T(8,128)(2,1)S(1)} %pad_maximum_fusion.2), channel_id=1, source_target_pairs={{2,4},{3,5},{4,2},{5,3},{10,12},{11,13},{12,10},{13,11},{18,20},{1... | collective-permute-start | bytes 589832 | tf_op jit(solution)/shard_map/ppermute | solution.py:813
  127.1 81.0 %collective-permute-start.2 = (f32[1,3072]{1,0:T(1,128)S(1)}, f32[1,3072]{1,0:T(1,128)S(1)}, u32[]{:S(2)}, u32[]{:S(2)}) collective-permute-start(f32[1,3072]{1,0:T(1,128)S(1)} %pad_maximum_fusion.4), channel_id=1, source_target_pairs={{2,4},{3,5},{4,2},{5,3},{10,12},{11,13},{12,10},{13,11},{18,20},{1... | collective-permute-start | bytes 36872 | tf_op jit(solution)/shard_map/ppermute | solution.py:813
  130.1 82.0 %collective-permute-start.3 = (bf16[128,2048]{1,0:T(8,128)(2,1)S(1)}, bf16[128,2048]{1,0:T(8,128)(2,1)S(1)}, u32[]{:S(2)}, u32[]{:S(2)}) collective-permute-start(bf16[128,2048]{1,0:T(8,128)(2,1)S(1)} %constant_dynamic-slice_fusion.2), channel_id=1, source_target_pairs={{2,4},{3,5},{4,2},{5,3},{10,12},{11,13},{12,10},{13,11},{18,20},{1... | collective-permute-start | bytes 1572872 | tf_op jit(solution)/shard_map/ppermute | solution.py:813
  138.4 97.5 %collective-permute-start.13 = (bf16[512,2048]{1,0:T(8,128)(2,1)}, bf16[512,2048]{1,0:T(8,128)(2,1)}, u32[]{:S(2)}, u32[]{:S(2)}) collective-permute-start(bf16[512,2048]{1,0:T(8,128)(2,1)} %constant_dynamic-slice_fusion), channel_id=1, source_target_pairs={{2,4},{3,5},{4,2},{5,3},{10,12},{11,13},{12,10},{13,11},{18,20},{1... | collective-permute-start | bytes 6291464 | tf_op jit(solution)/shard_map/ppermute | solution.py:813
  191.1 47.2 %collective-permute-start.10 = (bf16[2048,512]{1,0:T(8,128)(2,1)}, bf16[2048,512]{1,0:T(8,128)(2,1)}, u32[]{:S(2)}, u32[]{:S(2)}) collective-permute-start(bf16[2048,512]{1,0:T(8,128)(2,1)} %collective-permute-done.9), channel_id=1, source_target_pairs={{2,10},{3,11},{4,12},{5,13},{10,2},{11,3},{12,4},{13,5},{18,26},{1... | collective-permute-start | bytes 6291464 | tf_op jit(solution)/shard_map/ppermute | solution.py:813
  208.1 53.2 %collective-permute-start.7 = (bf16[256,2048]{1,0:T(8,128)(2,1)}, bf16[256,2048]{1,0:T(8,128)(2,1)}, u32[]{:S(2)}, u32[]{:S(2)}) collective-permute-start(bf16[256,2048]{1,0:T(8,128)(2,1)} %param.23), channel_id=1, source_target_pairs={{2,4},{3,5},{4,2},{5,3},{10,12},{11,13},{12,10},{13,11},{18,20},{1... | collective-permute-start | bytes 3145736 | tf_op jit(solution)/shard_map/ppermute | solution.py:813
  212.1 18.5 %collective-permute-start.4 = (bf16[128,2048]{1,0:T(8,128)(2,1)S(1)}, bf16[128,2048]{1,0:T(8,128)(2,1)S(1)}, u32[]{:S(2)}, u32[]{:S(2)}) collective-permute-start(bf16[128,2048]{1,0:T(8,128)(2,1)S(1)} %collective-permute-done.3), channel_id=1, source_target_pairs={{2,10},{3,11},{4,12},{5,13},{10,2},{11,3},{12,4},{13,5},{18,26},{1... | collective-permute-start | bytes 1572872 | tf_op jit(solution)/shard_map/ppermute | solution.py:813
  215.2 18.5 %collective-permute-start.6 = (bf16[128,2048]{1,0:T(8,128)(2,1)S(1)}, bf16[128,2048]{1,0:T(8,128)(2,1)S(1)}, u32[]{:S(2)}, u32[]{:S(2)}) collective-permute-start(bf16[128,2048]{1,0:T(8,128)(2,1)S(1)} %collective-permute-done.3), channel_id=1, source_target_pairs={{2,18},{3,19},{4,20},{5,21},{10,26},{11,27},{12,28},{13,29},{18,2}... | collective-permute-start | bytes 1572872 | tf_op jit(solution)/shard_map/ppermute | solution.py:813
  230.6 30.7 %copy-start.18 = (bf16[128,2048]{1,0:T(8,128)(2,1)}, bf16[128,2048]{1,0:T(8,128)(2,1)S(1)}, u32[]{:S(2)}) copy-start(bf16[128,2048]{1,0:T(8,128)(2,1)S(1)} %collective-permute-done.4) | copy-start | bytes 1572868
  230.6 32.4 %collective-permute-start.5 = (bf16[128,2048]{1,0:T(8,128)(2,1)S(1)}, bf16[128,2048]{1,0:T(8,128)(2,1)S(1)}, u32[]{:S(2)}, u32[]{:S(2)}) collective-permute-start(bf16[128,2048]{1,0:T(8,128)(2,1)S(1)} %collective-permute-done.4), channel_id=1, source_target_pairs={{2,18},{3,19},{4,20},{5,21},{10,26},{11,27},{12,28},{13,29},{18,2}... | collective-permute-start | bytes 1572872 | tf_op jit(solution)/shard_map/ppermute | solution.py:813
  233.8 27.6 %copy-start.19 = (bf16[128,2048]{1,0:T(8,128)(2,1)}, bf16[128,2048]{1,0:T(8,128)(2,1)S(1)}, u32[]{:S(2)}) copy-start(bf16[128,2048]{1,0:T(8,128)(2,1)S(1)} %collective-permute-done.6) | copy-start | bytes 1572868
  233.8 100.2 %collective-permute-start.12 = (bf16[2048,512]{1,0:T(8,128)(2,1)}, bf16[2048,512]{1,0:T(8,128)(2,1)S(1)}, u32[]{:S(2)}, u32[]{:S(2)}) collective-permute-start(bf16[2048,512]{1,0:T(8,128)(2,1)} %collective-permute-done.9), channel_id=1, source_target_pairs={{2,18},{3,19},{4,20},{5,21},{10,26},{11,27},{12,28},{13,29},{18,2}... | collective-permute-start | bytes 6291464 | tf_op jit(solution)/shard_map/ppermute | solution.py:813
  235.9 98.2 %collective-permute-start.14 = (bf16[512,2048]{1,0:T(8,128)(2,1)}, bf16[512,2048]{1,0:T(8,128)(2,1)S(1)}, u32[]{:S(2)}, u32[]{:S(2)}) collective-permute-start(bf16[512,2048]{1,0:T(8,128)(2,1)} %collective-permute-done.13), channel_id=1, source_target_pairs={{2,10},{3,11},{4,12},{5,13},{10,2},{11,3},{12,4},{13,5},{18,26},{1... | collective-permute-start | bytes 6291464 | tf_op jit(solution)/shard_map/ppermute | solution.py:813
  238.3 99.0 %collective-permute-start.11 = (bf16[2048,512]{1,0:T(8,128)(2,1)}, bf16[2048,512]{1,0:T(8,128)(2,1)}, u32[]{:S(2)}, u32[]{:S(2)}) collective-permute-start(bf16[2048,512]{1,0:T(8,128)(2,1)} %collective-permute-done.10), channel_id=1, source_target_pairs={{2,18},{3,19},{4,20},{5,21},{10,26},{11,27},{12,28},{13,29},{18,2}... | collective-permute-start | bytes 6291464 | tf_op jit(solution)/shard_map/ppermute | solution.py:813
  261.3 4.1 copy-start.14
  261.4 69.8 %collective-permute-start.18 = (bf16[256,2048]{1,0:T(8,128)(2,1)}, bf16[256,2048]{1,0:T(8,128)(2,1)}, u32[]{:S(2)}, u32[]{:S(2)}) collective-permute-start(bf16[256,2048]{1,0:T(8,128)(2,1)} %collective-permute-done.7.c0.cot), channel_id=1, source_target_pairs={{0,1},{1,0},{2,3},{3,2},{4,5},{5,4},{6,7},{7,6},{8,9},{9,8},{10,11... | collective-permute-start | bytes 3145736 | tf_op jit(solution)/shard_map/ppermute | solution.py:813
  263.8 159.2 %collective-permute-start.8 = (bf16[256,2048]{1,0:T(8,128)(2,1)}, bf16[256,2048]{1,0:T(8,128)(2,1)}, u32[]{:S(2)}, u32[]{:S(2)}) collective-permute-start(bf16[256,2048]{1,0:T(8,128)(2,1)} %collective-permute-done.7.c0.cot), channel_id=1, source_target_pairs={{0,4},{1,5},{2,6},{3,7},{4,0},{5,1},{6,2},{7,3},{8,12},{9,13},{10,... | collective-permute-start | bytes 3145736 | tf_op jit(solution)/shard_map/ppermute | solution.py:813
  267.7 7.9 %copy-start.11 = (f32[2048]{0:T(1024)S(1)}, f32[2048]{0:T(1024)}, u32[]{:S(2)}) copy-start(f32[2048]{0:T(1024)} %param.29) | copy-start | bytes 24580
  329.0 11.8 %slice-start = ((s8[8388608]{0:T(1024)(128)(4,1)}), s8[4194304]{0:T(1024)(128)(4,1)S(1)}, s32[]{:S(2)}) async-start(s8[8388608]{0:T(1024)(128)(4,1)} %bitcast.86), calls=%async_computation.2 | async-start | bytes 8388608
  331.2 9.6 %slice-start.1 = ((s8[8388608]{0:T(1024)(128)(4,1)}), s8[4194304]{0:T(1024)(128)(4,1)S(1)}, s32[]{:S(2)}) async-start(s8[8388608]{0:T(1024)(128)(4,1)} %bitcast.86), calls=%async_computation.3 | async-start | bytes 8388608
  331.2 27.3 %collective-permute-start.16 = (bf16[512,2048]{1,0:T(8,128)(2,1)}, bf16[512,2048]{1,0:T(8,128)(2,1)}, u32[]{:S(2)}, u32[]{:S(2)}) collective-permute-start(bf16[512,2048]{1,0:T(8,128)(2,1)} %collective-permute-done.13), channel_id=1, source_target_pairs={{2,18},{3,19},{4,20},{5,21},{10,26},{11,27},{12,28},{13,29},{18,2}... | collective-permute-start | bytes 6291464 | tf_op jit(solution)/shard_map/ppermute | solution.py:813
  334.0 57.0 %collective-permute-start.19 = (bf16[256,2048]{1,0:T(8,128)(2,1)}, bf16[256,2048]{1,0:T(8,128)(2,1)}, u32[]{:S(2)}, u32[]{:S(2)}) collective-permute-start(bf16[256,2048]{1,0:T(8,128)(2,1)} %collective-permute-done.18.c0), channel_id=1, source_target_pairs={{0,4},{1,5},{2,6},{3,7},{4,0},{5,1},{6,2},{7,3},{8,12},{9,13},{10,... | collective-permute-start | bytes 3145736 | tf_op jit(solution)/shard_map/ppermute | solution.py:813
  334.1 46.9 %collective-permute-start.15 = (bf16[512,2048]{1,0:T(8,128)(2,1)S(1)}, bf16[512,2048]{1,0:T(8,128)(2,1)}, u32[]{:S(2)}, u32[]{:S(2)}) collective-permute-start(bf16[512,2048]{1,0:T(8,128)(2,1)S(1)} %collective-permute-done.14), channel_id=1, source_target_pairs={{2,18},{3,19},{4,20},{5,21},{10,26},{11,27},{12,28},{13,29},{18,2}... | collective-permute-start | bytes 6291464 | tf_op jit(solution)/shard_map/ppermute | solution.py:813
  337.3 47.1 %slice-start.2 = ((s8[8388608]{0:T(1024)(128)(4,1)}), s8[4194304]{0:T(1024)(128)(4,1)S(1)}, s32[]{:S(2)}) async-start(s8[8388608]{0:T(1024)(128)(4,1)} %bitcast.88), calls=%async_computation.4 | async-start | bytes 8388608
  340.8 43.6 %slice-start.3 = ((s8[8388608]{0:T(1024)(128)(4,1)}), s8[4194304]{0:T(1024)(128)(4,1)S(1)}, s32[]{:S(2)}) async-start(s8[8388608]{0:T(1024)(128)(4,1)} %bitcast.88), calls=%async_computation.5 | async-start | bytes 8388608
  567.9 12.5 %collective-permute-start.26 = (bf16[16,6144]{1,0:T(8,128)(2,1)S(1)}, bf16[16,6144]{1,0:T(8,128)(2,1)S(1)}, u32[]{:S(2)}, u32[]{:S(2)}) collective-permute-start(bf16[16,6144]{1,0:T(8,128)(2,1)S(1)} %pad_maximum_fusion.3), channel_id=1, source_target_pairs={{2,4},{3,5},{4,2},{5,3},{10,12},{11,13},{12,10},{13,11},{18,20},{1... | collective-permute-start | bytes 589832 | tf_op jit(solution)/shard_map/ppermute | solution.py:813
  581.1 167.2 %all-gather.6.cloned.1.call-start = ((), (), s32[]{:S(2)}) async-start(), calls=%async_computation | async-start | bytes 2621440 | tf_op jit(solution)/shard_map/all_gather | solution.py:930
  582.1 2.9 collective-permute-start.23
  584.4 34.5 %collective-permute-start.20 = (bf16[256,2048]{1,0:T(8,128)(2,1)}, bf16[256,2048]{1,0:T(8,128)(2,1)}, u32[]{:S(2)}, u32[]{:S(2)}) collective-permute-start(bf16[256,2048]{1,0:T(8,128)(2,1)} %slice.164), channel_id=1, source_target_pairs={{0,4},{1,5},{2,6},{3,7},{4,0},{5,1},{6,2},{7,3},{8,12},{9,13},{10,... | collective-permute-start | bytes 3145736 | tf_op jit(solution)/shard_map/ppermute | solution.py:813
  585.9 8.1 %collective-permute-start.24 = (bf16[4,16,2048]{2,1,0:T(8,128)(2,1)}, bf16[4,16,2048]{2,1,0:T(8,128)(2,1)S(1)}, u32[]{:S(2)}, u32[]{:S(2)}) collective-permute-start(bf16[4,16,2048]{2,1,0:T(8,128)(2,1)} %get-tuple-element.142), channel_id=1, source_target_pairs={{0,1},{1,0},{2,3},{3,2},{4,5},{5,4},{6,7},{7,6},{8,9},{9,8},{10,11... | collective-permute-start | bytes 786440 | tf_op jit(solution)/shard_map/ppermute | solution.py:813
  595.0 13.9 %collective-permute-start.25 = (bf16[4,16,512]{2,1,0:T(8,128)(2,1)S(1)}, bf16[4,16,512]{2,1,0:T(8,128)(2,1)S(1)}, u32[]{:S(2)}, u32[]{:S(2)}) collective-permute-start(bf16[4,16,512]{2,1,0:T(8,128)(2,1)S(1)} %fusion.9), channel_id=1, source_target_pairs={{2,4},{3,5},{4,2},{5,3},{10,12},{11,13},{12,10},{13,11},{18,20},{1... | collective-permute-start | bytes 196616 | tf_op jit(solution)/shard_map/ppermute | solution.py:813
  606.3 12.7 %copy-start.15 = (bf16[512,2048]{1,0:T(8,128)(2,1)S(1)}, bf16[512,2048]{1,0:T(8,128)(2,1)}, u32[]{:S(2)}) copy-start(bf16[512,2048]{1,0:T(8,128)(2,1)} %get-tuple-element.58) | copy-start | bytes 6291460
  608.7 106.8 %collective-permute-start.17 = (bf16[256,2048]{1,0:T(8,128)(2,1)}, bf16[256,2048]{1,0:T(8,128)(2,1)}, u32[]{:S(2)}, u32[]{:S(2)}) collective-permute-start(bf16[256,2048]{1,0:T(8,128)(2,1)} %slice.160), channel_id=1, source_target_pairs={{0,4},{1,5},{2,6},{3,7},{4,0},{5,1},{6,2},{7,3},{8,12},{9,13},{10,... | collective-permute-start | bytes 3145736 | tf_op jit(solution)/shard_map/ppermute | solution.py:813
  621.5 94.0 %collective-permute-start.21 = (bf16[256,2048]{1,0:T(8,128)(2,1)}, bf16[256,2048]{1,0:T(8,128)(2,1)}, u32[]{:S(2)}, u32[]{:S(2)}) collective-permute-start(bf16[256,2048]{1,0:T(8,128)(2,1)} %add_convert_fusion.1), channel_id=1, source_target_pairs={{0,1},{1,0},{2,3},{3,2},{4,5},{5,4},{6,7},{7,6},{8,9},{9,8},{10,11... | collective-permute-start | bytes 3145736 | tf_op jit(solution)/shard_map/ppermute | solution.py:813
  628.2 87.3 %copy-start.16 = (bf16[512,2048]{1,0:T(8,128)(2,1)S(1)}, bf16[512,2048]{1,0:T(8,128)(2,1)}, u32[]{:S(2)}) copy-start(bf16[512,2048]{1,0:T(8,128)(2,1)} %get-tuple-element.57) | copy-start | bytes 6291460
  628.2 87.3 %copy-start.23 = (f32[2048]{0:T(1024)S(1)}, f32[2048]{0:T(1024)}, u32[]{:S(2)}) copy-start(f32[2048]{0:T(1024)} %param.33) | copy-start | bytes 24580
  715.5 3.5 copy-start.5
  719.0 29.2 %collective-permute-start.22 = (bf16[256,2048]{1,0:T(8,128)(2,1)}, bf16[256,2048]{1,0:T(8,128)(2,1)S(1)}, u32[]{:S(2)}, u32[]{:S(2)}) collective-permute-start(bf16[256,2048]{1,0:T(8,128)(2,1)} %add_convert_fusion), channel_id=1, source_target_pairs={{2,4},{3,5},{4,2},{5,3},{10,12},{11,13},{12,10},{13,11},{18,20},{1... | collective-permute-start | bytes 3145736 | tf_op jit(solution)/shard_map/ppermute | solution.py:813
  727.0 4.0 copy-start.17
  755.6 3.5 copy-start.1
  (11 other events, 19.3 us)
Sparse Core Ops, SparseCore 0:
  581.2 25.2 all-gather.7
  624.4 73.6 all-gather.5

commit v2 on v1

v2 whole, which is shorter than its diff:
```python
import functools
import math

import jax
import jax.numpy as jnp
from jax import lax
from jax.experimental import pallas as pl
from jax.experimental.pallas import tpu as pltpu
from jax.sharding import PartitionSpec as P

HEADS = 16
HEAD_DIM = 128
PIECE = 256
ITEM = 128
AHEAD = 3
EPS = 1e-05
GELU_C = 0.7978845608028654
GELU_K = 0.044715
LOG2E = 1.4426950408889634
FAR = 1e32
F32 = jnp.float32
BF16 = jnp.bfloat16
AXES = ("dp", "tensor")
VM = pltpu.VMEM
HERE = pl.BlockSpec(memory_space=pl.ANY)


def dot(a, b):
    return lax.dot_general(a, b, (((1,), (0,)), ((), ())), preferred_element_type=F32)


def dot_t(a, b):
    return lax.dot_general(a, b, (((1,), (1,)), ((), ())), preferred_element_type=F32)


def t_dot(a, b):
    return lax.dot_general(a, b, (((0,), (0,)), ((), ())), preferred_element_type=F32)


def whole(shape):
    zeros = (0,) * len(shape)
    return pl.BlockSpec(shape, lambda *_: zeros)


def params(mib=56):
    return pltpu.CompilerParams(vmem_limit_bytes=mib << 20)


def cost(flops, read):
    return pl.CostEstimate(flops=int(flops), bytes_accessed=int(read), transcendentals=0)


def displaced():
    return (lax.axis_index("dp") % 2 + lax.axis_index("tensor") // 2) % 2 == 1


def fetch(native, brought, into, sem):
    moved = displaced()

    @pl.when(moved)
    def _():
        pltpu.make_async_copy(brought, into, sem).start()

    @pl.when(jnp.logical_not(moved))
    def _():
        pltpu.make_async_copy(native, into, sem).start()

    return pltpu.make_async_copy(native, into, sem)


def bwd_o_kernel(g, native, brought, b, a, rank, x, out, tb, ta, w, sem):
    first = pl.program_id(0) == 0

    @pl.when(first)
    def _():
        fetch(native, brought, w, sem).wait()

    r = dot_t(g[...], b[...]).astype(BF16)
    out[...] = (dot_t(g[...], w[...]) + dot(r, a[...])).astype(BF16)
    one = t_dot(rank[...], g[...])
    two = t_dot(r, x[...])

    @pl.when(first)
    def _():
        tb[...] = one
        ta[...] = two

    @pl.when(jnp.logical_not(first))
    def _():
        tb[...] += one
        ta[...] += two


def bwd_o(g, w, brought, chosen, small, rank, x, tile):
    n, k = g.shape
    cols = w.shape[0]
    low = rank.shape[1]
    row = lambda c: pl.BlockSpec((tile, c), lambda i: (i, 0))
    return pl.pallas_call(
        bwd_o_kernel,
        grid=(n // tile,),
        in_specs=[row(k), HERE, HERE, pl.BlockSpec((low, k), lambda i: (1, 0)), pl.BlockSpec((low, cols), lambda i: (0, 3)), row(low), row(cols)],
        out_specs=[row(cols), whole((low, k)), whole((low, cols))],
        out_shape=[
            jax.ShapeDtypeStruct((n, cols), BF16),
            jax.ShapeDtypeStruct((low, k), F32),
            jax.ShapeDtypeStruct((low, cols), F32),
        ],
        scratch_shapes=[VM(w.shape, BF16), pltpu.SemaphoreType.DMA],
        compiler_params=params(),
        cost_estimate=cost(2 * n * k * cols, 2 * (n * k + k * cols + n * cols)),
        name="bwd_o",
    )(g, w, brought, chosen, small, rank, x)


def bwd_qkv_kernel(g, native, brought, b, a, rank, x, out, tb, ta, w, sem):
    first = pl.program_id(0) == 0

    @pl.when(first)
    def _():
        fetch(native, brought, w, sem).wait()

    cols = w.shape[2]
    r = dot_t(g[...], b[...]).astype(BF16)
    acc = dot(r, a[...])
    for j in range(3):
        acc = acc + dot_t(g[:, j * cols : (j + 1) * cols], w[j])
    out[...] = acc.astype(BF16)
    one = t_dot(rank[...], g[...])
    two = t_dot(r, x[...])

    @pl.when(first)
    def _():
        tb[...] = one
        ta[...] = two

    @pl.when(jnp.logical_not(first))
    def _():
        tb[...] += one
        ta[...] += two


def bwd_qkv(g, w3, brought, small, chosen, rank, x, tile):
    n, k = g.shape
    cols = w3.shape[1]
    low = rank.shape[1]
    row = lambda c: pl.BlockSpec((tile, c), lambda i: (i, 0))
    return pl.pallas_call(
        bwd_qkv_kernel,
        grid=(n // tile,),
        in_specs=[row(k), HERE, HERE, pl.BlockSpec((low, k), lambda i: (0, 0)), pl.BlockSpec((low, cols), lambda i: (0, 0)), row(low), row(cols)],
        out_specs=[row(cols), whole((low, k)), whole((low, cols))],
        out_shape=[
            jax.ShapeDtypeStruct((n, cols), BF16),
            jax.ShapeDtypeStruct((low, k), F32),
            jax.ShapeDtypeStruct((low, cols), F32),
        ],
        scratch_shapes=[VM(w3.shape, BF16), pltpu.SemaphoreType.DMA],
        compiler_params=params(),
        cost_estimate=cost(2 * n * k * cols, 2 * (n * k + k * cols + n * cols)),
        name="bwd_qkv",
    )(g, w3, brought, small, chosen, rank, x)


def distances(me, s0, s1, rows, step, dist):
    length = dist.shape[0]

    def piece(pos, none):
        one = jnp.where((pos >= s0) & (pos < s0 + PIECE), 1.0, none)
        return jnp.where((pos >= s1) & (pos < s1 + PIECE), 2.0, one)

    def rel(j):
        return ((j & 1) << 1) | (j >> 1)

    i = lax.broadcasted_iota(jnp.int32, (length, 128), 0)
    kpos = ((me ^ rel(i // rows)) * rows + i % rows).astype(F32)[:, :1]
    qpos = ((me ^ rel(step)) * rows + lax.broadcasted_iota(jnp.int32, (1, rows), 1)).astype(F32)
    seen = (kpos <= qpos) | (piece(kpos, -1.0) == piece(qpos, -2.0))
    dist[...] = jnp.where(seen, jnp.abs(kpos - qpos), FAR)


def head_slopes(me, heads):
    first = jnp.full((1, 1), me * heads, jnp.int32).astype(F32)
    return [jnp.exp2((first + float(h + 1)) * (-8.0 / HEADS)) * LOG2E for h in range(heads)]


def attend_back_kernel(nums, q, k, v, g, lse, out, dist, kt, gk, gv):
    step = pl.program_id(0)
    rows = q.shape[0]
    local = q.shape[1]
    heads = local // HEAD_DIM
    scale = 1.0 / math.sqrt(HEAD_DIM)
    me = 2 * (lax.axis_index("dp") % 2) + lax.axis_index("tensor") % 2
    base = nums.shape[1] - 128
    distances(me, nums[0:1, base : base + 1], nums[0:1, base + 1 : base + 2], rows, step, dist)
    slopes = head_slopes(me, heads)

    @pl.when(step == 0)
    def _():
        kt[...] = k[...].T
        gk[...] = jnp.zeros_like(gk)
        gv[...] = jnp.zeros_like(gv)

    at = pl.ds(pl.multiple_of(step * rows, rows), rows)
    for h in range(heads):
        span = slice(h * HEAD_DIM, (h + 1) * HEAD_DIM)
        s = dot_t(k[:, span], q[:, span]) * (scale * LOG2E) - dist[...] * slopes[h]
        p = jnp.exp2(s - lse[h : h + 1, :])
        gv[:, span] += dot(p.astype(BF16), g[:, span])
        gp = dot_t(v[:, span], g[:, span])
        inner = jnp.sum(p * gp, axis=0, keepdims=True)
        gs = (p * (gp - inner)).astype(BF16)
        gk[:, span] += dot(gs, q[:, span])
        out[at, span] = (dot(kt[span, :], gs).T * scale).astype(BF16)

    @pl.when(step == pl.num_programs(0) - 1)
    def _():
        out[:, local : 2 * local] = (gk[...] * scale).astype(BF16)
        out[:, 2 * local :] = gv[...].astype(BF16)


def attend_back(nums, proj, g, lse, rows):
    length, three = proj.shape
    local = three // 3
    heads = local // HEAD_DIM
    return pl.pallas_call(
        attend_back_kernel,
        grid=(length // rows,),
        in_specs=[
            whole(nums.shape),
            pl.BlockSpec((rows, local), lambda i: (i, 0)),
            pl.BlockSpec((length, local), lambda i: (0, 1)),
            pl.BlockSpec((length, local), lambda i: (0, 2)),
            pl.BlockSpec((rows, local), lambda i: (i, 0)),
            pl.BlockSpec((heads, rows), lambda i: (0, i)),
        ],
        out_specs=pl.BlockSpec((length, three), lambda i: (0, 0)),
        scratch_shapes=[
            VM((length, rows), F32), VM((local, length), BF16), VM((length, local), F32), VM((length, local), F32),
        ],
        out_shape=jax.ShapeDtypeStruct((length, three), BF16),
        compiler_params=params(),
        cost_estimate=cost(10 * length * length * local, 16 * length * local),
        name="attend_back",
    )(nums, proj, proj, proj, g, lse)


def gelu_parts(values):
    square = values * values
    tangent = jnp.tanh(GELU_C * (values + GELU_K * square * values))
    half = 0.5 * (1.0 + tangent)
    slope = half + (0.5 * GELU_C) * values * (1.0 - tangent * tangent) * (1.0 + 3.0 * GELU_K * square)
    return values * half, slope


def mlp_kernel(
    nm, cot, wu_native, wu_brought, wd_native, wd_brought, au, bu, ad, bd, bias, part, back, tuo, tdi, tui, tdo,
    up_rank, down_rank, g_up, g_down, acc, gacc, wu_slots, wd_slots, sem,
):
    step, half = pl.program_id(0), pl.program_id(1)
    last = pl.num_programs(0) - 1
    rows = nm.shape[0]
    tile = bu.shape[1]

    def load(j):
        slot = j % 2
        cut = pl.ds(pl.multiple_of(j * tile, tile), tile)
        return (
            fetch(wu_native.at[:, cut], wu_brought.at[:, cut], wu_slots.at[slot], sem.at[0, slot]),
            fetch(wd_native.at[cut], wd_brought.at[cut], wd_slots.at[slot], sem.at[1, slot]),
        )

    def await_slot(slot):
        pltpu.make_async_copy(wu_native.at[:, pl.ds(0, tile)], wu_slots.at[slot], sem.at[0, slot]).wait()
        pltpu.make_async_copy(wd_native.at[pl.ds(0, tile)], wd_slots.at[slot], sem.at[1, slot]).wait()

    @pl.when((step == 0) & (half == 0))
    def _():
        load(step)

    @pl.when(half == 0)
    def _():
        await_slot(step % 2)

        @pl.when(step < last)
        def _():
            load(step + 1)

    wu = wu_slots.at[step % 2]
    wd = wd_slots.at[step % 2]
    here = pl.ds(pl.multiple_of(half * rows, rows), rows)

    @pl.when(step == 0)
    def _():
        up_rank[here] = dot_t(nm[...], au[...]).astype(BF16)
        g_down[here] = dot_t(cot[...], bd[...]).astype(BF16)
        down_rank[here] = jnp.zeros((rows, au.shape[0]), F32)
        g_up[here] = jnp.zeros((rows, au.shape[0]), F32)
        acc[here] = jnp.zeros((rows, nm.shape[1]), F32)
        gacc[here] = jnp.zeros((rows, nm.shape[1]), F32)

    gate = dot(nm[...], wu[...]) + dot(up_rank[here], bu[...]) + bias[...]
    value, slope = gelu_parts(gate)
    hidden = value.astype(BF16)
    grad = dot_t(cot[...], wd[...]) + dot(g_down[here], ad[...])
    grad_gate = (grad * slope).astype(BF16)
    down_rank[here] += dot_t(hidden, ad[...])
    g_up[here] += dot_t(grad_gate, bu[...])
    acc[here] += dot(hidden, wd[...])
    gacc[here] += dot_t(grad_gate, wu[...])
    one = t_dot(up_rank[here], grad_gate)
    two = t_dot(g_down[here], hidden)

    @pl.when(half == 0)
    def _():
        tuo[...] = one
        tdi[...] = two

    @pl.when(half > 0)
    def _():
        tuo[...] += one
        tdi[...] += two

    @pl.when(step == last)
    def _():
        dr = down_rank[here].astype(BF16)
        gu = g_up[here].astype(BF16)
        part[...] = (acc[here] + dot(dr, bd[...])).astype(BF16)
        back[...] = (gacc[here] + dot(gu, au[...])).astype(BF16)
        three = t_dot(gu, nm[...])
        four = t_dot(dr, cot[...])

        @pl.when(half == 0)
        def _():
            tui[...] = three
            tdo[...] = four

        @pl.when(half > 0)
        def _():
            tui[...] += three
            tdo[...] += four


def mlp(nm, cot, wu, wu_brought, wd, wd_brought, chosen, small, nums, tile):
    n, width = nm.shape
    rows = n // 2
    hidden = wu.shape[1]
    last = hidden // tile - 1
    low = small.shape[0]
    first = (small.shape[1] - 2 * hidden) // tile
    bias_first = (nums.shape[1] - 128 - hidden) // tile
    cut = lambda r: pl.BlockSpec((r, tile), lambda j, i: (0, j))
    row = pl.BlockSpec((rows, width), lambda j, i: (i, 0))
    result = pl.BlockSpec((rows, width), lambda j, i: (jnp.where(j == last, i, 0), 0))
    return pl.pallas_call(
        mlp_kernel,
        grid=(hidden // tile, 2),
        in_specs=[
            row, row, HERE, HERE, HERE, HERE,
            pl.BlockSpec((low, width), lambda j, i: (2, 0)),
            pl.BlockSpec((low, tile), lambda j, i: (0, first + j)),
            pl.BlockSpec((low, tile), lambda j, i: (0, first + hidden // tile + j)),
            pl.BlockSpec((low, width), lambda j, i: (3, 0)),
            pl.BlockSpec((1, tile), lambda j, i: (0, bias_first + j)),
        ],
        out_specs=[result, result, cut(low), cut(low), whole((low, width)), whole((low, width))],
        out_shape=[
            jax.ShapeDtypeStruct((n, width), BF16),
            jax.ShapeDtypeStruct((n, width), BF16),
            jax.ShapeDtypeStruct((low, hidden), F32),
            jax.ShapeDtypeStruct((low, hidden), F32),
            jax.ShapeDtypeStruct((low, width), F32),
            jax.ShapeDtypeStruct((low, width), F32),
        ],
        scratch_shapes=[
            VM((n, low), BF16), VM((n, low), F32), VM((n, low), F32), VM((n, low), BF16),
            VM((n, width), F32), VM((n, width), F32),
            VM((2, width, tile), BF16), VM((2, tile, width), BF16), pltpu.SemaphoreType.DMA((2, 2)),
        ],
        compiler_params=params(60),
        cost_estimate=cost(8 * n * width * hidden, 4 * width * hidden + 12 * n * width),
        name="mlp",
    )(nm, cot, wu, wu_brought, wd, wd_brought, chosen, small, small, chosen, nums)


MESH = pl.DeviceIdType.MESH
CHUNKS = 4


def places():
    d, t = lax.axis_index("dp"), lax.axis_index("tensor")
    core, zh = d % 2, t // 2
    core_d = d + 1 - 2 * core
    near_t = t + 1 - 2 * (t % 2)
    left = d + 2 - 4 * ((d // 2) % 2)
    up = 4 - 8 * ((d // 4) % 2)
    return dict(
        moved=(core + zh) % 2 == 1,
        line=(d // 2) % 4,
        core=(core_d, t),
        near=(d, near_t),
        cross=(core_d, t + 2 - 4 * zh),
        left=(left, t),
        up=(d + up, t),
        both=(left + up, t),
    )


def greet(always, sometimes=(), when=None):
    barrier = pltpu.get_barrier_semaphore()
    for peer in always:
        pl.semaphore_signal(barrier, inc=1, device_id=peer, device_id_type=MESH)
    count = len(always)
    if sometimes:

        @pl.when(when)
        def _():
            for peer in sometimes:
                pl.semaphore_signal(barrier, inc=1, device_id=peer, device_id_type=MESH)

        count = count + len(sometimes) * when.astype(jnp.int32)
    pl.semaphore_wait(barrier, count)


def remote(src, dst, send, recv, peer):
    return pltpu.make_async_remote_copy(
        src_ref=src, dst_ref=dst, send_sem=send, recv_sem=recv, device_id=peer, device_id_type=MESH
    )


def unit_rows(v):
    centre = v - jnp.mean(v, axis=-1, keepdims=True)
    inverse = lax.rsqrt(jnp.mean(centre * centre, axis=-1, keepdims=True) + EPS)
    return centre * inverse, inverse


def unit_back(grad, scaled, inverse, gain):
    inner = grad * gain
    first = jnp.mean(inner, axis=-1, keepdims=True)
    second = jnp.mean(inner * scaled, axis=-1, keepdims=True)
    return inverse * (inner - first - scaled * second)


class Spread:
    def __init__(self, at, full, send, recv):
        self.at, self.full, self.send, self.recv = at, full, send, recv
        self.rows = full.shape[0] // 4
        self.step = self.rows // CHUNKS

    def block(self, k, i):
        return self.full.at[pl.ds(k * self.rows + i * self.step, self.step)]

    def side(self, i):
        return remote(self.block(0, i), self.block(1, i), self.send.at[0, i], self.recv.at[0, i], self.at["core"])

    def far(self, i):
        return remote(self.block(0, i), self.block(2, i), self.send.at[1, i], self.recv.at[1, i], self.at["near"])

    def onward(self, i):
        return remote(self.block(2, i), self.block(3, i), self.send.at[2, i], self.recv.at[2, i], self.at["core"])

    def post(self, i):
        self.far(i).start()
        self.side(i).start()

    def forward(self, i):
        self.far(i).wait_recv()
        self.onward(i).start()

    def finish(self):
        for i in range(CHUNKS):
            self.side(i).wait()
            self.far(i).wait_send()
            self.onward(i).wait()


class Gathered:
    def __init__(self, at, part, side, far, mix, send, recv):
        self.at, self.part, self.side, self.far, self.mix = at, part, side, far, mix
        self.send, self.recv = send, recv
        self.rows = part.shape[0] // 4
        self.step = self.rows // CHUNKS

    def away(self, i):
        src = self.part.at[pl.ds(3 * self.rows + i * self.step, self.step)]
        dst = self.side.at[pl.ds(self.rows + i * self.step, self.step)]
        return remote(src, dst, self.send.at[0, i], self.recv.at[0, i], self.at["core"])

    def home(self, i):
        src = self.part.at[pl.ds(self.rows + i * self.step, self.step)]
        dst = self.side.at[pl.ds(i * self.step, self.step)]
        return remote(src, dst, self.send.at[1, i], self.recv.at[1, i], self.at["core"])

    def over(self, i):
        here = pl.ds(i * self.step, self.step)
        return remote(self.mix.at[here], self.far.at[here], self.send.at[2, i], self.recv.at[2, i], self.at["near"])

    def send_away(self):
        for i in range(CHUNKS):
            self.away(i).start()

    def send_home(self):
        for i in range(CHUNKS):
            self.home(i).start()

    def send_over(self):
        for i in range(CHUNKS):
            self.away(i).wait_recv()
            here = pl.ds(i * self.step, self.step)
            ours = self.part[pl.ds(2 * self.rows + i * self.step, self.step)].astype(F32)
            theirs = self.side[pl.ds(self.rows + i * self.step, self.step)].astype(F32)
            self.mix[here] = (ours + theirs).astype(BF16)
            self.over(i).start()

    def begin(self):
        self.send_away()
        self.send_home()
        self.send_over()

    def take(self, i):
        self.home(i).wait_recv()
        self.over(i).wait_recv()
        here = pl.ds(i * self.step, self.step)
        return self.part[here].astype(F32) + self.side[here].astype(F32) + self.far[here].astype(F32)

    def finish(self):
        for i in range(CHUNKS):
            self.away(i).wait_send()
            self.home(i).wait_send()
            self.over(i).wait_send()


def sems(*shape):
    return [pltpu.SemaphoreType.DMA(shape), pltpu.SemaphoreType.DMA(shape)]


def comm_params(number, mib=56):
    return pltpu.CompilerParams(collective_id=number, has_side_effects=True, vmem_limit_bytes=mib << 20)


VMEM_SPEC = pl.BlockSpec(memory_space=pltpu.VMEM)
ANY_SPEC = pl.BlockSpec(memory_space=pl.ANY)


def turn_kernel(part, cot, mid, gain, full, grad, side, far, mix, rs, rr, gs, gr):
    at = places()
    greet((at["core"], at["near"]))
    step = cot.shape[0] // CHUNKS
    total = Gathered(at, part, side, far, mix, rs, rr)
    spread = Spread(at, full, gs, gr)
    total.begin()
    for i in range(CHUNKS):
        here = slice(i * step, (i + 1) * step)
        unit, inverse = unit_rows(mid[here])
        value = cot[here].astype(F32) + unit_back(total.take(i), unit, inverse, gain[...])
        grad[here] = value
        full[here] = value.astype(BF16)
        spread.post(i)
    for i in range(CHUNKS):
        spread.forward(i)
    total.finish()
    spread.finish()


def turn_rows(part, cot, mid, gain):
    rows, width = cot.shape
    return pl.pallas_call(
        turn_kernel,
        in_specs=[VMEM_SPEC] * 4,
        out_specs=[VMEM_SPEC] * 2,
        out_shape=[jax.ShapeDtypeStruct((4 * rows, width), BF16), jax.ShapeDtypeStruct((rows, width), F32)],
        scratch_shapes=[VM((2 * rows, width), BF16), VM((rows, width), BF16), VM((rows, width), BF16)]
        + sems(3, CHUNKS) + sems(3, CHUNKS),
        compiler_params=comm_params(3, 40),
        name="turn_rows",
    )(part, cot, mid, gain)


def leave_kernel(part, tok, grad, gain, out, side, far, mix, done, rs, rr, os, orr):
    at = places()
    moved = at["moved"]
    greet((at["core"], at["near"]), (at["cross"],), moved)
    step = tok.shape[0] // CHUNKS
    total = Gathered(at, part, side, far, mix, rs, rr)

    def back(i):
        here = pl.ds(i * step, step)
        return remote(done.at[here], out.at[here], os.at[i], orr.at[i], at["cross"])

    total.begin()
    for i in range(CHUNKS):
        here = slice(i * step, (i + 1) * step)
        unit, inverse = unit_rows(tok[here].astype(F32))
        value = (grad[here] + unit_back(total.take(i), unit, inverse, gain[...])).astype(BF16)

        @pl.when(moved)
        def _():
            done[here] = value
            back(i).start()

        @pl.when(jnp.logical_not(moved))
        def _():
            out[here] = value

    total.finish()

    @pl.when(moved)
    def _():
        for i in range(CHUNKS):
            back(i).wait()


def leave(part, tok, grad, gain):
    rows, width = tok.shape
    return pl.pallas_call(
        leave_kernel,
        in_specs=[VMEM_SPEC] * 4,
        out_specs=VMEM_SPEC,
        out_shape=jax.ShapeDtypeStruct((rows, width), BF16),
        scratch_shapes=[
            VM((2 * rows, width), BF16), VM((rows, width), BF16), VM((rows, width), BF16), VM((rows, width), BF16)
        ] + sems(3, CHUNKS) + sems(CHUNKS),
        compiler_params=comm_params(4, 40),
        name="leave",
    )(part, tok, grad, gain)


class Supply:
    def __init__(self, at, plan, cross_send, cross_recv, share_send, share_recv):
        self.at, self.plan = at, plan
        self.xs, self.xr, self.ss, self.sr = cross_send, cross_recv, share_send, share_recv
        self.moved = at["moved"]
        self.peers = (at["left"], at["up"], at["both"])
        self.items = []
        for k, (native, role, shared, span) in enumerate(plan):
            size = native.shape[0] // 4 if shared else native.shape[0]
            for i in range(size // span):
                self.items.append((k, size, i))

    def rows(self, n):
        k, size, i = self.items[n]
        span = self.plan[k][3]
        if self.plan[k][2]:
            return pl.ds(pl.multiple_of(self.at["line"] * size + i * span, span), span)
        return pl.ds(i * span, span)

    def cross(self, n):
        native, role = self.plan[self.items[n][0]][:2]
        return remote(native.at[self.rows(n)], role.at[self.rows(n)], self.xs.at[n], self.xr.at[n], self.at["cross"])

    def share(self, n, k):
        role = self.plan[self.items[n][0]][1]
        block = role.at[self.rows(n)]
        return remote(block, block, self.ss.at[n, k], self.sr.at[n, k], self.peers[k])

    def begin(self, ahead):
        for n in range(ahead):
            self.cross(n).start()
        self.ahead = ahead

    def tick(self, n):
        @pl.when(self.moved)
        def _():
            self.cross(n).wait_recv()
            if n + self.ahead < len(self.items):
                self.cross(n + self.ahead).start()
            if self.plan[self.items[n][0]][2]:
                for k in range(3):
                    self.share(n, k).start()

    def ready(self, k):
        @pl.when(self.moved)
        def _():
            for n, item in enumerate(self.items):
                if item[0] == k:
                    for j in range(3):
                        self.share(n, j).wait_recv()

    def finish(self):
        @pl.when(self.moved)
        def _():
            for n, item in enumerate(self.items):
                self.cross(n).wait_send()
                if self.plan[item[0]][2]:
                    for j in range(3):
                        self.share(n, j).wait_send()


class Relay:
    def __init__(self, at, full, send, recv):
        self.at, self.full, self.send, self.recv = at, full, send, recv
        self.rows = full.shape[0] // 4

    def block(self, k, i):
        return self.full.at[pl.ds(k * self.rows + i * ITEM, ITEM)]

    def side(self, i):
        return remote(self.block(0, i), self.block(1, i), self.send.at[0, i], self.recv.at[0, i], self.at["core"])

    def far(self, i):
        return remote(self.block(0, i), self.block(2, i), self.send.at[1, i], self.recv.at[1, i], self.at["near"])

    def last(self, i):
        return remote(self.block(2, i), self.block(3, i), self.send.at[2, i], self.recv.at[2, i], self.at["core"])

    def post(self, i):
        self.far(i).start()
        self.side(i).start()

    def forward(self, i):
        self.far(i).wait_recv()
        self.last(i).start()

    def finish(self, count):
        for i in range(count):
            self.side(i).wait()
            self.far(i).wait_send()
            self.last(i).wait()


def pick_row(table, key):
    total = jnp.zeros(table.shape[1:], F32)
    for e in range(table.shape[0]):
        total = total + jnp.where(key == float(e), table[e].astype(F32), 0.0)
    return total.astype(BF16)


def front_kernel(
    ids, tokens, numbers, t_bq, t_ao, t_bu, t_ad, t_aq, t_bo, t_au, t_bd, norm_gains, norm_shifts, obias,
    w3, wo, wu, wd, cot,
    x, tok, small, nums, chosen, proj, lse, ctx, rank_qkv, rank_out, full, mid, cot_full, wqkv, wo_role, wu_role, wd_role,
    small_own, part, wv, wov, dist, vt, side, far, mix,
    ts, tr, ps, pr, xs, xr, ss, sr, cs, cr, rs, rr, gs, gr, load,
):
    at = places()
    moved = at["moved"]
    still = jnp.logical_not(moved)
    rows = tok.shape[0]
    step = rows // CHUNKS
    cols = wov.shape[0]
    rank = small.shape[0]
    greet((at["core"], at["near"]), (at["cross"], at["left"], at["up"], at["both"]), moved)
    qkv_span = w3.shape[1] // 4
    supply = Supply(
        at,
        [(w3.at[j], wqkv.at[j], True, qkv_span) for j in range(3)]
        + [(wo, wo_role, True, ITEM), (cot, cot_full, False, ITEM), (wu, wu_role, True, ITEM), (wd, wd_role, True, ITEM)],
        xs, xr, ss, sr,
    )
    relay = Relay(at, cot_full, cs, cr)

    def token(i):
        here = pl.ds(i * step, step)
        return remote(tokens.at[here], tok.at[here], ts.at[i], tr.at[i], at["cross"])

    def packs():
        return (
            remote(small_own, small, ps.at[0], pr.at[0], at["cross"]),
            remote(numbers, nums, ps.at[1], pr.at[1], at["cross"]),
        )

    @pl.when(moved)
    def _():
        for i in range(CHUNKS):
            token(i).start()
        supply.begin(AHEAD)

    for j in range(3):
        small_own[:, j * cols : (j + 1) * cols] = t_bq[ids[0], j]
    at_col = 3 * cols
    small_own[:, at_col : at_col + cols] = t_ao[ids[1]]
    at_col += cols
    wide = t_bu.shape[2]
    small_own[:, at_col : at_col + wide] = t_bu[ids[2]]
    at_col += wide
    small_own[:, at_col : at_col + wide] = t_ad[ids[3]]
    get_c = pltpu.make_async_copy(cot, cot_full.at[pl.ds(0, rows)], load.at[4])

    @pl.when(moved)
    def _():
        for copy in packs():
            copy.start()

    @pl.when(still)
    def _():
        get_c.start()
        tok[...] = tokens[...]
        small[...] = small_own[...]
        nums[...] = numbers[...]

    spread = Spread(at, x, gs.at[0], gr.at[0])
    for i in range(CHUNKS):
        here = slice(i * step, (i + 1) * step)

        @pl.when(moved)
        def _():
            token(i).wait_recv()

        unit, _ = unit_rows(tok[here].astype(F32))
        x[here] = (unit * norm_gains[0:1] + norm_shifts[0:1]).astype(BF16)
        spread.post(i)
    supply.tick(0)

    @pl.when(moved)
    def _():
        for copy in packs():
            copy.wait_recv()

    base = 2 * cols + wide
    key = lambda k: nums[0:1, base + k : base + k + 1]
    for k, table in enumerate((t_aq, t_bo, t_au, t_bd)):
        chosen[k * rank : (k + 1) * rank] = pick_row(table, key(2 + k))
    for i in range(CHUNKS):
        spread.forward(i)
    supply.tick(1)
    spread.finish()
    supply.tick(2)
    aq, bo = chosen[0:rank], chosen[rank : 2 * rank]
    rank_qkv[...] = dot_t(x[...], aq).astype(BF16)
    for j in range(3):
        supply.ready(j)
        fetch(w3.at[j], wqkv.at[j], wv.at[j], load.at[j]).wait()
        span = slice(j * cols, (j + 1) * cols)

        def strip(i, carry):
            here = pl.ds(pl.multiple_of(i * rows, rows), rows)
            value = dot(x[here], wv[j]) + dot(rank_qkv[here], small[:, span])
            if j != 1:
                value = value + nums[0:1, (j // 2) * cols : (j // 2 + 1) * cols]
            proj[here, span] = value.astype(BF16)
            return carry

        lax.fori_loop(0, 4, strip, 0)
    supply.tick(3)
    me = 2 * (lax.axis_index("dp") % 2) + lax.axis_index("tensor") % 2
    vt[...] = proj[:, 2 * cols :].T
    scale = LOG2E / math.sqrt(HEAD_DIM)
    slopes = head_slopes(me, cols // HEAD_DIM)

    def attend_step(i, carry):
        here = pl.ds(pl.multiple_of(i * rows, rows), rows)
        distances(me, key(0), key(1), rows, i, dist)
        for h in range(cols // HEAD_DIM):
            span = slice(h * HEAD_DIM, (h + 1) * HEAD_DIM)
            keys = proj[:, cols + h * HEAD_DIM : cols + (h + 1) * HEAD_DIM]
            s = dot_t(keys, proj[here, span]) * scale - dist[...] * slopes[h]
            peak = jnp.max(s, axis=0, keepdims=True)
            e = jnp.exp2(s - peak)
            total = jnp.sum(e, axis=0, keepdims=True)
            c = dot(vt[span, :], e.astype(BF16)) * (1.0 / total)
            ctx[here, span] = c.T.astype(BF16)
            lse[h : h + 1, here] = peak + jnp.log2(total)
        return carry

    def attend(first, count):
        lax.fori_loop(first, first + count, attend_step, 0)

    attend(0, 1)
    supply.tick(4)

    @pl.when(still)
    def _():
        get_c.wait()

    relay.post(0)
    attend(1, 1)
    supply.tick(5)
    relay.post(1)
    attend(2, 1)
    supply.tick(6)
    relay.forward(0)
    attend(3, 1)
    supply.tick(7)
    relay.forward(1)
    supply.ready(3)
    fetch(wo, wo_role, wov, load.at[3]).wait()
    ao = small[:, 3 * cols : 4 * cols]

    def out_rows(i):
        here = pl.ds(i * rows, rows)
        r = dot_t(ctx[here], ao).astype(BF16)
        rank_out[here] = r
        part[here] = (dot(ctx[here], wov[...]) + dot(r, bo)).astype(BF16)

    total = Gathered(at, part, side, far, mix, rs, rr)
    out_rows(3)
    total.send_away()
    out_rows(1)
    total.send_home()
    out_rows(2)
    total.send_over()
    out_rows(0)
    supply.tick(8)
    spread_mid = Spread(at, full, gs.at[1], gr.at[1])
    for i in range(CHUNKS):
        here = slice(i * step, (i + 1) * step)
        value = tok[here].astype(F32) + (total.take(i) + obias[...])
        mid[here] = value
        unit, _ = unit_rows(value)
        full[here] = (unit * norm_gains[1:2] + norm_shifts[1:2]).astype(BF16)
        spread_mid.post(i)
        if i % 2 == 1:
            supply.tick(9 + i // 2)
    for i in range(CHUNKS):
        spread_mid.forward(i)
        if i == 1:
            supply.tick(11)
    for n in range(12, len(supply.items)):
        supply.tick(n)
    total.finish()
    spread_mid.finish()
    relay.finish(2)
    for k in (5, 6):
        supply.ready(k)
    supply.finish()

    @pl.when(moved)
    def _():
        for i in range(CHUNKS):
            token(i).wait_send()
        for copy in packs():
            copy.wait_send()


def front(ids, tokens, numbers, tables, norm_gains, norm_shifts, obias, w3, wo, wu, wd, cot):
    rows, width = tokens.shape
    n = 4 * rows
    cols = w3.shape[2]
    rank = tables[1].shape[1]
    packed = 4 * cols + 2 * wu.shape[1]
    items = 3 + (wo.shape[0] + wu.shape[0] + wd.shape[0]) // 4 // ITEM + rows // ITEM
    low = lambda *s: jax.ShapeDtypeStruct(s, BF16)
    high = lambda *s: jax.ShapeDtypeStruct(s, F32)
    return pl.pallas_call(
        front_kernel,
        in_specs=[pl.BlockSpec(memory_space=pltpu.SMEM)] + [VMEM_SPEC] * 13 + [ANY_SPEC] * 5,
        out_specs=[VMEM_SPEC] * 12 + [ANY_SPEC] * 5,
        out_shape=[
            low(n, width), low(rows, width), low(rank, packed), high(*numbers.shape), low(4 * rank, width),
            low(n, 3 * cols), high(cols // HEAD_DIM, n), low(n, cols), low(n, rank), low(n, rank),
            low(n, width), high(rows, width), low(n, width), low(*w3.shape), low(*wo.shape), low(*wu.shape), low(*wd.shape),
        ],
        scratch_shapes=[
            VM((rank, packed), BF16),
            VM((n, width), BF16), VM(w3.shape, BF16), VM(wo.shape, BF16), VM((n, rows), F32), VM((cols, n), BF16),
            VM((2 * rows, width), BF16), VM((rows, width), BF16), VM((rows, width), BF16),
        ]
        + sems(CHUNKS) + sems(2) + sems(items) + sems(items, 3) + sems(3, rows // ITEM)
        + sems(3, CHUNKS) + sems(2, 3, CHUNKS) + [pltpu.SemaphoreType.DMA((5,))],
        compiler_params=comm_params(1, 60),
        name="front",
    )(ids, tokens, numbers, *tables, norm_gains, norm_shifts, obias, w3, wo, wu, wd, cot)


def routes(nd, nt):
    def lin(d, t):
        return d * nt + t

    every = [(d, t) for d in range(nd) for t in range(nt)]
    moved = [(d, t) for d, t in every if (d & 1) != (t >> 1)]
    both = [(lin(d, t), lin(d ^ 1, t ^ 2)) for d, t in moved]
    return dict(
        swap=both + [(lin(d, t), lin(d, t)) for d, t in every if (d & 1) == (t >> 1)],
        cross=both,
        core=[(lin(d, t), lin(d ^ 1, t)) for d, t in every],
        near=[(lin(d, t), lin(d, t ^ 1)) for d, t in every],
        left=[(lin(d, t), lin(d ^ 2, t)) for d, t in moved],
        up=[(lin(d, t), lin(d ^ 4, t)) for d, t in moved],
    )


def body(
    tokens, cotangent, norm_gains, norm_shifts, query_key_value_weight, b_qv, output_weight,
    output_bias_vector, up_weight, b_up, down_weight, down_bias_vector, adapter_query_key_value_input,
    qkv_out, adapter_output_input, adapter_output_output, adapter_up_input, up_out, down_in,
    adapter_down_output, offsets, adapter_ids,
):
    nd, nt = lax.axis_size("dp"), lax.axis_size("tensor")
    route = routes(nd, nt)
    d, t = lax.axis_index("dp"), lax.axis_index("tensor")
    c, p = d % 2, (d // 2) % 4
    moved = c != t // 2
    me = 2 * c + t % 2
    rows, width = tokens.shape
    length = rows * nt
    local = output_weight.shape[0]
    local_heads = local // HEAD_DIM
    hidden_width = up_weight.shape[1]
    rank = adapter_up_input.shape[1]
    tables = adapter_up_input.shape[0]

    def go(x, name):
        return lax.ppermute(x, AXES, route[name])

    w3 = jnp.transpose(query_key_value_weight, (1, 0, 2))
    b3 = jnp.transpose(qkv_out, (0, 2, 1, 3))
    extra = jnp.pad(jnp.concatenate([offsets, adapter_ids], 1).astype(F32), ((0, 0), (0, 122)))
    numbers = jnp.concatenate([b_qv.reshape(1, 2 * local), b_up.reshape(1, hidden_width), extra], 1)
    tables_in = (
        b3, adapter_output_input, up_out, down_in, adapter_query_key_value_input, adapter_output_output,
        adapter_up_input, adapter_down_output,
    )
    (
        x, tok, small, nums, chosen, proj, lse, ctx, rank_qkv, rank_out, nm, middle, cot, wqkv, wo, wu, wd,
    ) = front(
        adapter_ids[0], tokens, numbers, tables_in, norm_gains, norm_shifts, output_bias_vector.reshape(1, width),
        w3, output_weight, up_weight, down_weight, cotangent,
    )
    cuts = [3 * local, 4 * local, 4 * local + hidden_width]
    gain = [norm_gains[i : i + 1] for i in range(2)]

    def scatter(home, away):
        far = (away[:rows].astype(F32) + go(away[rows:], "core").astype(F32)).astype(BF16)
        far = go(far, "near")
        side = go(home[rows:], "core")
        return home[:rows].astype(F32) + side.astype(F32) + far.astype(F32)

    part, back, t_up_out, t_down_in, t_up_in, t_down_out = mlp(
        nm, cot, up_weight, wu, down_weight, wd, chosen, small, nums, hidden_width // 4
    )
    cot_own = cot[:rows]
    gm, grad_middle = turn_rows(back, cot_own, middle, gain[1])
    result = (middle + (scatter(part[: 2 * rows], part[2 * rows :]) + down_bias_vector)).astype(BF16)
    grad_ctx, t_out_out, t_out_in = bwd_o(gm, output_weight, wo, chosen, small, rank_out, ctx, rows)
    grad_proj = attend_back(nums, proj, grad_ctx, lse, rows)
    gx, t_qkv_out, t_qkv_in = bwd_qkv(grad_proj, w3, wqkv, small, chosen, rank_qkv, x, rows)
    in_grad = leave(gx, tok, grad_middle, gain[0])

    result = go(result, "swap")

    def owned(pieces):
        return lax.all_gather(go(jnp.concatenate(pieces, 1).astype(BF16), "swap"), "dp", axis=0)

    everyone = lax.all_gather(adapter_ids, "dp", axis=0, tiled=True)
    hot = (everyone[:, :, None] == jnp.arange(tables, dtype=jnp.int32)).astype(BF16)

    def combine(per, which):
        return jnp.einsum("se,srm->erm", hot[:, which], per, preferred_element_type=F32)

    own = owned([t[:rank] for t in (t_qkv_out, t_out_in, t_up_out, t_down_in)])
    g_qkv_out = jnp.einsum(
        "se,srkm->erkm", hot[:, 0], own[:, :, : cuts[0]].reshape(nd, rank, 3, local), preferred_element_type=F32
    )
    g_out_in = combine(own[:, :, cuts[0] : cuts[1]], 1)
    g_up_out = combine(own[:, :, cuts[1] : cuts[2]], 2)
    g_down_in = combine(own[:, :, cuts[2] :], 3)

    shared = jnp.stack([t[:rank] for t in (t_qkv_in, t_out_out, t_up_in, t_down_out)]).astype(BF16)
    shared = shared.astype(F32) + go(shared, "core").astype(F32)
    shared = (shared + go(shared.astype(BF16), "near").astype(F32)).astype(BF16)
    quarter = width // 4
    mine = lax.dynamic_slice_in_dim(shared, me * quarter, quarter, 2)
    mine = go(mine, "swap")
    mine = lax.all_gather(mine, "dp", axis=0)
    sums = jnp.einsum("ske,skrm->kerm", hot.transpose(0, 1, 2), mine, preferred_element_type=F32)
    whole = lax.all_gather(sums.astype(BF16), "tensor", axis=3, tiled=True).astype(F32)
    return (
        result, in_grad, whole[0], g_qkv_out, g_out_in, whole[1], whole[2], g_up_out, g_down_in, whole[3],
    )


def solution(mesh):
    placed = (
        P(("dp", "tensor"), None), P(("dp", "tensor"), None), P(), P(), P(None, None, "tensor"), P(None, "tensor"),
        P("tensor", None), P(), P(None, "tensor"), P("tensor"), P("tensor", None), P(), P(),
        P(None, None, None, "tensor"), P(None, None, "tensor"), P(), P(), P(None, None, "tensor"),
        P(None, None, "tensor"), P(), P("dp", None), P("dp", None),
    )
    return jax.shard_map(
        body, mesh=mesh, in_specs=placed,
        out_specs=(
            P(("dp", "tensor"), None), P(("dp", "tensor"), None), P(), P(None, None, None, "tensor"),
            P(None, None, "tensor"), P(), P(), P(None, None, "tensor"), P(None, None, "tensor"), P(),
        ),
        check_vma=False,
    )
```

time: 774 us -> 627 us (0.81)
  waiting for transfers between devices: 110 us -> 29 us
  Pallas kernels: 428 us -> 495 us
  starting transfers between devices: 66.7 us -> 12 us
  local copies, waits for them, and re-layouts: 68.8 us -> 36 us
  other arithmetic: 41.4 us -> 14.1 us
  between operations: 30.8 us -> 14.6 us
    ppermute x27 -> x8, waiting for transfers between devices: 110 us -> 28.9 us  [go(): return lax.ppermute(x, AXES, route[name])]
    pallas_call x10 -> x5, Pallas kernels: 289 us -> 356 us  [the longest x1 249 us: front(): pl.pallas_call(front_kernel, in_specs=[pl.BlockSpec(memory_space=pltpu.SM...]
    ppermute x27 -> x8, starting transfers between devices: 66.6 us -> 11.9 us  [go(): return lax.ppermute(x, AXES, route[name])]
    select_n x6 -> x0, other arithmetic: 22.2 us -> none  [the longest x3 13.9 us: bring(): return jnp.where(moved, jnp.concatenate(whole, axis), weight)]
    unnamed x72 -> x43, local copies, waits for them, and re-layouts: 34.1 us -> 26.9 us
  transfers between devices with their start and end apart: 29 -> 10, of which waited for: 6 -> 3; matrix products, arithmetic and copies ran while one was open for 10% -> 4% of each run, Pallas kernels for 38% -> 14%
where the time goes in v2:
time: 627 us; the launch traced here: 622 us
  Pallas kernels  495 us (79%)
  local copies, waits for them, and re-layouts  36 us (6%)
  waiting for transfers between devices  29 us (5%)
  blocking collectives  17.9 us (3%)
  between operations  14.6 us (2%)
  other arithmetic  14.1 us (2%)
  starting transfers between devices  12 us (2%)
    pallas_call x1, Pallas kernels, front(): pl.pallas_call(front_kernel, in_specs=[pl.BlockSpec(memory_space=pltpu.SM...  249 us
    pallas_call x1, Pallas kernels, leave(): pl.pallas_call(leave_kernel, in_specs=[VMEM_SPEC] * 4, out_specs=VMEM_SPE...  89 us
    pallas_call x1, Pallas kernels, mlp(): pl.pallas_call(mlp_kernel, grid=(hidden // tile, 2), in_specs=[row, row,...  56.6 us
    pallas_call x1, Pallas kernels, turn_rows(): pl.pallas_call(turn_kernel, in_specs=[VMEM_SPEC] * 4, out_specs=[VMEM_SPE...  49.6 us
    ppermute x8, waiting for transfers between devices, go(): return lax.ppermute(x, AXES, route[name])  28.9 us
    unnamed x43, local copies, waits for them, and re-layouts  26.9 us
    pallas_call x1, Pallas kernels, attend_back(): pl.pallas_call(attend_back_kernel, grid=(length // rows,), in_specs=[whol...  24 us
    pallas_call x1, Pallas kernels, bwd_qkv(): pl.pallas_call(bwd_qkv_kernel, grid=(n // tile,), in_specs=[row(k), HERE,...  15.8 us
  transfers between devices with their start and end apart: 10, of which 3 were waited for; matrix products, arithmetic and copies ran while one was open for 4% of the time, Pallas kernels for 14%

profile of v2, /device:TPU:1, one launch (start us, length us, event | category | flops | bytes accessed | tf_op | source)
XLA Modules:
  0.0 621.5 jit_solution(4453784471335721122)
XLA Ops:
  7.9 0.8 fusion.15
  8.7 0.7 add_convert_fusion.2
  9.5 1.3 fusion.11.numbers
  10.8 249.0 %front.1 = (bf16[1024,2048]{1,0:T(8,128)(2,1)}, bf16[256,2048]{1,0:T(8,128)(2,1)}, bf16[16,6144]{1,0:T(8,128)(2,1)}, f32[1,3200]{1,0:T(1,128)}, bf16[64,2048]{1,...) custom-call(s32[4]{0:T(128)} %bitcast.66, ...), custom_call_target="tpu_custom_call" | custom-call | tf_op jit(solution)/shard_map/front/pallas_call | solution.py:934
  259.8 1.3 slice.67.cot
  261.1 56.6 %mlp.1 = (bf16[1024,2048]{1,0:T(8,128)(2,1)}, bf16[1024,2048]{1,0:T(8,128)(2,1)}, f32[16,2048]{1,0:T(8,128)}, f32[16,2048]{1,0:T(8,128)}, f32[16,2048]{1,0:T(8,128)}, /*index=5*/f32[16,2048]{1,0:T(8,128)}) custom-call(bf16[1024,2048]{1,0:T(8,128)(2,1)} %get-tuple-element.42.nm, bf16[1024,2048]{1,0:T(8,128)(2,1)} %get-tuple-element.43.cot, ...), custom_call_target="tpu_custom_call" | custom-call | flops 34359738368 | bytes 41943040 | tf_op jit(solution)/shard_map/mlp/pallas_call | solution.py:355
  317.7 2.2 copy-done.2
  319.8 49.6 %turn_rows.1 = (bf16[1024,2048]{1,0:T(8,128)(2,1)S(1)}, f32[256,2048]{1,0:T(8,128)S(1)}) custom-call(bf16[1024,2048]{1,0:T(8,128)(2,1)S(1)} %copy-done.2, bf16[256,2048]{1,0:T(8,128)(2,1)S(1)} %slice.67.cot, f32[256,2048]{1,0:T(8,128)S(1)} %copy-done, f32[1,2048]{1,0:T(1,128)S(1)} %get-tuple-element.123.gain), custom_call_target="tpu_custom_call" | custom-call | tf_op jit(solution)/shard_map/turn_rows/pallas_call | solution.py:567
  369.4 2.0 copy-done.3
  371.4 1.4 copy-done.4
  372.8 11.1 %bwd_o.1 = (bf16[1024,512]{1,0:T(8,128)(2,1)}, f32[16,2048]{1,0:T(8,128)}, f32[16,512]{1,0:T(8,128)}) custom-call(bf16[1024,2048]{1,0:T(8,128)(2,1)} %copy-done.3, bf16[512,2048]{1,0:T(8,128)(2,1)} %native.1, bf16[512,2048]{1,0:T(8,128)(2,1)} %get-tuple-element.53.brought, bf16[64,2048]{1,0:T(8,128)(2,1)} %get-tuple-element.46.au.bd.b.a, ...), custom_call_target="tpu_custom_call" | custom-call | flops 2147483648 | bytes 7340032 | tf_op jit(solution)/shard_map/bwd_o/pallas_call | solution.py:99
  383.9 24.0 %attend_back.1.g = bf16[1024,1536]{1,0:T(8,128)(2,1)} custom-call(f32[1,3200]{1,0:T(1,128)} %get-tuple-element.48.bias.nums, bf16[1024,1536]{1,0:T(8,128)(2,1)} %get-tuple-element.50.q.k.v, bf16[1024,1536]{1,0:T(8,128)(2,1)} %get-tuple-element.50.q.k.v, bf16[1024,1536]{1,0:T(8,128)(2,1)} %get-tuple-element.50.q.k.v, bf16[1024,512]{1,0:T(8,128)(2,1)} %get-tuple-element.56.g, ...), custom_call_target="tpu_custom_call" | custom-call | flops 5368709120 | bytes 8388608 | tf_op jit(solution)/shard_map/attend_back/pallas_call | solution.py:226
  407.9 15.8 %bwd_qkv.1 = (bf16[1024,2048]{1,0:T(8,128)(2,1)}, f32[16,1536]{1,0:T(8,128)}, f32[16,2048]{1,0:T(8,128)}) custom-call(bf16[1024,1536]{1,0:T(8,128)(2,1)} %attend_back.1.g, bf16[3,2048,512]{2,1,0:T(8,128)(2,1)} %bitcast.54, bf16[3,2048,512]{2,1,0:T(8,128)(2,1)} %get-tuple-element.58.brought, bf16[16,6144]{1,0:T(8,128)(2,1)} %get-tuple-element.47.bu.ad.a.b, ...), custom_call_target="tpu_custom_call" | custom-call | flops 6442450944 | bytes 13631488 | tf_op jit(solution)/shard_map/bwd_qkv/pallas_call | solution.py:148
  423.7 0.9 convert.32
  424.7 4.2 collective-permute-start.7
  428.9 0.9 convert_bitcast_fusion.2
  429.9 4.9 collective-permute-done.7
  435.7 3.1 fusion.13
  439.3 0.9 fusion.12
  440.1 8.0 %collective-permute-done.5 = bf16[4,16,2048]{2,1,0:T(8,128)(2,1)} collective-permute-done((bf16[4,16,2048]{2,1,0:T(8,128)(2,1)S(1)}, bf16[4,16,2048]{2,1,0:T(8,128)(2,1)}, u32[]{:S(2)}, u32[]{:S(2)}) %collective-permute-start.5) | collective-permute-done | bytes 262176 | tf_op jit(solution)/shard_map/ppermute | solution.py:993
  448.2 0.9 fusion.7
  449.1 3.6 collective-permute-start.6
  452.8 8.1 %all-gather.2 = s32[8,1,4]{2,1,0:T(1,128)S(1)} all-gather(s32[1,1,4]{2,1,0:T(1,128)S(1)} %bitcast.67), channel_id=1, replica_groups=mesh['dp'=8,'tensor'=4] {'dp'}, dimensions={0}, use_global_device_ids=true | all-gather | bytes 144 | tf_op jit(solution)/shard_map/all_gather | solution.py:1034
  460.9 9.8 %all-gather = bf16[32,16,512]{2,1,0:T(8,128)(2,1)S(1)} all-gather(bf16[4,16,512]{2,1,0:T(8,128)(2,1)S(1)} %collective-permute-done.6), channel_id=2, replica_groups=mesh['dp'=8,'tensor'=4] {'dp'}, dimensions={0}, use_global_device_ids=true | all-gather | bytes 589824 | tf_op jit(solution)/shard_map/all_gather | solution.py:1054
  470.8 2.6 add_convert_fusion.1
  473.4 1.5 collective-permute-start.2
  474.8 1.3 convolution_convert_fusion
  476.2 2.2 copy-done.1
  478.4 1.6 copy-done.5
  480.0 1.2 copy-done.6
  481.2 89.0 %leave.1 = bf16[256,2048]{1,0:T(8,128)(2,1)S(1)} custom-call(bf16[1024,2048]{1,0:T(8,128)(2,1)S(1)} %copy-done.1, bf16[256,2048]{1,0:T(8,128)(2,1)S(1)} %copy-done.6, f32[256,2048]{1,0:T(8,128)S(1)} %copy-done.5, f32[1,2048]{1,0:T(1,128)S(1)} %get-tuple-element.122.gain), custom_call_target="tpu_custom_call" | custom-call | tf_op jit(solution)/shard_map/leave/pallas_call | solution.py:615
  570.3 3.5 add_convert_fusion
  573.9 2.0 collective-permute-start.3
  575.9 1.3 fusion.14
  577.2 1.0 slice.84
  578.2 0.9 slice.86
  579.6 1.6 copy.103
  581.6 1.6 copy.104
  583.9 1.3 copy.99
  585.5 0.9 copy.100
  586.3 16.0 %collective-permute-done.3 = bf16[256,2048]{1,0:T(8,128)(2,1)} collective-permute-done((bf16[256,2048]{1,0:T(8,128)(2,1)}, bf16[256,2048]{1,0:T(8,128)(2,1)}, u32[]{:S(2)}, u32[]{:S(2)}) %collective-permute-start.3) | collective-permute-done | bytes 1048608 | tf_op jit(solution)/shard_map/ppermute | solution.py:993
  602.4 2.1 convert_element_type.72
  604.9 1.6 copy.101
  606.4 1.6 copy.102
  608.0 1.6 copy.105
  609.6 1.6 copy.98
  611.2 2.3 copy.133
  613.5 1.0 copy.134
  (56 shorter events, 4.6 us)
Async XLA Ops:
  7.2 568.7 %all-gather.8.cloned.1.call-start = ((), (), s32[]{:S(2)}) async-start(), calls=%async_computation.1 | async-start | bytes 1769472 | tf_op jit(solution)/shard_map/all_gather | solution.py:1032
  261.1 56.6 %copy-start = (f32[256,2048]{1,0:T(8,128)S(1)}, f32[256,2048]{1,0:T(8,128)}, u32[]{:S(2)}) copy-start(f32[256,2048]{1,0:T(8,128)} %get-tuple-element.41.mid) | copy-start | bytes 6291460
  317.7 2.2 copy-start.2
  369.4 2.0 copy-start.3
  371.4 1.4 copy-start.4
  407.9 16.7 %copy-start.13 = (f32[16,512]{1,0:T(8,128)S(1)}, f32[16,512]{1,0:T(8,128)}, u32[]{:S(2)}) copy-start(f32[16,512]{1,0:T(8,128)} %get-tuple-element.69) | copy-start | bytes 98308
  407.9 16.8 %copy-start.12 = (f32[16,2048]{1,0:T(8,128)S(1)}, f32[16,2048]{1,0:T(8,128)}, u32[]{:S(2)}) copy-start(f32[16,2048]{1,0:T(8,128)} %get-tuple-element.70) | copy-start | bytes 393220
  407.9 16.8 %copy-start.11 = (f32[16,2048]{1,0:T(8,128)S(1)}, f32[16,2048]{1,0:T(8,128)}, u32[]{:S(2)}) copy-start(f32[16,2048]{1,0:T(8,128)} %get-tuple-element.71) | copy-start | bytes 393220
  407.9 21.0 %copy-start.10 = (f32[16,2048]{1,0:T(8,128)S(1)}, f32[16,2048]{1,0:T(8,128)}, u32[]{:S(2)}) copy-start(f32[16,2048]{1,0:T(8,128)} %get-tuple-element.65) | copy-start | bytes 393220
  407.9 27.6 %copy-start.8 = (f32[16,2048]{1,0:T(8,128)S(1)}, f32[16,2048]{1,0:T(8,128)}, u32[]{:S(2)}) copy-start(f32[16,2048]{1,0:T(8,128)} %get-tuple-element.66) | copy-start | bytes 393220
  407.9 27.6 %copy-start.9 = (f32[16,2048]{1,0:T(8,128)S(1)}, f32[16,2048]{1,0:T(8,128)}, u32[]{:S(2)}) copy-start(f32[16,2048]{1,0:T(8,128)} %get-tuple-element.67) | copy-start | bytes 393220
  424.7 10.0 %collective-permute-start.7 = (bf16[16,6144]{1,0:T(8,128)(2,1)S(1)}, bf16[16,6144]{1,0:T(8,128)(2,1)S(1)}, u32[]{:S(2)}, u32[]{:S(2)}) collective-permute-start(bf16[16,6144]{1,0:T(8,128)(2,1)S(1)} %pad_maximum_fusion.1), channel_id=1, source_target_pairs={{2,4},{3,5},{4,2},{5,3},{10,12},{11,13},{12,10},{13,11},{18,20},{1... | collective-permute-start | bytes 589832 | tf_op jit(solution)/shard_map/ppermute | solution.py:993
  434.7 0.7 copy-start.7
  435.4 166.9 %all-gather.6.cloned.1.call-start = ((), (), s32[]{:S(2)}) async-start(), calls=%async_computation | async-start | bytes 2621440 | tf_op jit(solution)/shard_map/all_gather | solution.py:1056
  435.5 17.3 %copy-start.15 = (s32[1,4]{1,0:T(1,128)S(1)}, s32[1,4]{1,0:T(1,128)}, u32[]{:S(2)}) copy-start(s32[1,4]{1,0:T(1,128)} %param.43) | copy-start | bytes 52
  435.6 3.7 collective-permute-start.4
  438.8 32.0 %collective-permute-start.1 = (bf16[256,2048]{1,0:T(8,128)(2,1)}, bf16[256,2048]{1,0:T(8,128)(2,1)S(1)}, u32[]{:S(2)}, u32[]{:S(2)}) collective-permute-start(bf16[256,2048]{1,0:T(8,128)(2,1)} %get-tuple-element.117), channel_id=1, source_target_pairs={{0,4},{1,5},{2,6},{3,7},{4,0},{5,1},{6,2},{7,3},{8,12},{9,13},{10,... | collective-permute-start | bytes 3145736 | tf_op jit(solution)/shard_map/ppermute | solution.py:993
  440.1 8.0 %collective-permute-start.5 = (bf16[4,16,2048]{2,1,0:T(8,128)(2,1)S(1)}, bf16[4,16,2048]{2,1,0:T(8,128)(2,1)}, u32[]{:S(2)}, u32[]{:S(2)}) collective-permute-start(bf16[4,16,2048]{2,1,0:T(8,128)(2,1)S(1)} %get-tuple-element.120), channel_id=1, source_target_pairs={{0,1},{1,0},{2,3},{3,2},{4,5},{5,4},{6,7},{7,6},{8,9},{9,8},{10,11... | collective-permute-start | bytes 786440 | tf_op jit(solution)/shard_map/ppermute | solution.py:993
  449.1 11.8 %collective-permute-start.6 = (bf16[4,16,512]{2,1,0:T(8,128)(2,1)S(1)}, bf16[4,16,512]{2,1,0:T(8,128)(2,1)S(1)}, u32[]{:S(2)}, u32[]{:S(2)}) collective-permute-start(bf16[4,16,512]{2,1,0:T(8,128)(2,1)S(1)} %fusion.7), channel_id=1, source_target_pairs={{2,4},{3,5},{4,2},{5,3},{10,12},{11,13},{12,10},{13,11},{18,20},{1... | collective-permute-start | bytes 196616 | tf_op jit(solution)/shard_map/ppermute | solution.py:993
  452.7 117.6 %collective-permute-start = (bf16[256,2048]{1,0:T(8,128)(2,1)}, bf16[256,2048]{1,0:T(8,128)(2,1)}, u32[]{:S(2)}, u32[]{:S(2)}) collective-permute-start(bf16[256,2048]{1,0:T(8,128)(2,1)} %get-tuple-element.116), channel_id=1, source_target_pairs={{0,4},{1,5},{2,6},{3,7},{4,0},{5,1},{6,2},{7,3},{8,12},{9,13},{10,... | collective-permute-start | bytes 3145736 | tf_op jit(solution)/shard_map/ppermute | solution.py:993
  473.4 97.0 %collective-permute-start.2 = (bf16[256,2048]{1,0:T(8,128)(2,1)}, bf16[256,2048]{1,0:T(8,128)(2,1)}, u32[]{:S(2)}, u32[]{:S(2)}) collective-permute-start(bf16[256,2048]{1,0:T(8,128)(2,1)} %add_convert_fusion.1), channel_id=1, source_target_pairs={{0,1},{1,0},{2,3},{3,2},{4,5},{5,4},{6,7},{7,6},{8,9},{9,8},{10,11... | collective-permute-start | bytes 3145736 | tf_op jit(solution)/shard_map/ppermute | solution.py:993
  476.2 2.2 copy-start.1
  478.4 1.6 copy-start.5
  480.0 1.2 copy-start.6
  481.2 89.1 %copy-start.14 = (f32[2048]{0:T(1024)S(1)}, f32[2048]{0:T(1024)}, u32[]{:S(2)}) copy-start(f32[2048]{0:T(1024)} %param.33) | copy-start | bytes 24580
  573.9 28.5 %collective-permute-start.3 = (bf16[256,2048]{1,0:T(8,128)(2,1)}, bf16[256,2048]{1,0:T(8,128)(2,1)}, u32[]{:S(2)}, u32[]{:S(2)}) collective-permute-start(bf16[256,2048]{1,0:T(8,128)(2,1)} %add_convert_fusion), channel_id=1, source_target_pairs={{2,4},{3,5},{4,2},{5,3},{10,12},{11,13},{12,10},{13,11},{18,20},{1... | collective-permute-start | bytes 3145736 | tf_op jit(solution)/shard_map/ppermute | solution.py:993
Sparse Core Ops, SparseCore 0:
  435.6 24.3 all-gather.7
  476.3 74.0 all-gather.5

commit v3 on v2

--- a/solution.py
+++ b/solution.py
@@ -12,7 +12,7 @@
 HEAD_DIM = 128
 PIECE = 256
 ITEM = 128
-AHEAD = 3
+AHEAD = 2
 EPS = 1e-05
 GELU_C = 0.7978845608028654
 GELU_K = 0.044715
@@ -68,100 +68,6 @@
     return pltpu.make_async_copy(native, into, sem)
 
 
-def bwd_o_kernel(g, native, brought, b, a, rank, x, out, tb, ta, w, sem):
-    first = pl.program_id(0) == 0
-
-    @pl.when(first)
-    def _():
-        fetch(native, brought, w, sem).wait()
-
-    r = dot_t(g[...], b[...]).astype(BF16)
-    out[...] = (dot_t(g[...], w[...]) + dot(r, a[...])).astype(BF16)
-    one = t_dot(rank[...], g[...])
-    two = t_dot(r, x[...])
-
-    @pl.when(first)
-    def _():
-        tb[...] = one
-        ta[...] = two
-
-    @pl.when(jnp.logical_not(first))
-    def _():
-        tb[...] += one
-        ta[...] += two
-
-
-def bwd_o(g, w, brought, chosen, small, rank, x, tile):
-    n, k = g.shape
-    cols = w.shape[0]
-    low = rank.shape[1]
-    row = lambda c: pl.BlockSpec((tile, c), lambda i: (i, 0))
-    return pl.pallas_call(
-        bwd_o_kernel,
-        grid=(n // tile,),
-        in_specs=[row(k), HERE, HERE, pl.BlockSpec((low, k), lambda i: (1, 0)), pl.BlockSpec((low, cols), lambda i: (0, 3)), row(low), row(cols)],
-        out_specs=[row(cols), whole((low, k)), whole((low, cols))],
-        out_shape=[
-            jax.ShapeDtypeStruct((n, cols), BF16),
-            jax.ShapeDtypeStruct((low, k), F32),
-            jax.ShapeDtypeStruct((low, cols), F32),
-        ],
-        scratch_shapes=[VM(w.shape, BF16), pltpu.SemaphoreType.DMA],
-        compiler_params=params(),
-        cost_estimate=cost(2 * n * k * cols, 2 * (n * k + k * cols + n * cols)),
-        name="bwd_o",
-    )(g, w, brought, chosen, small, rank, x)
-
-
-def bwd_qkv_kernel(g, native, brought, b, a, rank, x, out, tb, ta, w, sem):
-    first = pl.program_id(0) == 0
-
-    @pl.when(first)
-    def _():
-        fetch(native, brought, w, sem).wait()
-
-    cols = w.shape[2]
-    r = dot_t(g[...], b[...]).astype(BF16)
-    acc = dot(r, a[...])
-    for j in range(3):
-        acc = acc + dot_t(g[:, j * cols : (j + 1) * cols], w[j])
-    out[...] = acc.astype(BF16)
-    one = t_dot(rank[...], g[...])
-    two = t_dot(r, x[...])
-
-    @pl.when(first)
-    def _():
-        tb[...] = one
-        ta[...] = two
-
-    @pl.when(jnp.logical_not(first))
-    def _():
-        tb[...] += one
-        ta[...] += two
-
-
-def bwd_qkv(g, w3, brought, small, chosen, rank, x, tile):
-    n, k = g.shape
-    cols = w3.shape[1]
-    low = rank.shape[1]
-    row = lambda c: pl.BlockSpec((tile, c), lambda i: (i, 0))
-    return pl.pallas_call(
-        bwd_qkv_kernel,
-        grid=(n // tile,),
-        in_specs=[row(k), HERE, HERE, pl.BlockSpec((low, k), lambda i: (0, 0)), pl.BlockSpec((low, cols), lambda i: (0, 0)), row(low), row(cols)],
-        out_specs=[row(cols), whole((low, k)), whole((low, cols))],
-        out_shape=[
-            jax.ShapeDtypeStruct((n, cols), BF16),
-            jax.ShapeDtypeStruct((low, k), F32),
-            jax.ShapeDtypeStruct((low, cols), F32),
-        ],
-        scratch_shapes=[VM(w3.shape, BF16), pltpu.SemaphoreType.DMA],
-        compiler_params=params(),
-        cost_estimate=cost(2 * n * k * cols, 2 * (n * k + k * cols + n * cols)),
-        name="bwd_qkv",
-    )(g, w3, brought, small, chosen, rank, x)
-
-
 def distances(me, s0, s1, rows, step, dist):
     length = dist.shape[0]
 
@@ -182,67 +88,6 @@
 def head_slopes(me, heads):
     first = jnp.full((1, 1), me * heads, jnp.int32).astype(F32)
     return [jnp.exp2((first + float(h + 1)) * (-8.0 / HEADS)) * LOG2E for h in range(heads)]
-
-
-def attend_back_kernel(nums, q, k, v, g, lse, out, dist, kt, gk, gv):
-    step = pl.program_id(0)
-    rows = q.shape[0]
-    local = q.shape[1]
-    heads = local // HEAD_DIM
-    scale = 1.0 / math.sqrt(HEAD_DIM)
-    me = 2 * (lax.axis_index("dp") % 2) + lax.axis_index("tensor") % 2
-    base = nums.shape[1] - 128
-    distances(me, nums[0:1, base : base + 1], nums[0:1, base + 1 : base + 2], rows, step, dist)
-    slopes = head_slopes(me, heads)
-
-    @pl.when(step == 0)
-    def _():
-        kt[...] = k[...].T
-        gk[...] = jnp.zeros_like(gk)
-        gv[...] = jnp.zeros_like(gv)
-
-    at = pl.ds(pl.multiple_of(step * rows, rows), rows)
-    for h in range(heads):
-        span = slice(h * HEAD_DIM, (h + 1) * HEAD_DIM)
-        s = dot_t(k[:, span], q[:, span]) * (scale * LOG2E) - dist[...] * slopes[h]
-        p = jnp.exp2(s - lse[h : h + 1, :])
-        gv[:, span] += dot(p.astype(BF16), g[:, span])
-        gp = dot_t(v[:, span], g[:, span])
-        inner = jnp.sum(p * gp, axis=0, keepdims=True)
-        gs = (p * (gp - inner)).astype(BF16)
-        gk[:, span] += dot(gs, q[:, span])
-        out[at, span] = (dot(kt[span, :], gs).T * scale).astype(BF16)
-
-    @pl.when(step == pl.num_programs(0) - 1)
-    def _():
-        out[:, local : 2 * local] = (gk[...] * scale).astype(BF16)
-        out[:, 2 * local :] = gv[...].astype(BF16)
-
-
-def attend_back(nums, proj, g, lse, rows):
-    length, three = proj.shape
-    local = three // 3
-    heads = local // HEAD_DIM
-    return pl.pallas_call(
-        attend_back_kernel,
-        grid=(length // rows,),
-        in_specs=[
-            whole(nums.shape),
-            pl.BlockSpec((rows, local), lambda i: (i, 0)),
-            pl.BlockSpec((length, local), lambda i: (0, 1)),
-            pl.BlockSpec((length, local), lambda i: (0, 2)),
-            pl.BlockSpec((rows, local), lambda i: (i, 0)),
-            pl.BlockSpec((heads, rows), lambda i: (0, i)),
-        ],
-        out_specs=pl.BlockSpec((length, three), lambda i: (0, 0)),
-        scratch_shapes=[
-            VM((length, rows), F32), VM((local, length), BF16), VM((length, local), F32), VM((length, local), F32),
-        ],
-        out_shape=jax.ShapeDtypeStruct((length, three), BF16),
-        compiler_params=params(),
-        cost_estimate=cost(10 * length * length * local, 16 * length * local),
-        name="attend_back",
-    )(nums, proj, proj, proj, g, lse)
 
 
 def gelu_parts(values):
@@ -475,8 +320,9 @@
 
 
 class Gathered:
-    def __init__(self, at, part, side, far, mix, send, recv):
+    def __init__(self, at, part, side, far, mix, send, recv, kept=None):
         self.at, self.part, self.side, self.far, self.mix = at, part, side, far, mix
+        self.kept, self.second = (part, 2) if kept is None else (kept, 1)
         self.send, self.recv = send, recv
         self.rows = part.shape[0] // 4
         self.step = self.rows // CHUNKS
@@ -507,7 +353,7 @@
         for i in range(CHUNKS):
             self.away(i).wait_recv()
             here = pl.ds(i * self.step, self.step)
-            ours = self.part[pl.ds(2 * self.rows + i * self.step, self.step)].astype(F32)
+            ours = self.kept[pl.ds(self.second * self.rows + i * self.step, self.step)].astype(F32)
             theirs = self.side[pl.ds(self.rows + i * self.step, self.step)].astype(F32)
             self.mix[here] = (ours + theirs).astype(BF16)
             self.over(i).start()
@@ -521,7 +367,7 @@
         self.home(i).wait_recv()
         self.over(i).wait_recv()
         here = pl.ds(i * self.step, self.step)
-        return self.part[here].astype(F32) + self.side[here].astype(F32) + self.far[here].astype(F32)
+        return self.kept[here].astype(F32) + self.side[here].astype(F32) + self.far[here].astype(F32)
 
     def finish(self):
         for i in range(CHUNKS):
@@ -540,89 +386,6 @@
 
 VMEM_SPEC = pl.BlockSpec(memory_space=pltpu.VMEM)
 ANY_SPEC = pl.BlockSpec(memory_space=pl.ANY)
-
-
-def turn_kernel(part, cot, mid, gain, full, grad, side, far, mix, rs, rr, gs, gr):
-    at = places()
-    greet((at["core"], at["near"]))
-    step = cot.shape[0] // CHUNKS
-    total = Gathered(at, part, side, far, mix, rs, rr)
-    spread = Spread(at, full, gs, gr)
-    total.begin()
-    for i in range(CHUNKS):
-        here = slice(i * step, (i + 1) * step)
-        unit, inverse = unit_rows(mid[here])
-        value = cot[here].astype(F32) + unit_back(total.take(i), unit, inverse, gain[...])
-        grad[here] = value
-        full[here] = value.astype(BF16)
-        spread.post(i)
-    for i in range(CHUNKS):
-        spread.forward(i)
-    total.finish()
-    spread.finish()
-
-
-def turn_rows(part, cot, mid, gain):
-    rows, width = cot.shape
-    return pl.pallas_call(
-        turn_kernel,
-        in_specs=[VMEM_SPEC] * 4,
-        out_specs=[VMEM_SPEC] * 2,
-        out_shape=[jax.ShapeDtypeStruct((4 * rows, width), BF16), jax.ShapeDtypeStruct((rows, width), F32)],
-        scratch_shapes=[VM((2 * rows, width), BF16), VM((rows, width), BF16), VM((rows, width), BF16)]
-        + sems(3, CHUNKS) + sems(3, CHUNKS),
-        compiler_params=comm_params(3, 40),
-        name="turn_rows",
-    )(part, cot, mid, gain)
-
-
-def leave_kernel(part, tok, grad, gain, out, side, far, mix, done, rs, rr, os, orr):
-    at = places()
-    moved = at["moved"]
-    greet((at["core"], at["near"]), (at["cross"],), moved)
-    step = tok.shape[0] // CHUNKS
-    total = Gathered(at, part, side, far, mix, rs, rr)
-
-    def back(i):
-        here = pl.ds(i * step, step)
-        return remote(done.at[here], out.at[here], os.at[i], orr.at[i], at["cross"])
-
-    total.begin()
-    for i in range(CHUNKS):
-        here = slice(i * step, (i + 1) * step)
-        unit, inverse = unit_rows(tok[here].astype(F32))
-        value = (grad[here] + unit_back(total.take(i), unit, inverse, gain[...])).astype(BF16)
-
-        @pl.when(moved)
-        def _():
-            done[here] = value
-            back(i).start()
-
-        @pl.when(jnp.logical_not(moved))
-        def _():
-            out[here] = value
-
-    total.finish()
-
-    @pl.when(moved)
-    def _():
-        for i in range(CHUNKS):
-            back(i).wait()
-
-
-def leave(part, tok, grad, gain):
-    rows, width = tok.shape
-    return pl.pallas_call(
-        leave_kernel,
-        in_specs=[VMEM_SPEC] * 4,
-        out_specs=VMEM_SPEC,
-        out_shape=jax.ShapeDtypeStruct((rows, width), BF16),
-        scratch_shapes=[
-            VM((2 * rows, width), BF16), VM((rows, width), BF16), VM((rows, width), BF16), VM((rows, width), BF16)
-        ] + sems(3, CHUNKS) + sems(CHUNKS),
-        compiler_params=comm_params(4, 40),
-        name="leave",
-    )(part, tok, grad, gain)
 
 
 class Supply:
@@ -952,21 +715,455 @@
     )(ids, tokens, numbers, *tables, norm_gains, norm_shifts, obias, w3, wo, wu, wd, cot)
 
 
-def routes(nd, nt):
-    def lin(d, t):
-        return d * nt + t
-
-    every = [(d, t) for d in range(nd) for t in range(nt)]
-    moved = [(d, t) for d, t in every if (d & 1) != (t >> 1)]
-    both = [(lin(d, t), lin(d ^ 1, t ^ 2)) for d, t in moved]
-    return dict(
-        swap=both + [(lin(d, t), lin(d, t)) for d, t in every if (d & 1) == (t >> 1)],
-        cross=both,
-        core=[(lin(d, t), lin(d ^ 1, t)) for d, t in every],
-        near=[(lin(d, t), lin(d, t ^ 1)) for d, t in every],
-        left=[(lin(d, t), lin(d ^ 2, t)) for d, t in moved],
-        up=[(lin(d, t), lin(d ^ 4, t)) for d, t in moved],
+class Tables:
+    def __init__(self, at, own, shared, own_home, quarter_home, own_all, quarter_all, every, buffers, semaphores):
+        self.at, self.own, self.shared = at, own, shared
+        self.own_home, self.quarter_home = own_home, quarter_home
+        self.own_all, self.quarter_all, self.every = own_all, quarter_all, every
+        self.half_in, self.half, self.quarter_in, self.quarter = buffers
+        (self.s1, self.r1, self.s2, self.r2, self.s3, self.r3, self.s4, self.r4, self.s5, self.r5, self.s6, self.r6, self.keep) = semaphores
+        self.d, self.t = lax.axis_index("dp"), lax.axis_index("tensor")
+        self.nd, self.nt = own_all.shape[0], every.shape[0]
+        self.core, self.low = self.d % 2, self.t % 2
+        self.wide = shared.shape[1] // 2
+        self.narrow = self.wide // 2
+
+    def first(self):
+        away = pl.ds(pl.multiple_of((1 - self.core) * self.wide, self.wide), self.wide)
+        return remote(self.shared.at[:, away], self.half_in, self.s1, self.r1, self.at["core"])
+
+    def second(self):
+        away = pl.ds(pl.multiple_of((1 - self.low) * self.narrow, self.narrow), self.narrow)
+        return remote(self.half.at[:, away], self.quarter_in, self.s2, self.r2, self.at["near"])
+
+    def third(self):
+        return (
+            remote(self.own, self.own_home, self.s3.at[0], self.r3.at[0], self.at["cross"]),
+            remote(self.quarter, self.quarter_home, self.s3.at[1], self.r3.at[1], self.at["cross"]),
+        )
+
+    def fourth(self, k):
+        peer = (lax.rem(self.d + k, self.nd), self.t)
+        return (
+            remote(self.own_home, self.own_all.at[self.d], self.s4.at[0, k], self.r4.at[0, k], peer),
+            remote(self.quarter_home, self.quarter_all.at[self.d], self.s4.at[1, k], self.r4.at[1, k], peer),
+        )
+
+    def stay(self):
+        return (
+            pltpu.make_async_copy(self.own_home, self.own_all.at[self.d], self.keep.at[0]),
+            pltpu.make_async_copy(self.quarter_home, self.quarter_all.at[self.d], self.keep.at[1]),
+        )
+
+    def share_of(self, core):
+        return pl.ds(core * (self.nd // 2), self.nd // 2)
+
+    def fifth(self, k):
+        peer = (self.d, lax.rem(self.t + k, self.nt))
+        slots = self.share_of(self.core)
+        return remote(
+            self.quarter_all.at[slots], self.every.at[self.t, slots], self.s5.at[k], self.r5.at[k], peer
+        )
+
+    def sixth(self, k):
+        block = self.every.at[lax.rem(self.t + k, self.nt), self.share_of(self.core)]
+        return remote(block, block, self.s6.at[k], self.r6.at[k], self.at["core"])
+
+    def stay_every(self):
+        return pltpu.make_async_copy(self.quarter_all, self.every.at[self.t], self.keep.at[2])
+
+    def peers(self, act):
+        def body(k, carry):
+            for copy in self.fourth(k):
+                act(copy)
+            return carry
+
+        lax.fori_loop(1, self.nd, body, 0)
+
+    def hop1(self):
+        self.first().start()
+
+    def hop2(self):
+        self.first().wait_recv()
+        mine = pl.ds(pl.multiple_of(self.core * self.wide, self.wide), self.wide)
+        self.half[...] = (self.shared[:, mine].astype(F32) + self.half_in[...].astype(F32)).astype(BF16)
+        self.second().start()
+
+    def hop3(self):
+        self.second().wait_recv()
+        mine = pl.ds(pl.multiple_of(self.low * self.narrow, self.narrow), self.narrow)
+        self.quarter[...] = (self.half[:, mine].astype(F32) + self.quarter_in[...].astype(F32)).astype(BF16)
+
+        @pl.when(self.at["moved"])
+        def _():
+            for copy in self.third():
+                copy.start()
+
+        @pl.when(jnp.logical_not(self.at["moved"]))
+        def _():
+            self.own_home[...] = self.own[...]
+            self.quarter_home[...] = self.quarter[...]
+
+    def hop4(self):
+        @pl.when(self.at["moved"])
+        def _():
+            for copy in self.third():
+                copy.wait_recv()
+
+        for copy in self.stay():
+            copy.start()
+        self.peers(lambda copy: copy.start())
+
+    def hop5(self):
+        self.peers(lambda copy: copy.wait_recv())
+        for copy in self.stay():
+            copy.wait()
+        self.stay_every().start()
+        for k in range(1, self.nt):
+            self.fifth(k).start()
+
+    def hop6(self):
+        for k in range(1, self.nt):
+            self.fifth(self.nt - k).wait_recv()
+            self.sixth(k).start()
+
+    def finish(self):
+        self.first().wait_send()
+        self.second().wait_send()
+
+        @pl.when(self.at["moved"])
+        def _():
+            for copy in self.third():
+                copy.wait_send()
+
+        self.peers(lambda copy: copy.wait_send())
+        self.stay_every().wait()
+        for k in range(1, self.nt):
+            self.fifth(k).wait_send()
+            self.sixth(k).wait()
+
+
+def tables_scratch(nd, rank, own, count, width):
+    rows = count * rank
+    return (
+        [
+            VM((rank, own), BF16), VM((rows, width), BF16), VM((rank, own), BF16), VM((rows, width // 4), BF16),
+            VM((nd, rows, width // 4), BF16),
+            VM((rows, width // 2), BF16), VM((rows, width // 2), BF16), VM((rows, width // 4), BF16),
+            VM((rows, width // 4), BF16),
+        ],
+        [pltpu.SemaphoreType.DMA] * 4 + sems(2) + sems(2, nd) + sems(4) + sems(4) + [pltpu.SemaphoreType.DMA((3,))],
     )
+
+
+def back_kernel(
+    gmid, mlp_part, x, w3, wqkv, wo, wo_role, cot, mid, tok, gains, dbias, proj, ctx, lse, rank_qkv, rank_out,
+    small, chosen, nums, tuo, tdi, tui, tdo, ids,
+    out, in_grad, own_early, every_early, own_late, every_late, all_ids,
+    work, kept, gm, grad, gctx, gproj, dist, kt, gk, gv, wv, wov, side, far, mix, side2, far2, mix2, done, done2,
+    *rest,
+):
+    early_buffers, late_buffers = rest[:9], rest[9:18]
+    early_sems, late_sems = rest[18:31], rest[31:44]
+    rs, rr, ms, mr, ls, lr, gs, gr, os, orr, bs, br, ns, nr, load = rest[44:]
+    at = places()
+    moved = at["moved"]
+    still = jnp.logical_not(moved)
+    d, t = lax.axis_index("dp"), lax.axis_index("tensor")
+    nd, nt = own_early.shape[0], every_early.shape[0]
+    barrier = pltpu.get_barrier_semaphore()
+
+    def hail(k, carry):
+        pl.semaphore_signal(barrier, inc=1, device_id=(lax.rem(d + k, nd), t), device_id_type=MESH)
+        return carry
+
+    lax.fori_loop(1, nd, hail, 0)
+    for k in range(1, nt):
+        pl.semaphore_signal(barrier, inc=1, device_id=(d, lax.rem(t + k, nt)), device_id_type=MESH)
+
+    @pl.when(moved)
+    def _():
+        pl.semaphore_signal(barrier, inc=1, device_id=at["cross"], device_id_type=MESH)
+
+    pl.semaphore_wait(barrier, nd - 1 + nt - 1 + moved.astype(jnp.int32))
+
+    rows = tok.shape[0]
+    step = rows // CHUNKS
+    cols = ctx.shape[1]
+    rank = small.shape[0]
+    heads = cols // HEAD_DIM
+    scale = 1.0 / math.sqrt(HEAD_DIM)
+    get_work = pltpu.make_async_copy(gmid, work, load.at[0])
+    get_work.start()
+    get_kept = [
+        pltpu.make_async_copy(mlp_part.at[pl.ds(2 * j * rows, rows)], kept.at[pl.ds(j * rows, rows)], load.at[1 + j])
+        for j in range(2)
+    ]
+    for copy in get_kept:
+        copy.start()
+    fetch(wo, wo_role, wov, load.at[3])
+    all_ids[d] = ids[...]
+
+    def number(k):
+        return remote(ids, all_ids.at[d], ns.at[k], nr.at[k], (lax.rem(d + k, nd), t))
+
+    def send_number(k, carry):
+        number(k).start()
+        return carry
+
+    def await_number(k, carry):
+        number(k).wait()
+        return carry
+
+    get_work.wait()
+    total = Gathered(at, work, side, far, mix, rs, rr)
+    spread = Spread(at, gm, gs, gr)
+    total.begin()
+    own, shared, own_home, quarter_home, quarter_all = early_buffers[:5]
+    wide = tuo.shape[1]
+    own[:, :wide] = tuo[...].astype(BF16)
+    own[:, wide:] = tdi[...].astype(BF16)
+    shared[0:rank] = tui[...].astype(BF16)
+    shared[rank : 2 * rank] = tdo[...].astype(BF16)
+    early = Tables(
+        at, own, shared, own_home, quarter_home, own_early, quarter_all, every_early, early_buffers[5:], early_sems
+    )
+    early.hop1()
+    lax.fori_loop(1, nd, send_number, 0)
+    for i in range(CHUNKS):
+        here = slice(i * step, (i + 1) * step)
+        unit, inverse = unit_rows(mid[here])
+        value = cot[here].astype(F32) + unit_back(total.take(i), unit, inverse, gains[1:2])
+        grad[here] = value
+        gm[here] = value.astype(BF16)
+        spread.post(i)
+    early.hop2()
+    for i in range(CHUNKS):
+        spread.forward(i)
+    early.hop3()
+    spread.finish()
+    total.finish()
+
+    for copy in get_kept:
+        copy.wait()
+    mlp = Gathered(at, mlp_part, side, far, mix, ms, mr, kept)
+    mlp.send_away()
+    mlp.send_home()
+    pltpu.make_async_copy(wo, wov, load.at[3]).wait()
+    bq, ao = small[:, : 3 * cols], small[:, 3 * cols : 4 * cols]
+    aq, bo = chosen[0:rank], chosen[rank : 2 * rank]
+
+    def context_rows(i, sums):
+        here = pl.ds(i * rows, rows)
+        g = gm[here]
+        r = dot_t(g, bo).astype(BF16)
+        gctx[here] = (dot_t(g, wov[...]) + dot(r, ao)).astype(BF16)
+        return sums[0] + t_dot(rank_out[here], g), sums[1] + t_dot(r, ctx[here])
+
+    sums = (jnp.zeros((rank, gm.shape[1]), F32), jnp.zeros((rank, cols), F32))
+    sums = context_rows(0, sums)
+    mlp.send_over()
+    early.hop4()
+    for i in range(1, 4):
+        sums = context_rows(i, sums)
+    early.hop5()
+    context_sums = sums
+    get_x = pltpu.make_async_copy(x, gm, load.at[4])
+    get_x.start()
+    for j in range(3):
+        fetch(w3.at[j], wqkv.at[j], wv.at[j], load.at[5 + j])
+
+    me = 2 * (d % 2) + t % 2
+    base = nums.shape[1] - 128
+    slopes = head_slopes(me, heads)
+    kt[...] = proj[:, cols : 2 * cols].T
+    gk[...] = jnp.zeros_like(gk)
+    gv[...] = jnp.zeros_like(gv)
+
+    def attend_step(i, carry):
+        here = pl.ds(pl.multiple_of(i * rows, rows), rows)
+        distances(me, nums[0:1, base : base + 1], nums[0:1, base + 1 : base + 2], rows, i, dist)
+        for h in range(heads):
+            span = slice(h * HEAD_DIM, (h + 1) * HEAD_DIM)
+            q, g = proj[here, span], gctx[here, span]
+            keys = proj[:, cols + h * HEAD_DIM : cols + (h + 1) * HEAD_DIM]
+            values = proj[:, 2 * cols + h * HEAD_DIM : 2 * cols + (h + 1) * HEAD_DIM]
+            s = dot_t(keys, q) * (scale * LOG2E) - dist[...] * slopes[h]
+            p = jnp.exp2(s - lse[h : h + 1, here])
+            gv[:, span] += dot(p.astype(BF16), g)
+            gp = dot_t(values, g)
+            inner = jnp.sum(p * gp, axis=0, keepdims=True)
+            gsc = (p * (gp - inner)).astype(BF16)
+            gk[:, span] += dot(gsc, q)
+            gproj[here, span] = (dot(kt[span, :], gsc).T * scale).astype(BF16)
+        return carry
+
+    lax.fori_loop(0, 2, attend_step, 0)
+    early.hop6()
+    lax.fori_loop(2, 4, attend_step, 0)
+    gproj[:, cols : 2 * cols] = (gk[...] * scale).astype(BF16)
+    gproj[:, 2 * cols :] = gv[...].astype(BF16)
+
+    def out_back(i):
+        here = pl.ds(i * step, step)
+        return remote(done.at[here], out.at[here], os.at[i], orr.at[i], at["cross"])
+
+    def grad_back(i):
+        here = pl.ds(i * step, step)
+        return remote(done2.at[here], in_grad.at[here], bs.at[i], br.at[i], at["cross"])
+
+    for i in range(CHUNKS):
+        here = slice(i * step, (i + 1) * step)
+        value = (mid[here] + (mlp.take(i) + dbias[...])).astype(BF16)
+
+        @pl.when(moved)
+        def _():
+            done[here] = value
+            out_back(i).start()
+
+        @pl.when(still)
+        def _():
+            out[here] = value
+
+    get_x.wait()
+    for j in range(3):
+        pltpu.make_async_copy(w3.at[j], wv.at[j], load.at[5 + j]).wait()
+    own, shared, own_home, quarter_home, quarter_all = late_buffers[:5]
+
+    def input_rows(i, sums):
+        here = pl.ds(i * rows, rows)
+        g = gproj[here]
+        r = dot_t(g, bq).astype(BF16)
+        acc = dot(r, aq)
+        for j in range(3):
+            acc = acc + dot_t(g[:, j * cols : (j + 1) * cols], wv[j])
+        work[here] = acc.astype(BF16)
+        return sums[0] + t_dot(rank_qkv[here], g), sums[1] + t_dot(r, gm[here])
+
+    last = Gathered(at, work, side2, far2, mix2, ls, lr)
+    sums = (jnp.zeros((rank, 3 * cols), F32), jnp.zeros((rank, gm.shape[1]), F32))
+    sums = input_rows(3, sums)
+    last.send_away()
+    sums = input_rows(1, sums)
+    last.send_home()
+    sums = input_rows(2, sums)
+    last.send_over()
+    sums = input_rows(0, sums)
+    own[:, : 3 * cols] = sums[0].astype(BF16)
+    own[:, 3 * cols :] = context_sums[1].astype(BF16)
+    shared[0:rank] = sums[1].astype(BF16)
+    shared[rank : 2 * rank] = context_sums[0].astype(BF16)
+    late = Tables(at, own, shared, own_home, quarter_home, own_late, quarter_all, every_late, late_buffers[5:], late_sems)
+    late.hop1()
+    hops = (late.hop2, late.hop3, late.hop4, late.hop5)
+    for i in range(CHUNKS):
+        here = slice(i * step, (i + 1) * step)
+        unit, inverse = unit_rows(tok[here].astype(F32))
+        value = (grad[here] + unit_back(last.take(i), unit, inverse, gains[0:1])).astype(BF16)
+
+        @pl.when(moved)
+        def _():
+            done2[here] = value
+            grad_back(i).start()
+
+        @pl.when(still)
+        def _():
+            in_grad[here] = value
+
+        hops[i]()
+    late.hop6()
+    lax.fori_loop(1, nd, await_number, 0)
+    mlp.finish()
+    last.finish()
+    early.finish()
+    late.finish()
+
+    @pl.when(moved)
+    def _():
+        for i in range(CHUNKS):
+            out_back(i).wait()
+            grad_back(i).wait()
+
+
+def back(nd, nt, gmid, mlp_part, x, w3, wqkv, wo, wo_role, cot, mid, tok, gains, dbias, proj, ctx, lse, rank_qkv,
+         rank_out, small, chosen, nums, tuo, tdi, tui, tdo, ids):
+    rows, width = tok.shape
+    n = 4 * rows
+    cols = ctx.shape[1]
+    rank = small.shape[0]
+    early_own = 2 * tuo.shape[1]
+    low = lambda *s: jax.ShapeDtypeStruct(s, BF16)
+    early = tables_scratch(nd, rank, early_own, 2, width)
+    late = tables_scratch(nd, rank, 4 * cols, 2, width)
+    return pl.pallas_call(
+        back_kernel,
+        in_specs=[ANY_SPEC] * 7 + [VMEM_SPEC] * 18,
+        out_specs=[VMEM_SPEC] * 2 + [ANY_SPEC] * 4 + [VMEM_SPEC],
+        out_shape=[
+            low(rows, width), low(rows, width),
+            low(nd, rank, early_own), low(nt, nd, 2 * rank, width // 4),
+            low(nd, rank, 4 * cols), low(nt, nd, 2 * rank, width // 4),
+            jax.ShapeDtypeStruct((nd,) + ids.shape, jnp.int32),
+        ],
+        scratch_shapes=[
+            VM((n, width), BF16), VM((2 * rows, width), BF16), VM((n, width), BF16), VM((rows, width), F32),
+            VM((n, cols), BF16), VM((n, 3 * cols), BF16), VM((n, rows), F32), VM((cols, n), BF16),
+            VM((n, cols), F32), VM((n, cols), F32), VM(w3.shape, BF16), VM(wo.shape, BF16),
+            VM((2 * rows, width), BF16), VM((rows, width), BF16), VM((rows, width), BF16),
+            VM((2 * rows, width), BF16), VM((rows, width), BF16), VM((rows, width), BF16),
+            VM((rows, width), BF16), VM((rows, width), BF16),
+        ]
+        + early[0] + late[0] + early[1] + late[1]
+        + sems(3, CHUNKS) * 4 + sems(CHUNKS) * 2 + sems(nd) + [pltpu.SemaphoreType.DMA((8,))],
+        compiler_params=comm_params(2, 62),
+        name="back",
+    )(gmid, mlp_part, x, w3, wqkv, wo, wo_role, cot, mid, tok, gains, dbias, proj, ctx, lse, rank_qkv, rank_out,
+      small, chosen, nums, tuo, tdi, tui, tdo, ids)
+
+
+def combine_kernel(ids, own_early, every_early, own_late, every_late, gqi, gqo, goi, goo, gui, guo, gdi, gdo):
+    nd = own_early.shape[0]
+    cols = goi.shape[2]
+    wide = guo.shape[2]
+    rank = goi.shape[1]
+    quarter = every_late.shape[3]
+    for ref in (gqi, gqo, goi, goo, gui, guo, gdi, gdo):
+        ref[...] = jnp.zeros_like(ref)
+
+    def add(s, carry):
+        e = [ids[s, 0, k] for k in range(4)]
+        for j in range(3):
+            gqo[e[0], j] += own_late[s, :, j * cols : (j + 1) * cols].astype(F32)
+        goi[e[1]] += own_late[s, :, 3 * cols :].astype(F32)
+        guo[e[2]] += own_early[s, :, :wide].astype(F32)
+        gdi[e[3]] += own_early[s, :, wide:].astype(F32)
+        for z in range(every_late.shape[0]):
+            at = slice(z * quarter, (z + 1) * quarter)
+            gqi[e[0], :, at] += every_late[z, s, 0:rank].astype(F32)
+            goo[e[1], :, at] += every_late[z, s, rank:].astype(F32)
+            gui[e[2], :, at] += every_early[z, s, 0:rank].astype(F32)
+            gdo[e[3], :, at] += every_early[z, s, rank:].astype(F32)
+        return carry
+
+    lax.fori_loop(0, nd, add, 0)
+
+
+def combine(ids, own_early, every_early, own_late, every_late, tables, cols, wide):
+    rank = own_early.shape[1]
+    width = every_late.shape[0] * every_late.shape[3]
+    high = lambda *s: jax.ShapeDtypeStruct(s, F32)
+    full = high(tables, rank, width)
+    return pl.pallas_call(
+        combine_kernel,
+        in_specs=[pl.BlockSpec(memory_space=pltpu.SMEM)] + [VMEM_SPEC] * 4,
+        out_specs=[VMEM_SPEC] * 8,
+        out_shape=[
+            full, high(tables, 3, rank, cols), high(tables, rank, cols), full, full, high(tables, rank, wide),
+            high(tables, rank, wide), full,
+        ],
+        compiler_params=params(48),
+        name="combine",
+    )(ids, own_early, every_early, own_late, every_late)
 
 
 def body(
@@ -976,21 +1173,10 @@
     adapter_down_output, offsets, adapter_ids,
 ):
     nd, nt = lax.axis_size("dp"), lax.axis_size("tensor")
-    route = routes(nd, nt)
-    d, t = lax.axis_index("dp"), lax.axis_index("tensor")
-    c, p = d % 2, (d // 2) % 4
-    moved = c != t // 2
-    me = 2 * c + t % 2
     rows, width = tokens.shape
-    length = rows * nt
     local = output_weight.shape[0]
-    local_heads = local // HEAD_DIM
     hidden_width = up_weight.shape[1]
-    rank = adapter_up_input.shape[1]
     tables = adapter_up_input.shape[0]
-
-    def go(x, name):
-        return lax.ppermute(x, AXES, route[name])
 
     w3 = jnp.transpose(query_key_value_weight, (1, 0, 2))
     b3 = jnp.transpose(qkv_out, (0, 2, 1, 3))
@@ -1006,57 +1192,18 @@
         adapter_ids[0], tokens, numbers, tables_in, norm_gains, norm_shifts, output_bias_vector.reshape(1, width),
         w3, output_weight, up_weight, down_weight, cotangent,
     )
-    cuts = [3 * local, 4 * local, 4 * local + hidden_width]
-    gain = [norm_gains[i : i + 1] for i in range(2)]
-
-    def scatter(home, away):
-        far = (away[:rows].astype(F32) + go(away[rows:], "core").astype(F32)).astype(BF16)
-        far = go(far, "near")
-        side = go(home[rows:], "core")
-        return home[:rows].astype(F32) + side.astype(F32) + far.astype(F32)
-
-    part, back, t_up_out, t_down_in, t_up_in, t_down_out = mlp(
+    part, gmid, t_up_out, t_down_in, t_up_in, t_down_out = mlp(
         nm, cot, up_weight, wu, down_weight, wd, chosen, small, nums, hidden_width // 4
     )
-    cot_own = cot[:rows]
-    gm, grad_middle = turn_rows(back, cot_own, middle, gain[1])
-    result = (middle + (scatter(part[: 2 * rows], part[2 * rows :]) + down_bias_vector)).astype(BF16)
-    grad_ctx, t_out_out, t_out_in = bwd_o(gm, output_weight, wo, chosen, small, rank_out, ctx, rows)
-    grad_proj = attend_back(nums, proj, grad_ctx, lse, rows)
-    gx, t_qkv_out, t_qkv_in = bwd_qkv(grad_proj, w3, wqkv, small, chosen, rank_qkv, x, rows)
-    in_grad = leave(gx, tok, grad_middle, gain[0])
-
-    result = go(result, "swap")
-
-    def owned(pieces):
-        return lax.all_gather(go(jnp.concatenate(pieces, 1).astype(BF16), "swap"), "dp", axis=0)
-
-    everyone = lax.all_gather(adapter_ids, "dp", axis=0, tiled=True)
-    hot = (everyone[:, :, None] == jnp.arange(tables, dtype=jnp.int32)).astype(BF16)
-
-    def combine(per, which):
-        return jnp.einsum("se,srm->erm", hot[:, which], per, preferred_element_type=F32)
-
-    own = owned([t[:rank] for t in (t_qkv_out, t_out_in, t_up_out, t_down_in)])
-    g_qkv_out = jnp.einsum(
-        "se,srkm->erkm", hot[:, 0], own[:, :, : cuts[0]].reshape(nd, rank, 3, local), preferred_element_type=F32
+    result, in_grad, own_early, every_early, own_late, every_late, everyone = back(
+        nd, nt, gmid, part, x, w3, wqkv, output_weight, wo, cot[:rows], middle, tok, norm_gains,
+        down_bias_vector.reshape(1, width), proj, ctx, lse, rank_qkv, rank_out, small, chosen, nums,
+        t_up_out, t_down_in, t_up_in, t_down_out, jnp.pad(adapter_ids, ((0, 0), (0, 124))),
     )
-    g_out_in = combine(own[:, :, cuts[0] : cuts[1]], 1)
-    g_up_out = combine(own[:, :, cuts[1] : cuts[2]], 2)
-    g_down_in = combine(own[:, :, cuts[2] :], 3)
-
-    shared = jnp.stack([t[:rank] for t in (t_qkv_in, t_out_out, t_up_in, t_down_out)]).astype(BF16)
-    shared = shared.astype(F32) + go(shared, "core").astype(F32)
-    shared = (shared + go(shared.astype(BF16), "near").astype(F32)).astype(BF16)
-    quarter = width // 4
-    mine = lax.dynamic_slice_in_dim(shared, me * quarter, quarter, 2)
-    mine = go(mine, "swap")
-    mine = lax.all_gather(mine, "dp", axis=0)
-    sums = jnp.einsum("ske,skrm->kerm", hot.transpose(0, 1, 2), mine, preferred_element_type=F32)
-    whole = lax.all_gather(sums.astype(BF16), "tensor", axis=3, tiled=True).astype(F32)
-    return (
-        result, in_grad, whole[0], g_qkv_out, g_out_in, whole[1], whole[2], g_up_out, g_down_in, whole[3],
+    gqi, gqo, goi, goo, gui, guo, gdi, gdo = combine(
+        everyone, own_early, every_early, own_late, every_late, tables, local, hidden_width
     )
+    return (result, in_grad, gqi, jnp.transpose(gqo, (0, 2, 1, 3)), goi, goo, gui, guo, gdi, gdo)
 
 
 def solution(mesh):

time: 627 us -> 504 us (0.80)
  waiting for transfers between devices: 29 us -> 0 us
  local copies, waits for them, and re-layouts: 36 us -> 10.8 us
  blocking collectives: 17.9 us -> 0 us
  between operations: 14.6 us -> 0.92 us
  other arithmetic: 14.1 us -> 2.05 us
  starting transfers between devices: 12 us -> 0 us
  Pallas kernels: 495 us -> 486 us
    ppermute x8 -> x0, waiting for transfers between devices: 28.9 us -> none  [go(): return lax.ppermute(x, AXES, route[name])]
    unnamed x43 -> x19, local copies, waits for them, and re-layouts: 26.9 us -> 8.03 us
    all_gather x2 -> x0, blocking collectives: 17.9 us -> none  [the longest x1 9.85 us: body(): mine = lax.all_gather(mine, 'dp', axis=0)]
    ppermute x8 -> x0, starting transfers between devices: 11.9 us -> none  [go(): return lax.ppermute(x, AXES, route[name])]
    convert_element_type x5 -> x0, other arithmetic: 10 us -> none  [the longest x1 3.53 us: body(): (middle + (scatter(part[:2 * rows], part[2 * rows:]) + down_bias_vector))...]
    pallas_call x5 -> x2, Pallas kernels: 190 us -> 186 us  [the longest x1 181 us: back(): pl.pallas_call(back_kernel, in_specs=[ANY_SPEC] * 7 + [VMEM_SPEC] * 18, o...]
  transfers between devices with their start and end apart: 10 -> 0, of which waited for: 3 -> 0; matrix products, arithmetic and copies ran while one was open for 4% -> 0% of each run, Pallas kernels for 14% -> 0%
where the time goes in v3:
time: 504 us; the launch traced here: 500 us
  Pallas kernels  486 us (96%)
  local copies, waits for them, and re-layouts  10.8 us (2%)
    pallas_call x1, Pallas kernels, front(): pl.pallas_call(front_kernel, in_specs=[pl.BlockSpec(memory_space=pltpu.SM...  244 us
    pallas_call x1, Pallas kernels, back(): pl.pallas_call(back_kernel, in_specs=[ANY_SPEC] * 7 + [VMEM_SPEC] * 18, o...  181 us
    pallas_call x1, Pallas kernels, mlp(): pl.pallas_call(mlp_kernel, grid=(hidden // tile, 2), in_specs=[row, row,...  56 us

profile of v3, /device:TPU:1, one launch (start us, length us, event | category | flops | bytes accessed | tf_op | source)
XLA Modules:
  0.0 499.8 jit_solution(15452313218067516263)
XLA Ops:
  0.6 0.7 copy.32
  1.3 0.7 add_convert_fusion
  2.1 1.3 fusion.numbers
  3.4 244.3 %front.1 = (bf16[1024,2048]{1,0:T(8,128)(2,1)}, bf16[256,2048]{1,0:T(8,128)(2,1)}, bf16[16,6144]{1,0:T(8,128)(2,1)}, f32[1,3200]{1,0:T(1,128)}, bf16[64,2048]{1,...) custom-call(s32[4]{0:T(128)} %bitcast.18, ...), custom_call_target="tpu_custom_call" | custom-call | tf_op jit(solution)/shard_map/front/pallas_call | solution.py:697
  247.7 0.0 copy-start.7
  247.7 56.0 %mlp.1 = (bf16[1024,2048]{1,0:T(8,128)(2,1)}, bf16[1024,2048]{1,0:T(8,128)(2,1)}, f32[16,2048]{1,0:T(8,128)}, f32[16,2048]{1,0:T(8,128)}, f32[16,2048]{1,0:T(8,128)}, /*index=5*/f32[16,2048]{1,0:T(8,128)}) custom-call(bf16[1024,2048]{1,0:T(8,128)(2,1)} %get-tuple-element.48.nm, bf16[1024,2048]{1,0:T(8,128)(2,1)} %get-tuple-element.49.cot, ...), custom_call_target="tpu_custom_call" | custom-call | flops 34359738368 | bytes 41943040 | tf_op jit(solution)/shard_map/mlp/pallas_call | solution.py:200
  303.7 2.3 slice.3.cot
  306.0 0.0 copy-done.7
  306.0 0.5 pad.9.ids
  306.5 181.0 %back.1 = (bf16[256,2048]{1,0:T(8,128)(2,1)}, bf16[256,2048]{1,0:T(8,128)(2,1)}, bf16[8,16,4096]{2,1,0:T(8,128)(2,1)}, bf16[4,8,32,512]{3,2,1,0:T(8,128)(2,1)}, ...) custom-call(bf16[1024,2048]{1,0:T(8,128)(2,1)} %get-tuple-element.55.gmid, ...), custom_call_target="tpu_custom_call" | custom-call | tf_op jit(solution)/shard_map/back/pallas_call | solution.py:1098
  487.5 0.0 copy-start
  487.6 1.2 copy-done
  488.8 0.0 copy-start.1
  488.8 1.2 copy-done.1
  490.0 0.0 copy-start.2
  490.0 1.2 copy-done.2
  491.2 0.0 copy-start.3
  491.2 1.0 copy-done.3
  492.3 0.0 copy-start.4
  492.3 0.7 copy-done.4
  492.9 0.0 copy-start.6
  492.9 0.0 copy-start.5
  492.9 4.7 combine.1
  497.6 0.0 copy-done.6
  497.6 1.0 copy.35
  498.6 0.0 copy-done.5
  498.6 1.0 copy.36
Async XLA Ops:
  247.7 58.3 %copy-start.7 = (s32[1,4]{1,0:T(1,128)S(1)}, s32[1,4]{1,0:T(1,128)}, u32[]{:S(2)}) copy-start(s32[1,4]{1,0:T(1,128)} %param.43) | copy-start | bytes 52
  487.5 1.2 copy-start
  488.8 1.2 copy-start.1
  490.0 1.2 copy-start.2
  491.2 1.0 copy-start.3
  492.3 0.7 copy-start.4
  492.9 4.7 copy-start.6
  492.9 5.7 %copy-start.5 = (bf16[256,2048]{1,0:T(8,128)(2,1)S(1)}, bf16[256,2048]{1,0:T(8,128)(2,1)}, u32[]{:S(2)}) copy-start(bf16[256,2048]{1,0:T(8,128)(2,1)} %get-tuple-element.97) | copy-start | bytes 3145732

commit v4 on v3

--- a/solution.py
+++ b/solution.py
@@ -96,136 +96,6 @@
     half = 0.5 * (1.0 + tangent)
     slope = half + (0.5 * GELU_C) * values * (1.0 - tangent * tangent) * (1.0 + 3.0 * GELU_K * square)
     return values * half, slope
-
-
-def mlp_kernel(
-    nm, cot, wu_native, wu_brought, wd_native, wd_brought, au, bu, ad, bd, bias, part, back, tuo, tdi, tui, tdo,
-    up_rank, down_rank, g_up, g_down, acc, gacc, wu_slots, wd_slots, sem,
-):
-    step, half = pl.program_id(0), pl.program_id(1)
-    last = pl.num_programs(0) - 1
-    rows = nm.shape[0]
-    tile = bu.shape[1]
-
-    def load(j):
-        slot = j % 2
-        cut = pl.ds(pl.multiple_of(j * tile, tile), tile)
-        return (
-            fetch(wu_native.at[:, cut], wu_brought.at[:, cut], wu_slots.at[slot], sem.at[0, slot]),
-            fetch(wd_native.at[cut], wd_brought.at[cut], wd_slots.at[slot], sem.at[1, slot]),
-        )
-
-    def await_slot(slot):
-        pltpu.make_async_copy(wu_native.at[:, pl.ds(0, tile)], wu_slots.at[slot], sem.at[0, slot]).wait()
-        pltpu.make_async_copy(wd_native.at[pl.ds(0, tile)], wd_slots.at[slot], sem.at[1, slot]).wait()
-
-    @pl.when((step == 0) & (half == 0))
-    def _():
-        load(step)
-
-    @pl.when(half == 0)
-    def _():
-        await_slot(step % 2)
-
-        @pl.when(step < last)
-        def _():
-            load(step + 1)
-
-    wu = wu_slots.at[step % 2]
-    wd = wd_slots.at[step % 2]
-    here = pl.ds(pl.multiple_of(half * rows, rows), rows)
-
-    @pl.when(step == 0)
-    def _():
-        up_rank[here] = dot_t(nm[...], au[...]).astype(BF16)
-        g_down[here] = dot_t(cot[...], bd[...]).astype(BF16)
-        down_rank[here] = jnp.zeros((rows, au.shape[0]), F32)
-        g_up[here] = jnp.zeros((rows, au.shape[0]), F32)
-        acc[here] = jnp.zeros((rows, nm.shape[1]), F32)
-        gacc[here] = jnp.zeros((rows, nm.shape[1]), F32)
-
-    gate = dot(nm[...], wu[...]) + dot(up_rank[here], bu[...]) + bias[...]
-    value, slope = gelu_parts(gate)
-    hidden = value.astype(BF16)
-    grad = dot_t(cot[...], wd[...]) + dot(g_down[here], ad[...])
-    grad_gate = (grad * slope).astype(BF16)
-    down_rank[here] += dot_t(hidden, ad[...])
-    g_up[here] += dot_t(grad_gate, bu[...])
-    acc[here] += dot(hidden, wd[...])
-    gacc[here] += dot_t(grad_gate, wu[...])
-    one = t_dot(up_rank[here], grad_gate)
-    two = t_dot(g_down[here], hidden)
-
-    @pl.when(half == 0)
-    def _():
-        tuo[...] = one
-        tdi[...] = two
-
-    @pl.when(half > 0)
-    def _():
-        tuo[...] += one
-        tdi[...] += two
-
-    @pl.when(step == last)
-    def _():
-        dr = down_rank[here].astype(BF16)
-        gu = g_up[here].astype(BF16)
-        part[...] = (acc[here] + dot(dr, bd[...])).astype(BF16)
-        back[...] = (gacc[here] + dot(gu, au[...])).astype(BF16)
-        three = t_dot(gu, nm[...])
-        four = t_dot(dr, cot[...])
-
-        @pl.when(half == 0)
-        def _():
-            tui[...] = three
-            tdo[...] = four
-
-        @pl.when(half > 0)
-        def _():
-            tui[...] += three
-            tdo[...] += four
-
-
-def mlp(nm, cot, wu, wu_brought, wd, wd_brought, chosen, small, nums, tile):
-    n, width = nm.shape
-    rows = n // 2
-    hidden = wu.shape[1]
-    last = hidden // tile - 1
-    low = small.shape[0]
-    first = (small.shape[1] - 2 * hidden) // tile
-    bias_first = (nums.shape[1] - 128 - hidden) // tile
-    cut = lambda r: pl.BlockSpec((r, tile), lambda j, i: (0, j))
-    row = pl.BlockSpec((rows, width), lambda j, i: (i, 0))
-    result = pl.BlockSpec((rows, width), lambda j, i: (jnp.where(j == last, i, 0), 0))
-    return pl.pallas_call(
-        mlp_kernel,
-        grid=(hidden // tile, 2),
-        in_specs=[
-            row, row, HERE, HERE, HERE, HERE,
-            pl.BlockSpec((low, width), lambda j, i: (2, 0)),
-            pl.BlockSpec((low, tile), lambda j, i: (0, first + j)),
-            pl.BlockSpec((low, tile), lambda j, i: (0, first + hidden // tile + j)),
-            pl.BlockSpec((low, width), lambda j, i: (3, 0)),
-            pl.BlockSpec((1, tile), lambda j, i: (0, bias_first + j)),
-        ],
-        out_specs=[result, result, cut(low), cut(low), whole((low, width)), whole((low, width))],
-        out_shape=[
-            jax.ShapeDtypeStruct((n, width), BF16),
-            jax.ShapeDtypeStruct((n, width), BF16),
-            jax.ShapeDtypeStruct((low, hidden), F32),
-            jax.ShapeDtypeStruct((low, hidden), F32),
-            jax.ShapeDtypeStruct((low, width), F32),
-            jax.ShapeDtypeStruct((low, width), F32),
-        ],
-        scratch_shapes=[
-            VM((n, low), BF16), VM((n, low), F32), VM((n, low), F32), VM((n, low), BF16),
-            VM((n, width), F32), VM((n, width), F32),
-            VM((2, width, tile), BF16), VM((2, tile, width), BF16), pltpu.SemaphoreType.DMA((2, 2)),
-        ],
-        compiler_params=params(60),
-        cost_estimate=cost(8 * n * width * hidden, 4 * width * hidden + 12 * n * width),
-        name="mlp",
-    )(nm, cot, wu, wu_brought, wd, wd_brought, chosen, small, small, chosen, nums)
 
 
 MESH = pl.DeviceIdType.MESH
@@ -291,6 +161,7 @@
         self.at, self.full, self.send, self.recv = at, full, send, recv
         self.rows = full.shape[0] // 4
         self.step = self.rows // CHUNKS
+        self.waited = False
 
     def block(self, k, i):
         return self.full.at[pl.ds(k * self.rows + i * self.step, self.step)]
@@ -312,9 +183,16 @@
         self.far(i).wait_recv()
         self.onward(i).start()
 
+    def beside(self):
+        for i in range(CHUNKS):
+            self.side(i).wait_recv()
+        self.waited = True
+
     def finish(self):
         for i in range(CHUNKS):
-            self.side(i).wait()
+            if not self.waited:
+                self.side(i).wait_recv()
+            self.side(i).wait_send()
             self.far(i).wait_send()
             self.onward(i).wait()
 
@@ -439,6 +317,12 @@
                     for j in range(3):
                         self.share(n, j).wait_recv()
 
+    def ready_item(self, n):
+        @pl.when(self.moved)
+        def _():
+            for j in range(3):
+                self.share(n, j).wait_recv()
+
     def finish(self):
         @pl.when(self.moved)
         def _():
@@ -490,8 +374,8 @@
 
 def front_kernel(
     ids, tokens, numbers, t_bq, t_ao, t_bu, t_ad, t_aq, t_bo, t_au, t_bd, norm_gains, norm_shifts, obias,
-    w3, wo, wu, wd, cot,
-    x, tok, small, nums, chosen, proj, lse, ctx, rank_qkv, rank_out, full, mid, cot_full, wqkv, wo_role, wu_role, wd_role,
+    w3, wo, wu, cot,
+    x, tok, small, nums, chosen, proj, lse, ctx, rank_qkv, rank_out, full, mid, cot_full, wqkv, wo_role, wu_role,
     small_own, part, wv, wov, dist, vt, side, far, mix,
     ts, tr, ps, pr, xs, xr, ss, sr, cs, cr, rs, rr, gs, gr, load,
 ):
@@ -507,7 +391,7 @@
     supply = Supply(
         at,
         [(w3.at[j], wqkv.at[j], True, qkv_span) for j in range(3)]
-        + [(wo, wo_role, True, ITEM), (cot, cot_full, False, ITEM), (wu, wu_role, True, ITEM), (wd, wd_role, True, ITEM)],
+        + [(wo, wo_role, True, ITEM), (cot, cot_full, False, ITEM), (wu, wu_role, True, ITEM)],
         xs, xr, ss, sr,
     )
     relay = Relay(at, cot_full, cs, cr)
@@ -586,14 +470,14 @@
         span = slice(j * cols, (j + 1) * cols)
 
         def strip(i, carry):
-            here = pl.ds(pl.multiple_of(i * rows, rows), rows)
+            here = pl.ds(pl.multiple_of(2 * i * rows, 2 * rows), 2 * rows)
             value = dot(x[here], wv[j]) + dot(rank_qkv[here], small[:, span])
             if j != 1:
                 value = value + nums[0:1, (j // 2) * cols : (j // 2 + 1) * cols]
             proj[here, span] = value.astype(BF16)
             return carry
 
-        lax.fori_loop(0, 4, strip, 0)
+        lax.fori_loop(0, 2, strip, 0)
     supply.tick(3)
     me = 2 * (lax.axis_index("dp") % 2) + lax.axis_index("tensor") % 2
     vt[...] = proj[:, 2 * cols :].T
@@ -662,19 +546,16 @@
         unit, _ = unit_rows(value)
         full[here] = (unit * norm_gains[1:2] + norm_shifts[1:2]).astype(BF16)
         spread_mid.post(i)
-        if i % 2 == 1:
-            supply.tick(9 + i // 2)
+        if i == 1:
+            supply.tick(9)
     for i in range(CHUNKS):
         spread_mid.forward(i)
-        if i == 1:
-            supply.tick(11)
-    for n in range(12, len(supply.items)):
+    for n in range(10, len(supply.items)):
         supply.tick(n)
     total.finish()
     spread_mid.finish()
     relay.finish(2)
-    for k in (5, 6):
-        supply.ready(k)
+    supply.ready(5)
     supply.finish()
 
     @pl.when(moved)
@@ -685,23 +566,23 @@
             copy.wait_send()
 
 
-def front(ids, tokens, numbers, tables, norm_gains, norm_shifts, obias, w3, wo, wu, wd, cot):
+def front(ids, tokens, numbers, tables, norm_gains, norm_shifts, obias, w3, wo, wu, cot):
     rows, width = tokens.shape
     n = 4 * rows
     cols = w3.shape[2]
     rank = tables[1].shape[1]
     packed = 4 * cols + 2 * wu.shape[1]
-    items = 3 + (wo.shape[0] + wu.shape[0] + wd.shape[0]) // 4 // ITEM + rows // ITEM
+    items = 3 + (wo.shape[0] + wu.shape[0]) // 4 // ITEM + rows // ITEM
     low = lambda *s: jax.ShapeDtypeStruct(s, BF16)
     high = lambda *s: jax.ShapeDtypeStruct(s, F32)
     return pl.pallas_call(
         front_kernel,
-        in_specs=[pl.BlockSpec(memory_space=pltpu.SMEM)] + [VMEM_SPEC] * 13 + [ANY_SPEC] * 5,
-        out_specs=[VMEM_SPEC] * 12 + [ANY_SPEC] * 5,
+        in_specs=[pl.BlockSpec(memory_space=pltpu.SMEM)] + [VMEM_SPEC] * 13 + [ANY_SPEC] * 4,
+        out_specs=[VMEM_SPEC] * 12 + [ANY_SPEC] * 4,
         out_shape=[
             low(n, width), low(rows, width), low(rank, packed), high(*numbers.shape), low(4 * rank, width),
             low(n, 3 * cols), high(cols // HEAD_DIM, n), low(n, cols), low(n, rank), low(n, rank),
-            low(n, width), high(rows, width), low(n, width), low(*w3.shape), low(*wo.shape), low(*wu.shape), low(*wd.shape),
+            low(n, width), high(rows, width), low(n, width), low(*w3.shape), low(*wo.shape), low(*wu.shape),
         ],
         scratch_shapes=[
             VM((rank, packed), BF16),
@@ -712,21 +593,186 @@
         + sems(3, CHUNKS) + sems(2, 3, CHUNKS) + [pltpu.SemaphoreType.DMA((5,))],
         compiler_params=comm_params(1, 60),
         name="front",
-    )(ids, tokens, numbers, *tables, norm_gains, norm_shifts, obias, w3, wo, wu, wd, cot)
+    )(ids, tokens, numbers, *tables, norm_gains, norm_shifts, obias, w3, wo, wu, cot)
+
+
+def mlp_kernel(
+    nm, cot, wu, wu_role, wd, chosen, small, nums,
+    part, gmid, tuo, tdi, tui, tdo, wd_role,
+    wus, wds, hid, gg, stage, up_rank, g_down, down_rank, g_up,
+    xs, xr, ss, sr, up_sem, down_sem, out_sem,
+):
+    at = places()
+    moved = at["moved"]
+    greet((at["core"], at["near"]), (at["cross"], at["left"], at["up"], at["both"]), moved)
+    supply = Supply(at, [(wd, wd_role, True, ITEM)], xs, xr, ss, sr)
+
+    @pl.when(moved)
+    def _():
+        supply.begin(1)
+
+    n = nm.shape[0]
+    rank = small.shape[0]
+    count, tile = wus.shape[0], wus.shape[2]
+    hidden = count * tile
+    lines = tile // ITEM
+    rows = n // 2
+    au, bd = chosen[2 * rank : 3 * rank], chosen[3 * rank :]
+    bu_at = small.shape[1] - 2 * hidden
+    ad_at = small.shape[1] - hidden
+    bias_at = nums.shape[1] - 128 - hidden
+    size = hidden // lines
+
+    def cut(i, q):
+        return slice(q * size + i * ITEM, q * size + (i + 1) * ITEM)
+
+    def columns(ref, first, i):
+        return jnp.concatenate(
+            [ref[:, first + q * size + i * ITEM : first + q * size + (i + 1) * ITEM] for q in range(lines)], axis=1
+        )
+
+    def load_up(i):
+        for q in range(lines):
+            span = pl.ds(q * size + i * ITEM, ITEM)
+            fetch(wu.at[:, span], wu_role.at[:, span], wus.at[i, :, pl.ds(q * ITEM, ITEM)], up_sem.at[i, q])
+
+    def await_up(i):
+        for q in range(lines):
+            span = pl.ds(q * size + i * ITEM, ITEM)
+            pltpu.make_async_copy(wu.at[:, span], wus.at[i, :, pl.ds(q * ITEM, ITEM)], up_sem.at[i, q]).wait()
+
+    def load_down(i):
+        for q in range(lines):
+            span = pl.ds(q * size + i * ITEM, ITEM)
+            fetch(wd.at[span], wd_role.at[span], wds.at[i, pl.ds(q * ITEM, ITEM)], down_sem.at[i, q])
+
+    def await_down(i):
+        for q in range(lines):
+            span = pl.ds(q * size + i * ITEM, ITEM)
+            pltpu.make_async_copy(wd.at[span], wds.at[i, pl.ds(q * ITEM, ITEM)], down_sem.at[i, q]).wait()
+
+    def by_rows(act):
+        def body(r, carry):
+            act(pl.ds(pl.multiple_of(r * rows, rows), rows))
+            return carry
+
+        lax.fori_loop(0, 2, body, 0)
+
+    for i in range(count):
+        load_up(i)
+    up_rank[...] = dot_t(nm[...], au).astype(BF16)
+    g_down[...] = dot_t(cot[...], bd).astype(BF16)
+    for i in range(count):
+        bu_i, bias_i = columns(small, bu_at, i), columns(nums, bias_at, i)
+        await_up(i)
+
+        def open_gate(here):
+            gate = dot(nm[here], wus[i]) + dot(up_rank[here], bu_i) + bias_i
+            value, slope = gelu_parts(gate)
+            hid[i, here] = value.astype(BF16)
+            gg[i, here] = slope.astype(BF16)
+
+        by_rows(open_gate)
+        supply.tick(i)
+    for i in range(count):
+        supply.ready_item(i)
+        load_down(i)
+        ad_i, bu_i = columns(small, ad_at, i), columns(small, bu_at, i)
+        await_down(i)
+
+        def close_gate(here):
+            grad = dot_t(cot[here], wds[i]) + dot(g_down[here], ad_i)
+            gg[i, here] = (grad * gg[i, here].astype(F32)).astype(BF16)
+
+        by_rows(close_gate)
+        up_part = dot_t(gg[i], bu_i)
+        down_part = dot_t(hid[i], ad_i)
+        if i == 0:
+            g_up[...] = up_part
+            down_rank[...] = down_part
+        else:
+            g_up[...] += up_part
+            down_rank[...] += down_part
+        one = t_dot(up_rank[...], gg[i])
+        two = t_dot(g_down[...], hid[i])
+        for q in range(lines):
+            tuo[:, cut(i, q)] = one[:, q * ITEM : (q + 1) * ITEM]
+            tdi[:, cut(i, q)] = two[:, q * ITEM : (q + 1) * ITEM]
+    gu = g_up[...].astype(BF16)
+    dr = down_rank[...].astype(BF16)
+    up_rank[...] = gu
+    g_down[...] = dr
+
+    def store(slot, target, r):
+        return pltpu.make_async_copy(stage.at[slot], target.at[pl.ds(r * rows, rows)], out_sem.at[slot])
+
+    for r in range(2):
+        here = slice(r * rows, (r + 1) * rows)
+        value = dot(up_rank[here], au)
+        for i in range(count):
+            value = value + dot_t(gg[i, here], wus[i])
+        if r > 0:
+            store(0, gmid, r - 1).wait()
+        stage[0] = value.astype(BF16)
+        store(0, gmid, r).start()
+        value = dot(g_down[here], bd)
+        for i in range(count):
+            value = value + dot(hid[i, here], wds[i])
+        if r > 0:
+            store(1, part, r - 1).wait()
+        stage[1] = value.astype(BF16)
+        store(1, part, r).start()
+    tui[...] = t_dot(gu, nm[...])
+    tdo[...] = t_dot(dr, cot[...])
+    store(0, gmid, 1).wait()
+    store(1, part, 1).wait()
+    supply.finish()
+
+
+def mlp(nm, cot, wu, wu_role, wd, chosen, small, nums):
+    n, width = nm.shape
+    hidden = wu.shape[1]
+    rank = small.shape[0]
+    items = wd.shape[0] // 4 // ITEM
+    tile = hidden // items
+    low = lambda *s: jax.ShapeDtypeStruct(s, BF16)
+    high = lambda *s: jax.ShapeDtypeStruct(s, F32)
+    return pl.pallas_call(
+        mlp_kernel,
+        in_specs=[VMEM_SPEC] * 2 + [ANY_SPEC] * 3 + [VMEM_SPEC] * 3,
+        out_specs=[ANY_SPEC] * 2 + [VMEM_SPEC] * 4 + [ANY_SPEC],
+        out_shape=[
+            low(n, width), low(n, width), high(rank, hidden), high(rank, hidden), high(rank, width), high(rank, width),
+            low(*wd.shape),
+        ],
+        scratch_shapes=[
+            VM((items, width, tile), BF16), VM((items, tile, width), BF16), VM((items, n, tile), BF16),
+            VM((items, n, tile), BF16), VM((2, n // 2, width), BF16),
+            VM((n, rank), BF16), VM((n, rank), BF16), VM((n, rank), F32), VM((n, rank), F32),
+        ]
+        + sems(items) + sems(items, 3)
+        + [pltpu.SemaphoreType.DMA((items, 4)), pltpu.SemaphoreType.DMA((items, 4)), pltpu.SemaphoreType.DMA((2,))],
+        compiler_params=comm_params(3, 60),
+        name="mlp",
+    )(nm, cot, wu, wu_role, wd, chosen, small, nums)
 
 
 class Tables:
-    def __init__(self, at, own, shared, own_home, quarter_home, own_all, quarter_all, every, buffers, semaphores):
-        self.at, self.own, self.shared = at, own, shared
-        self.own_home, self.quarter_home = own_home, quarter_home
-        self.own_all, self.quarter_all, self.every = own_all, quarter_all, every
-        self.half_in, self.half, self.quarter_in, self.quarter = buffers
-        (self.s1, self.r1, self.s2, self.r2, self.s3, self.r3, self.s4, self.r4, self.s5, self.r5, self.s6, self.r6, self.keep) = semaphores
+    def __init__(self, at, pack, shared, home, gathered, every, buffers, semaphores):
+        self.at, self.pack, self.shared, self.home = at, pack, shared, home
+        self.gathered, self.every = gathered, every
+        self.half_in, self.half, self.quarter_in = buffers
+        (
+            self.s1, self.r1, self.s2, self.r2, self.s3, self.r3, self.s4, self.r4, self.s5, self.r5, self.s6, self.r6,
+            self.keep,
+        ) = semaphores
         self.d, self.t = lax.axis_index("dp"), lax.axis_index("tensor")
-        self.nd, self.nt = own_all.shape[0], every.shape[0]
+        self.nd, self.nt = gathered.shape[0], every.shape[0]
         self.core, self.low = self.d % 2, self.t % 2
         self.wide = shared.shape[1] // 2
         self.narrow = self.wide // 2
+        self.count = shared.shape[0]
+        self.own = pack.shape[0] - self.count
 
     def first(self):
         away = pl.ds(pl.multiple_of((1 - self.core) * self.wide, self.wide), self.wide)
@@ -737,23 +783,14 @@
         return remote(self.half.at[:, away], self.quarter_in, self.s2, self.r2, self.at["near"])
 
     def third(self):
-        return (
-            remote(self.own, self.own_home, self.s3.at[0], self.r3.at[0], self.at["cross"]),
-            remote(self.quarter, self.quarter_home, self.s3.at[1], self.r3.at[1], self.at["cross"]),
-        )
+        return remote(self.pack, self.home, self.s3, self.r3, self.at["cross"])
 
     def fourth(self, k):
         peer = (lax.rem(self.d + k, self.nd), self.t)
-        return (
-            remote(self.own_home, self.own_all.at[self.d], self.s4.at[0, k], self.r4.at[0, k], peer),
-            remote(self.quarter_home, self.quarter_all.at[self.d], self.s4.at[1, k], self.r4.at[1, k], peer),
-        )
+        return remote(self.home, self.gathered.at[self.d], self.s4.at[k], self.r4.at[k], peer)
 
     def stay(self):
-        return (
-            pltpu.make_async_copy(self.own_home, self.own_all.at[self.d], self.keep.at[0]),
-            pltpu.make_async_copy(self.quarter_home, self.quarter_all.at[self.d], self.keep.at[1]),
-        )
+        return pltpu.make_async_copy(self.home, self.gathered.at[self.d], self.keep.at[0])
 
     def share_of(self, core):
         return pl.ds(core * (self.nd // 2), self.nd // 2)
@@ -761,21 +798,20 @@
     def fifth(self, k):
         peer = (self.d, lax.rem(self.t + k, self.nt))
         slots = self.share_of(self.core)
-        return remote(
-            self.quarter_all.at[slots], self.every.at[self.t, slots], self.s5.at[k], self.r5.at[k], peer
-        )
+        mine = self.gathered.at[slots, pl.ds(self.own, self.count)]
+        return remote(mine, self.every.at[self.t, slots], self.s5.at[k], self.r5.at[k], peer)
 
     def sixth(self, k):
         block = self.every.at[lax.rem(self.t + k, self.nt), self.share_of(self.core)]
         return remote(block, block, self.s6.at[k], self.r6.at[k], self.at["core"])
 
     def stay_every(self):
-        return pltpu.make_async_copy(self.quarter_all, self.every.at[self.t], self.keep.at[2])
+        mine = self.gathered.at[pl.ds(0, self.nd), pl.ds(self.own, self.count)]
+        return pltpu.make_async_copy(mine, self.every.at[self.t], self.keep.at[1])
 
     def peers(self, act):
         def body(k, carry):
-            for copy in self.fourth(k):
-                act(copy)
+            act(self.fourth(k))
             return carry
 
         lax.fori_loop(1, self.nd, body, 0)
@@ -792,32 +828,28 @@
     def hop3(self):
         self.second().wait_recv()
         mine = pl.ds(pl.multiple_of(self.low * self.narrow, self.narrow), self.narrow)
-        self.quarter[...] = (self.half[:, mine].astype(F32) + self.quarter_in[...].astype(F32)).astype(BF16)
+        total = self.half[:, mine].astype(F32) + self.quarter_in[...].astype(F32)
+        self.pack[self.own :] = total.astype(BF16)
 
         @pl.when(self.at["moved"])
         def _():
-            for copy in self.third():
-                copy.start()
+            self.third().start()
 
         @pl.when(jnp.logical_not(self.at["moved"]))
         def _():
-            self.own_home[...] = self.own[...]
-            self.quarter_home[...] = self.quarter[...]
+            self.home[...] = self.pack[...]
 
     def hop4(self):
         @pl.when(self.at["moved"])
         def _():
-            for copy in self.third():
-                copy.wait_recv()
-
-        for copy in self.stay():
-            copy.start()
+            self.third().wait_recv()
+
+        self.stay().start()
         self.peers(lambda copy: copy.start())
 
     def hop5(self):
         self.peers(lambda copy: copy.wait_recv())
-        for copy in self.stay():
-            copy.wait()
+        self.stay().wait()
         self.stay_every().start()
         for k in range(1, self.nt):
             self.fifth(k).start()
@@ -833,8 +865,7 @@
 
         @pl.when(self.at["moved"])
         def _():
-            for copy in self.third():
-                copy.wait_send()
+            self.third().wait_send()
 
         self.peers(lambda copy: copy.wait_send())
         self.stay_every().wait()
@@ -843,16 +874,14 @@
             self.sixth(k).wait()
 
 
-def tables_scratch(nd, rank, own, count, width):
-    rows = count * rank
+def tables_scratch(nd, own, count, width):
+    one = pltpu.SemaphoreType.DMA
     return (
         [
-            VM((rank, own), BF16), VM((rows, width), BF16), VM((rank, own), BF16), VM((rows, width // 4), BF16),
-            VM((nd, rows, width // 4), BF16),
-            VM((rows, width // 2), BF16), VM((rows, width // 2), BF16), VM((rows, width // 4), BF16),
-            VM((rows, width // 4), BF16),
+            VM((own + count, width // 4), BF16), VM((count, width), BF16), VM((own + count, width // 4), BF16),
+            VM((count, width // 2), BF16), VM((count, width // 2), BF16), VM((count, width // 4), BF16),
         ],
-        [pltpu.SemaphoreType.DMA] * 4 + sems(2) + sems(2, nd) + sems(4) + sems(4) + [pltpu.SemaphoreType.DMA((3,))],
+        [one] * 6 + sems(nd) + sems(4) + sems(4) + [one((2,))],
     )
 
 
@@ -860,12 +889,12 @@
     gmid, mlp_part, x, w3, wqkv, wo, wo_role, cot, mid, tok, gains, dbias, proj, ctx, lse, rank_qkv, rank_out,
     small, chosen, nums, tuo, tdi, tui, tdo, ids,
     out, in_grad, own_early, every_early, own_late, every_late, all_ids,
-    work, kept, gm, grad, gctx, gproj, dist, kt, gk, gv, wv, wov, side, far, mix, side2, far2, mix2, done, done2,
+    work, kept, gm, grad, gctx, gproj, dist, kt, gk, gv, wv, wov, side, far, mix, side2, far2, mix2, done, done2, low_rank,
     *rest,
 ):
-    early_buffers, late_buffers = rest[:9], rest[9:18]
-    early_sems, late_sems = rest[18:31], rest[31:44]
-    rs, rr, ms, mr, ls, lr, gs, gr, os, orr, bs, br, ns, nr, load = rest[44:]
+    early_buffers, late_buffers = rest[:6], rest[6:12]
+    early_sems, late_sems = rest[12:25], rest[25:38]
+    rs, rr, ms, mr, ls, lr, gs, gr, os, orr, bs, br, ns, nr, load = rest[38:]
     at = places()
     moved = at["moved"]
     still = jnp.logical_not(moved)
@@ -919,16 +948,6 @@
     total = Gathered(at, work, side, far, mix, rs, rr)
     spread = Spread(at, gm, gs, gr)
     total.begin()
-    own, shared, own_home, quarter_home, quarter_all = early_buffers[:5]
-    wide = tuo.shape[1]
-    own[:, :wide] = tuo[...].astype(BF16)
-    own[:, wide:] = tdi[...].astype(BF16)
-    shared[0:rank] = tui[...].astype(BF16)
-    shared[rank : 2 * rank] = tdo[...].astype(BF16)
-    early = Tables(
-        at, own, shared, own_home, quarter_home, own_early, quarter_all, every_early, early_buffers[5:], early_sems
-    )
-    early.hop1()
     lax.fori_loop(1, nd, send_number, 0)
     for i in range(CHUNKS):
         here = slice(i * step, (i + 1) * step)
@@ -937,18 +956,6 @@
         grad[here] = value
         gm[here] = value.astype(BF16)
         spread.post(i)
-    early.hop2()
-    for i in range(CHUNKS):
-        spread.forward(i)
-    early.hop3()
-    spread.finish()
-    total.finish()
-
-    for copy in get_kept:
-        copy.wait()
-    mlp = Gathered(at, mlp_part, side, far, mix, ms, mr, kept)
-    mlp.send_away()
-    mlp.send_home()
     pltpu.make_async_copy(wo, wov, load.at[3]).wait()
     bq, ao = small[:, : 3 * cols], small[:, 3 * cols : 4 * cols]
     aq, bo = chosen[0:rank], chosen[rank : 2 * rank]
@@ -962,12 +969,37 @@
 
     sums = (jnp.zeros((rank, gm.shape[1]), F32), jnp.zeros((rank, cols), F32))
     sums = context_rows(0, sums)
+    for i in range(2):
+        spread.forward(i)
+    spread.beside()
+    sums = context_rows(1, sums)
+    for i in range(2, CHUNKS):
+        spread.forward(i)
+    spread.finish()
+    total.finish()
+    for copy in get_kept:
+        copy.wait()
+    mlp = Gathered(at, mlp_part, side, far, mix, ms, mr, kept)
+    mlp.send_away()
+    mlp.send_home()
+    sums = context_rows(2, sums)
     mlp.send_over()
-    early.hop4()
-    for i in range(1, 4):
-        sums = context_rows(i, sums)
-    early.hop5()
-    context_sums = sums
+    sums = context_rows(3, sums)
+    pack, shared, home = early_buffers[:3]
+
+    def lay(blocks, value):
+        for k in range(value.shape[1] // cols):
+            here = (blocks + k) * rank
+            pack[here : here + rank] = value[:, k * cols : (k + 1) * cols].astype(BF16)
+
+    lay(0, sums[1])
+    lay(1, tuo)
+    lay(1 + tuo.shape[1] // cols, tdi)
+    shared[0:rank] = sums[0].astype(BF16)
+    shared[rank : 2 * rank] = tui[...].astype(BF16)
+    shared[2 * rank :] = tdo[...].astype(BF16)
+    early = Tables(at, pack, shared, home, own_early, every_early, early_buffers[3:], early_sems)
+    early.hop1()
     get_x = pltpu.make_async_copy(x, gm, load.at[4])
     get_x.start()
     for j in range(3):
@@ -999,8 +1031,9 @@
         return carry
 
     lax.fori_loop(0, 2, attend_step, 0)
-    early.hop6()
+    early.hop2()
     lax.fori_loop(2, 4, attend_step, 0)
+    early.hop3()
     gproj[:, cols : 2 * cols] = (gk[...] * scale).astype(BF16)
     gproj[:, 2 * cols :] = gv[...].astype(BF16)
 
@@ -1028,34 +1061,34 @@
     get_x.wait()
     for j in range(3):
         pltpu.make_async_copy(w3.at[j], wv.at[j], load.at[5 + j]).wait()
-    own, shared, own_home, quarter_home, quarter_all = late_buffers[:5]
-
-    def input_rows(i, sums):
+    pack, shared, home = late_buffers[:3]
+    low = dot_t(gproj[...], bq).astype(BF16)
+    lay_rows = t_dot(rank_qkv[...], gproj[...]).astype(BF16)
+    for j in range(3):
+        pack[j * rank : (j + 1) * rank] = lay_rows[:, j * cols : (j + 1) * cols]
+    shared[...] = t_dot(low, gm[...]).astype(BF16)
+    low_rank[...] = low
+    late = Tables(at, pack, shared, home, own_late, every_late, late_buffers[3:], late_sems)
+    late.hop1()
+
+    def input_rows(i):
         here = pl.ds(i * rows, rows)
-        g = gproj[here]
-        r = dot_t(g, bq).astype(BF16)
-        acc = dot(r, aq)
+        acc = dot(low_rank[here], aq)
         for j in range(3):
-            acc = acc + dot_t(g[:, j * cols : (j + 1) * cols], wv[j])
+            acc = acc + dot_t(gproj[here, j * cols : (j + 1) * cols], wv[j])
         work[here] = acc.astype(BF16)
-        return sums[0] + t_dot(rank_qkv[here], g), sums[1] + t_dot(r, gm[here])
 
     last = Gathered(at, work, side2, far2, mix2, ls, lr)
-    sums = (jnp.zeros((rank, 3 * cols), F32), jnp.zeros((rank, gm.shape[1]), F32))
-    sums = input_rows(3, sums)
+    input_rows(3)
     last.send_away()
-    sums = input_rows(1, sums)
+    early.hop4()
+    input_rows(1)
     last.send_home()
-    sums = input_rows(2, sums)
+    late.hop2()
+    input_rows(2)
     last.send_over()
-    sums = input_rows(0, sums)
-    own[:, : 3 * cols] = sums[0].astype(BF16)
-    own[:, 3 * cols :] = context_sums[1].astype(BF16)
-    shared[0:rank] = sums[1].astype(BF16)
-    shared[rank : 2 * rank] = context_sums[0].astype(BF16)
-    late = Tables(at, own, shared, own_home, quarter_home, own_late, quarter_all, every_late, late_buffers[5:], late_sems)
-    late.hop1()
-    hops = (late.hop2, late.hop3, late.hop4, late.hop5)
+    late.hop3()
+    input_rows(0)
     for i in range(CHUNKS):
         here = slice(i * step, (i + 1) * step)
         unit, inverse = unit_rows(tok[here].astype(F32))
@@ -1070,7 +1103,13 @@
         def _():
             in_grad[here] = value
 
-        hops[i]()
+        if i == 0:
+            late.hop4()
+        if i == 1:
+            early.hop5()
+        if i == 3:
+            late.hop5()
+    early.hop6()
     late.hop6()
     lax.fori_loop(1, nd, await_number, 0)
     mlp.finish()
@@ -1091,18 +1130,18 @@
     n = 4 * rows
     cols = ctx.shape[1]
     rank = small.shape[0]
-    early_own = 2 * tuo.shape[1]
+    early_own = (1 + 2 * tuo.shape[1] // cols) * rank
     low = lambda *s: jax.ShapeDtypeStruct(s, BF16)
-    early = tables_scratch(nd, rank, early_own, 2, width)
-    late = tables_scratch(nd, rank, 4 * cols, 2, width)
+    early = tables_scratch(nd, early_own, 3 * rank, width)
+    late = tables_scratch(nd, 3 * rank, rank, width)
     return pl.pallas_call(
         back_kernel,
         in_specs=[ANY_SPEC] * 7 + [VMEM_SPEC] * 18,
         out_specs=[VMEM_SPEC] * 2 + [ANY_SPEC] * 4 + [VMEM_SPEC],
         out_shape=[
             low(rows, width), low(rows, width),
-            low(nd, rank, early_own), low(nt, nd, 2 * rank, width // 4),
-            low(nd, rank, 4 * cols), low(nt, nd, 2 * rank, width // 4),
+            low(nd, early_own + 3 * rank, width // 4), low(nt, nd, 3 * rank, width // 4),
+            low(nd, 4 * rank, width // 4), low(nt, nd, rank, width // 4),
             jax.ShapeDtypeStruct((nd,) + ids.shape, jnp.int32),
         ],
         scratch_shapes=[
@@ -1111,7 +1150,7 @@
             VM((n, cols), F32), VM((n, cols), F32), VM(w3.shape, BF16), VM(wo.shape, BF16),
             VM((2 * rows, width), BF16), VM((rows, width), BF16), VM((rows, width), BF16),
             VM((2 * rows, width), BF16), VM((rows, width), BF16), VM((rows, width), BF16),
-            VM((rows, width), BF16), VM((rows, width), BF16),
+            VM((rows, width), BF16), VM((rows, width), BF16), VM((n, rank), BF16),
         ]
         + early[0] + late[0] + early[1] + late[1]
         + sems(3, CHUNKS) * 4 + sems(CHUNKS) * 2 + sems(nd) + [pltpu.SemaphoreType.DMA((8,))],
@@ -1130,26 +1169,32 @@
     for ref in (gqi, gqo, goi, goo, gui, guo, gdi, gdo):
         ref[...] = jnp.zeros_like(ref)
 
+    def block(ref, s, k):
+        return ref[s, k * rank : (k + 1) * rank].astype(F32)
+
     def add(s, carry):
         e = [ids[s, 0, k] for k in range(4)]
+        many = wide // cols
         for j in range(3):
-            gqo[e[0], j] += own_late[s, :, j * cols : (j + 1) * cols].astype(F32)
-        goi[e[1]] += own_late[s, :, 3 * cols :].astype(F32)
-        guo[e[2]] += own_early[s, :, :wide].astype(F32)
-        gdi[e[3]] += own_early[s, :, wide:].astype(F32)
+            gqo[e[0], j] += block(own_late, s, j)
+        goi[e[1]] += block(own_early, s, 0)
+        for j in range(many):
+            at = slice(j * cols, (j + 1) * cols)
+            guo[e[2], :, at] += block(own_early, s, 1 + j)
+            gdi[e[3], :, at] += block(own_early, s, 1 + many + j)
         for z in range(every_late.shape[0]):
             at = slice(z * quarter, (z + 1) * quarter)
-            gqi[e[0], :, at] += every_late[z, s, 0:rank].astype(F32)
-            goo[e[1], :, at] += every_late[z, s, rank:].astype(F32)
-            gui[e[2], :, at] += every_early[z, s, 0:rank].astype(F32)
-            gdo[e[3], :, at] += every_early[z, s, rank:].astype(F32)
+            gqi[e[0], :, at] += every_late[z, s].astype(F32)
+            goo[e[1], :, at] += every_early[z, s, 0:rank].astype(F32)
+            gui[e[2], :, at] += every_early[z, s, rank : 2 * rank].astype(F32)
+            gdo[e[3], :, at] += every_early[z, s, 2 * rank :].astype(F32)
         return carry
 
     lax.fori_loop(0, nd, add, 0)
 
 
 def combine(ids, own_early, every_early, own_late, every_late, tables, cols, wide):
-    rank = own_early.shape[1]
+    rank = every_late.shape[2]
     width = every_late.shape[0] * every_late.shape[3]
     high = lambda *s: jax.ShapeDtypeStruct(s, F32)
     full = high(tables, rank, width)
@@ -1187,13 +1232,13 @@
         adapter_up_input, adapter_down_output,
     )
     (
-        x, tok, small, nums, chosen, proj, lse, ctx, rank_qkv, rank_out, nm, middle, cot, wqkv, wo, wu, wd,
+        x, tok, small, nums, chosen, proj, lse, ctx, rank_qkv, rank_out, nm, middle, cot, wqkv, wo, wu,
     ) = front(
         adapter_ids[0], tokens, numbers, tables_in, norm_gains, norm_shifts, output_bias_vector.reshape(1, width),
-        w3, output_weight, up_weight, down_weight, cotangent,
+        w3, output_weight, up_weight, cotangent,
     )
-    part, gmid, t_up_out, t_down_in, t_up_in, t_down_out = mlp(
-        nm, cot, up_weight, wu, down_weight, wd, chosen, small, nums, hidden_width // 4
+    part, gmid, t_up_out, t_down_in, t_up_in, t_down_out, _ = mlp(
+        nm, cot, up_weight, wu, down_weight, chosen, small, nums
     )
     result, in_grad, own_early, every_early, own_late, every_late, everyone = back(
         nd, nt, gmid, part, x, w3, wqkv, output_weight, wo, cot[:rows], middle, tok, norm_gains,

time: 504 us -> 488 us (0.968)
  Pallas kernels: 486 us -> 469 us
    pallas_call x1, Pallas kernels: 244 us -> 198 us  [front(): pl.pallas_call(front_kernel, in_specs=[pl.BlockSpec(memory_space=pltpu.SM...]
    pallas_call x1, Pallas kernels: 56 us -> 98.4 us  [mlp(): pl.pallas_call(mlp_kernel, in_specs=[VMEM_SPEC] * 2 + [ANY_SPEC] * 3 + [V...]
    pallas_call x1, Pallas kernels: 181 us -> 168 us  [back(): pl.pallas_call(back_kernel, in_specs=[ANY_SPEC] * 7 + [VMEM_SPEC] * 18, o...]
where the time goes in v4:
time: 488 us; the launch traced here: 483 us
  Pallas kernels  469 us (96%)
  local copies, waits for them, and re-layouts  11 us (2%)
    pallas_call x1, Pallas kernels, front(): pl.pallas_call(front_kernel, in_specs=[pl.BlockSpec(memory_space=pltpu.SM...  198 us
    pallas_call x1, Pallas kernels, back(): pl.pallas_call(back_kernel, in_specs=[ANY_SPEC] * 7 + [VMEM_SPEC] * 18, o...  168 us
    pallas_call x1, Pallas kernels, mlp(): pl.pallas_call(mlp_kernel, in_specs=[VMEM_SPEC] * 2 + [ANY_SPEC] * 3 + [V...  98.4 us

profile of v4, /device:TPU:1, one launch (start us, length us, event | category | flops | bytes accessed | tf_op | source)
XLA Modules:
  0.0 483.2 jit_solution(11932695162724772418)
XLA Ops:
  0.6 0.7 copy.32
  1.3 0.7 add_convert_fusion
  2.1 1.3 fusion.numbers
  3.4 197.9 %front.1 = (bf16[1024,2048]{1,0:T(8,128)(2,1)}, bf16[256,2048]{1,0:T(8,128)(2,1)}, bf16[16,6144]{1,0:T(8,128)(2,1)}, f32[1,3200]{1,0:T(1,128)}, bf16[64,2048]{1,...) custom-call(s32[4]{0:T(128)} %bitcast.18, ...), custom_call_target="tpu_custom_call" | custom-call | tf_op jit(solution)/shard_map/front/pallas_call | solution.py:578
  201.3 0.0 copy-start.7
  201.3 98.4 %mlp.1 = (bf16[1024,2048]{1,0:T(8,128)(2,1)}, bf16[1024,2048]{1,0:T(8,128)(2,1)}, f32[16,2048]{1,0:T(8,128)}, f32[16,2048]{1,0:T(8,128)}, f32[16,2048]{1,0:T(8,1...) custom-call(bf16[1024,2048]{1,0:T(8,128)(2,1)} %get-tuple-element.47.nm, bf16[1024,2048]{1,0:T(8,128)(2,1)} %get-tuple-element.48.cot, ...), custom_call_target="tpu_custom_call" | custom-call | tf_op jit(solution)/shard_map/mlp/pallas_call | solution.py:740
  299.7 2.3 slice.3.cot
  302.0 0.0 copy-done.7
  302.0 0.5 pad.9.ids
  302.6 168.2 %back.1 = (bf16[256,2048]{1,0:T(8,128)(2,1)}, bf16[256,2048]{1,0:T(8,128)(2,1)}, bf16[8,192,512]{2,1,0:T(8,128)(2,1)}, bf16[4,8,48,512]{3,2,1,0:T(8,128)(2,1)}, ...) custom-call(bf16[1024,2048]{1,0:T(8,128)(2,1)} %get-tuple-element.53.gmid, ...), custom_call_target="tpu_custom_call" | custom-call | tf_op jit(solution)/shard_map/back/pallas_call | solution.py:1137
  470.7 0.0 copy-start
  470.8 1.4 copy-done
  472.2 0.0 copy-start.1
  472.2 1.4 copy-done.1
  473.6 0.0 copy-start.2
  473.6 1.0 copy-done.2
  474.6 0.0 copy-start.3
  474.6 1.0 copy-done.3
  475.6 0.0 copy-start.4
  475.6 0.7 copy-done.4
  476.3 0.0 copy-start.6
  476.3 0.0 copy-start.5
  476.3 4.7 combine.1
  481.0 0.0 copy-done.6
  481.0 1.0 copy.35
  482.0 0.0 copy-done.5
  482.0 1.0 copy.36
Async XLA Ops:
  201.3 100.7 %copy-start.7 = (s32[1,4]{1,0:T(1,128)S(1)}, s32[1,4]{1,0:T(1,128)}, u32[]{:S(2)}) copy-start(s32[1,4]{1,0:T(1,128)} %param.43) | copy-start | bytes 52
  470.7 1.4 copy-start
  472.2 1.4 copy-start.1
  473.6 1.0 copy-start.2
  474.6 1.0 copy-start.3
  475.6 0.7 copy-start.4
  476.3 4.7 copy-start.6
  476.3 5.7 %copy-start.5 = (bf16[256,2048]{1,0:T(8,128)(2,1)S(1)}, bf16[256,2048]{1,0:T(8,128)(2,1)}, u32[]{:S(2)}) copy-start(bf16[256,2048]{1,0:T(8,128)(2,1)} %get-tuple-element.95) | copy-start | bytes 3145732
